TPU v7x, 128 devices: a whole 4x4x4 slice. The times are simulated.
128 devices in a mesh: dp: 2 (over x_lo), tile: 64 (over y, x_hi, z, core).
Axes of the slice: x: 4 (x_hi: 2, x_lo: 2; x = x_hi * 2 + x_lo), y: 4, z: 4, core: 2. Of those that a mesh axis runs over, the one named last changes fastest.
Arguments:
- grad_out: bfloat16 [2, 256, 640, 512], P('dp', 'tile'), may hold values from -6 to 6
- bev_act: bfloat16 [2, 256, 640, 512], P('dp', 'tile'), may hold values from -16 to 16
- conv_weight: bfloat16 [512, 3, 3, 512], replicated, may hold values from -0.09375 to 0.09375
- img_in: bfloat16 [2, 32768, 512], P('dp', 'tile'), may hold values from -16 to 16
- backbone_weight: bfloat16 [512, 512], replicated, may hold values from -0.25 to 0.25
- route: int32 [2, 2560], P('dp'), may hold values from 0 to 255, as said below
- offsets: int32 [2, 163840], P('dp', 'tile'), may hold values from 0 to 62
- frac_x: int32 [2, 163840], P('dp', 'tile'), may hold values from 0 to 255
- frac_y: int32 [2, 163840], P('dp', 'tile'), may hold values from 0 to 255
Outputs:
- image_grad: bfloat16 [2, 32768, 512], P('dp', 'tile')
- conv_grad: bfloat16 [512, 3, 3, 512], replicated
- backbone_grad: bfloat16 [512, 512], replicated
Inputs may be any that keep to these rules, and one draw needn't show every extreme that they name: `route`: owner of image block id is id // 4. Among the 40 ground blocks k * 40 to k * 40 + 39 of one sample, at most 2 have sources with one owner; in every sample some owner has exactly 2 such blocks from every device.
All inputs are finite; a program needn't handle non-finite values.
Results may differ from a plain program's by a relative error of at most 0.0073.
Values may be sent and summed in bfloat16 or wider, within the bound.
A program may use at most 192 MiB of HBM per device.

v0:
```python
import math

import jax
import jax.numpy as jnp
from jax import lax
from jax.sharding import PartitionSpec as P

BLK = 64
IMGW = 64


def extended(block, sides, width):
    for axis, dim in sides:
        count = lax.axis_size(axis)
        forward = [(i, i + 1) for i in range(count - 1)]
        backward = [(target, source) for source, target in forward]
        low = lax.ppermute(
            lax.slice_in_dim(block, block.shape[dim] - width, None, axis=dim), axis, forward
        )
        high = lax.ppermute(lax.slice_in_dim(block, 0, width, axis=dim), axis, backward)
        block = jnp.concatenate([low, block, high], axis=dim)
    return block


def make_band(offsets, frac_x, frac_y, blocks, width):
    columns = lax.broadcasted_iota(jnp.int32, (1, 1, width), 2)
    shaped = offsets.reshape(blocks, -1, 1)
    right_w = frac_x.reshape(blocks, -1, 1).astype(jnp.float32) / 256.0
    lower_w = frac_y.reshape(blocks, -1, 1).astype(jnp.float32) / 256.0
    across = jnp.where(columns == shaped, 1.0 - right_w, 0.0) + jnp.where(
        columns == shaped + 1, right_w, 0.0
    )
    return jnp.concatenate([(1.0 - lower_w) * across, lower_w * across], axis=2).astype(
        jnp.bfloat16
    )


def silu_slope(value):
    sigma = jax.nn.sigmoid(value)
    return sigma * (1.0 + value * (1.0 - sigma))


def body(grad_out, bev_act, conv_weight, img_in, backbone_weight, route, offsets, frac_x, frac_y):
    tiles = lax.axis_size("tile")
    my_tile = lax.axis_index("tile")
    rows = grad_out.shape[1]
    cols = grad_out.shape[2]
    chans = grad_out.shape[3]
    stacked = jnp.stack([grad_out[0], bev_act[0]])
    framed = extended(stacked, (("tile", 1),), 1)
    framed = jnp.pad(framed, ((0, 0), (0, 0), (1, 1), (0, 0)))
    out_frame = framed[0]
    act_frame = framed[1]
    center = grad_out[0]
    bev_sum = jnp.zeros((rows, cols, chans), jnp.float32)
    conv_parts = []
    for row_tap in range(3):
        tap_terms = []
        for col_tap in range(3):
            shifted = out_frame[2 - row_tap : 2 - row_tap + rows, 2 - col_tap : 2 - col_tap + cols]
            bev_sum = bev_sum + jnp.einsum(
                "rvo,co->rvc",
                shifted,
                conv_weight[:, row_tap, col_tap, :],
                preferred_element_type=jnp.float32,
            )
            moved = act_frame[row_tap : row_tap + rows, col_tap : col_tap + cols]
            tap_terms.append(
                jnp.einsum("rvc,rvo->co", moved, center, preferred_element_type=jnp.float32)
            )
        conv_parts.append(jnp.stack(tap_terms, axis=1))
    conv_local = jnp.stack(conv_parts, axis=1)
    bev_grad = bev_sum.astype(jnp.bfloat16)
    block_count = rows * cols // BLK
    blocks = bev_grad.reshape(block_count, BLK, chans)
    band = make_band(offsets[0], frac_x[0], frac_y[0], block_count, IMGW)
    capacity = max(2, 2 * block_count // tiles)
    image = img_in[0]
    per_device = image.shape[0] // (2 * IMGW)
    owners = (route[0] // per_device).reshape(tiles, block_count)
    local_ids = (route[0] % per_device).reshape(tiles, block_count)
    same_owner = owners[:, :, None] == owners[:, None, :]
    earlier = lax.broadcasted_iota(
        jnp.int32, (1, block_count, block_count), 2
    ) < lax.broadcasted_iota(jnp.int32, (1, block_count, block_count), 1)
    ranks = jnp.sum((same_owner & earlier).astype(jnp.int32), axis=2)
    slots = owners * capacity + ranks
    my_slots = lax.dynamic_index_in_dim(slots, my_tile, 0, keepdims=False)
    slot_total = tiles * capacity
    pieces = jnp.einsum("kmp,kmc->kpc", band, blocks, preferred_element_type=jnp.float32).astype(
        jnp.bfloat16
    )
    outgoing = jnp.zeros((slot_total, 2 * IMGW, chans), jnp.bfloat16).at[my_slots].set(pieces)
    arrived = lax.all_to_all(
        outgoing.reshape(tiles, capacity, 2 * IMGW, chans),
        "tile",
        split_axis=0,
        concat_axis=0,
        tiled=True,
    )
    mine = owners == my_tile
    block_iota = lax.broadcasted_iota(jnp.int32, (per_device, 1, 1, 1), 0)
    slot_iota = lax.broadcasted_iota(jnp.int32, (1, 1, 1, capacity), 3)
    picks = (
        mine[None, :, :, None]
        & (local_ids[None, :, :, None] == block_iota)
        & (ranks[None, :, :, None] == slot_iota)
    )
    gather_table = (
        jnp.sum(picks.astype(jnp.int32), axis=2)
        .astype(jnp.bfloat16)
        .reshape(per_device, slot_total)
    )
    feature_grad = jnp.dot(
        gather_table,
        arrived.reshape(slot_total, 2 * IMGW * chans),
        preferred_element_type=jnp.float32,
    ).reshape(image.shape[0], chans)
    pre_act = jnp.dot(image, backbone_weight, preferred_element_type=jnp.float32)
    scaled = (feature_grad * silu_slope(pre_act)).astype(jnp.bfloat16)
    image_grad = lax.dot_general(
        scaled, backbone_weight, (((1,), (1,)), ((), ())), preferred_element_type=jnp.float32
    ).astype(jnp.bfloat16)
    backbone_local = lax.dot_general(
        image, scaled, (((0,), (0,)), ((), ())), preferred_element_type=jnp.float32
    )
    cell_scale = 1.0 / math.sqrt(lax.axis_size("dp") * tiles * rows * cols)
    pixel_scale = 1.0 / math.sqrt(lax.axis_size("dp") * tiles * image.shape[0])
    conv_total, backbone_total = lax.psum((conv_local, backbone_local), ("dp", "tile"))
    conv_grad = (conv_total * cell_scale).astype(jnp.bfloat16)
    backbone_grad = (backbone_total * pixel_scale).astype(jnp.bfloat16)
    return (image_grad[None], conv_grad, backbone_grad)


def solution(mesh):
    return jax.shard_map(
        body,
        mesh=mesh,
        in_specs=(
            P("dp", "tile", None, None),
            P("dp", "tile", None, None),
            P(),
            P("dp", "tile", None),
            P(),
            P("dp", None),
            P("dp", "tile"),
            P("dp", "tile"),
            P("dp", "tile"),
        ),
        out_specs=(P("dp", "tile", None), P(), P()),
        check_vma=False,
    )
```

profile of v0, /device:TPU:1, one launch (start us, length us, event | category | flops | bytes accessed | tf_op | source)
XLA Modules:
  0.0 588.5 jit_solution(5111267187542343596)
XLA Ops:
  7.2 2.1 constant_dynamic-update-slice_fusion.1
  10.0 2.3 copy-done.2
  12.4 4.9 collective-permute-start
  17.3 1.9 collective-permute-start.1
  20.4 4.3 multiply_convert_fusion.2
  24.8 7.1 %collective-permute-done = bf16[2,1,640,512]{3,2,1,0:T(8,128)(2,1)} collective-permute-done((bf16[2,1,640,512]{3,2,1,0:T(8,128)(2,1)S(1)}, bf16[2,1,640,512]{3,2,1,0:T(8,128)(2,1)}, u32[]{:S(2)}, u32[]{:S(2)}) %collective-permute-start) | collective-permute-done | bytes 1310752 | tf_op jit(solution)/shard_map/ppermute | solution.py:17
  31.9 4.5 collective-permute-done.1
  36.4 5.3 fusion.5
  41.7 2.6 slice_bitcast_fusion
  44.3 3.9 fusion.26
  48.2 3.9 fusion.28
  52.1 4.0 fusion.30
  56.1 3.8 fusion.32
  60.0 3.9 fusion.34
  63.9 4.0 fusion.36
  67.9 3.9 fusion.38
  71.8 3.9 fusion.40
  75.7 29.1 %add_convert_fusion = bf16[4,640,512]{2,1,0:T(8,128)(2,1)S(1)} fusion(f32[4,640,512]{2,1,0:T(8,128)} %fusion.26, f32[4,640,512]{2,1,0:T(8,128)} %fusion.28, f32[4,640,512]{2,1,0:T(8,128)} %fusion.30, f32[4,640,512]{2,1,0:T(8,128)} %fusion.32, f32[4,640,512]{2,1,0:T(8,128)} %fusion.34, f32[4,640,512]{2,1,0:T(8,128)} %fusion.36, f32[4,640,512]{2,1,0:T(8,128)} %fusion.40, ...), kind=kOutput, calls=%fused_computation.11 | convolution fusion | flops 1353973760 | bytes 47710208 | tf_op jit(solution)/shard_map/rvo,co->rvc/dot_general | solution.py:61
  104.8 6.5 %convolution_convert_fusion = bf16[40,128,512]{2,1,0:T(8,128)(2,1)} fusion(bf16[40,64,512]{2,1,0:T(8,128)(2,1)S(1)} %bitcast.149, bf16[40,64,64]{2,1,0:T(8,128)(2,1)} %get-tuple-element.24, bf16[40,64,64]{2,1,0:T(8,128)(2,1)} %get-tuple-element.23), kind=kOutput, calls=%fused_computation.17 | convolution fusion | flops 339476480 | bytes 8519680 | tf_op jit(solution)/shard_map/kmp,kmc->kpc/dot_general | solution.py:90
  111.3 5.9 %broadcast_in_dim.27 = bf16[128,128,512]{2,1,0:T(8,128)(2,1)} broadcast(bf16[]{:T(256)} %constant.51.clone.1), dimensions={} | broadcast | bytes 16777218 | tf_op jit(solution)/shard_map/broadcast_in_dim | solution.py:93
  117.2 14.1 %scatter_fusion = bf16[128,128,512]{2,1,0:T(8,128)(2,1)} fusion(bf16[128,128,512]{2,1,0:T(8,128)(2,1)} %broadcast_in_dim.27, s32[40]{0:T(128)S(1)} %fusion.129, bf16[40,128,512]{2,1,0:T(8,128)(2,1)} %convolution_convert_fusion), kind=kCustom, calls=%fused_computation | custom fusion | bytes 15728800 | tf_op jit(solution)/shard_map/scatter | solution.py:93
  131.3 13.9 %all-to-all-start = ((bf16[64,2,128,512]{3,2,1,0:T(8,128)(2,1)}), bf16[64,2,128,512]{3,2,1,0:T(8,128)(2,1)}, u32[]{:S(2)}, u32[]{:S(2)}) async-start(bf16[64,2,128,512]{3,2,1,0:T(8,128)(2,1)} %bitcast.147), calls=%async_computation | async-start | bytes 33554432 | tf_op jit(solution)/shard_map/all_to_all | solution.py:94
  145.5 3.4 fusion.93
  150.5 1.6 fusion.78
  158.6 1.6 fusion.58
  160.1 1.6 fusion.68
  163.1 4.9 pad_maximum_fusion
  167.9 193.8 %all-to-all-done = bf16[64,2,128,512]{3,2,1,0:T(8,128)(2,1)} async-done(((bf16[64,2,128,512]{3,2,1,0:T(8,128)(2,1)}), bf16[64,2,128,512]{3,2,1,0:T(8,128)(2,1)}, u32[]{:S(2)}, u32[]{:S(2)}) %all-to-all-start) | async-done | bytes 16777248 | tf_op jit(solution)/shard_map/all_to_all | solution.py:94
  361.7 15.8 %copy.71 = bf16[16,8,128,512]{3,1,2,0:T(8,128)(2,1)S(1)} copy(bf16[16,8,128,512]{3,2,1,0:T(8,128)(2,1)} %bitcast.60) | data formatting | bytes 33554432
  377.5 2.3 fusion.132
  384.0 188.9 %all-reduce.4.cloned.1.call-done = (f32[512,3,3,512]{3,0,2,1:T(8,128)}, f32[512,512]{0,1:T(8,128)}) async-done(((f32[512,3,3,512]{3,0,2,1:T(8,128)}, f32[512,512]{0,1:T(8,128)}), (f32[512,3,3,512]{3,0,2,1:T(8,128)}, f32[512,512]{0,1:T(8,128)})) %all-reduce.4.cloned.1.call-update) | async-done | bytes 10485776 | tf_op jit(solution)/shard_map/psum | solution.py:129
  573.0 7.3 %multiply_convert_fusion = bf16[512,3,3,512]{3,0,2,1:T(8,128)(2,1)} fusion(f32[512,3,3,512]{3,0,2,1:T(8,128)} %get-tuple-element.15), kind=kLoop, calls=%fused_computation.5 | loop fusion | flops 4718592 | bytes 14155776 | tf_op jit(solution)/shard_map/convert_element_type | solution.py:130
  (67 shorter events, 16.9 us)
Async XLA Ops:
  7.2 373.4 %copy-start = (bf16[1,512,512]{2,1,0:T(8,128)(2,1)S(1)}, bf16[1,512,512]{2,1,0:T(8,128)(2,1)}, u32[]{:S(2)}) copy-start(bf16[1,512,512]{2,1,0:T(8,128)(2,1)} %param.12) | copy-start | bytes 1572868
  7.2 2.6 copy-start.4
  9.8 9.5 %copy-start.8 = (s32[1,2560]{1,0:T(1,128)S(1)}, s32[1,2560]{1,0:T(1,128)}, u32[]{:S(2)}) copy-start(s32[1,2560]{1,0:T(1,128)} %param.17) | copy-start | bytes 30724
  9.8 9.6 %copy-start.9 = (s32[1,2560]{1,0:T(1,128)S(1)}, s32[1,2560]{1,0:T(1,128)}, u32[]{:S(2)}) copy-start(s32[1,2560]{1,0:T(1,128)} %param.16) | copy-start | bytes 30724
  9.9 2.3 copy-start.2
  12.2 7.3 %copy-start.10 = (s32[1,2560]{1,0:T(1,128)S(1)}, s32[1,2560]{1,0:T(1,128)}, u32[]{:S(2)}) copy-start(s32[1,2560]{1,0:T(1,128)} %param.15) | copy-start | bytes 30724
  12.2 7.4 %copy-start.11 = (s32[1,2560]{1,0:T(1,128)S(1)}, s32[1,2560]{1,0:T(1,128)}, u32[]{:S(2)}) copy-start(s32[1,2560]{1,0:T(1,128)} %param.14) | copy-start | bytes 30724
  12.4 19.5 %collective-permute-start = (bf16[2,1,640,512]{3,2,1,0:T(8,128)(2,1)S(1)}, bf16[2,1,640,512]{3,2,1,0:T(8,128)(2,1)}, u32[]{:S(2)}, u32[]{:S(2)}) collective-permute-start(bf16[2,1,640,512]{3,2,1,0:T(8,128)(2,1)S(1)} %get-tuple-element.21), channel_id=1, source_target_pairs={{0,1},{1,2},{2,3},{3,4},{4,5},{5,6},{6,7},{7,8},{8,9},{9,10},{10,1... | collective-permute-start | bytes 3932168 | tf_op jit(solution)/shard_map/ppermute | solution.py:17
  17.3 19.0 %collective-permute-start.1 = (bf16[2,1,640,512]{3,2,1,0:T(8,128)(2,1)S(1)}, bf16[2,1,640,512]{3,2,1,0:T(8,128)(2,1)}, u32[]{:S(2)}, u32[]{:S(2)}) collective-permute-start(bf16[2,1,640,512]{3,2,1,0:T(8,128)(2,1)S(1)} %get-tuple-element.22), channel_id=1, source_target_pairs={{1,0},{2,1},{3,2},{4,3},{5,4},{6,5},{7,6},{8,7},{9,8},{10,9},{11,1... | collective-permute-start | bytes 3932168 | tf_op jit(solution)/shard_map/ppermute | solution.py:20
  36.4 7.9 %slice-start = ((s8[4718592]{0:T(1024)(128)(4,1)}), s8[4194304]{0:T(1024)(128)(4,1)S(1)}, s32[]{:S(2)}) async-start(s8[4718592]{0:T(1024)(128)(4,1)} %bitcast.150), calls=%async_computation.2 | async-start | bytes 8388608
  41.6 2.6 slice-start.1
  44.2 27.6 %copy-start.1 = (bf16[6,642,512]{2,1,0:T(8,128)(2,1)}, bf16[6,642,512]{2,1,0:T(8,128)(2,1)S(1)}, u32[]{:S(2)}) copy-start(bf16[6,642,512]{2,1,0:T(8,128)(2,1)S(1)} %get-tuple-element.20) | copy-start | bytes 11833348
  131.3 14.2 %copy-start.5 = (bf16[1,4,640,512]{3,2,1,0:T(8,128)(2,1)S(1)}, bf16[1,4,640,512]{3,2,1,0:T(8,128)(2,1)}, u32[]{:S(2)}) copy-start(bf16[1,4,640,512]{3,2,1,0:T(8,128)(2,1)} %param.9) | copy-start | bytes 7864324
  131.3 230.4 %all-to-all-start = ((bf16[64,2,128,512]{3,2,1,0:T(8,128)(2,1)}), bf16[64,2,128,512]{3,2,1,0:T(8,128)(2,1)}, u32[]{:S(2)}, u32[]{:S(2)}) async-start(bf16[64,2,128,512]{3,2,1,0:T(8,128)(2,1)} %bitcast.147), calls=%async_computation | async-start | bytes 33554432 | tf_op jit(solution)/shard_map/all_to_all | solution.py:94
  145.2 427.8 %all-reduce.4.cloned.1.call-start = ((), (), s32[]{:S(2)}) async-start(), calls=%async_computation.1 | async-start | bytes 20971520 | tf_op jit(solution)/shard_map/psum | solution.py:129
  145.5 3.5 copy-start.3
  377.5 3.1 copy-start.7
  573.0 7.3 %copy-start.6 = (f32[512,512]{0,1:T(8,128)S(1)}, f32[512,512]{0,1:T(8,128)}, u32[]{:S(2)}) copy-start(f32[512,512]{0,1:T(8,128)} %get-tuple-element.16) | copy-start | bytes 3145732
Sparse Core Ops, SparseCore 0:
  382.9 190.0 all-reduce.3
where the time goes:
time: 592 us; the launch traced here: 588 us
  waiting for transfers between devices  394 us (67%)
  matrix products  88.5 us (15%)
  local copies, waits for them, and re-layouts  45.9 us (8%)
  other arithmetic  24.4 us (4%)
  starting transfers between devices  20.8 us (4%)
  between operations  14.6 us (2%)
    all_to_all x1, waiting for transfers between devices, body(): lax.all_to_all(outgoing.reshape(tiles, capacity, 2 * IMGW, chans), 'tile'...  194 us
    psum x1, waiting for transfers between devices, body(): lax.psum((conv_local, backbone_local), ('dp', 'tile'))  189 us
    dot_general x9, matrix products, body(): jnp.einsum('rvo,co->rvc', shifted, conv_weight[:, row_tap, col_tap, :], p...  60.5 us
    unnamed x31, local copies, waits for them, and re-layouts  21.8 us
    dot_general x9, matrix products, body(): jnp.einsum('rvc,rvo->co', moved, center, preferred_element_type=jnp.float32)  15.8 us
    scatter x1, local copies, waits for them, and re-layouts, body(): jnp.zeros((slot_total, 2 * IMGW, chans), jnp.bfloat16).at[my_slots]  14.1 us
    all_to_all x1, starting transfers between devices, body(): lax.all_to_all(outgoing.reshape(tiles, capacity, 2 * IMGW, chans), 'tile'...  13.9 us
  transfers between devices with their start and end apart: 4, of which 4 were waited for; matrix products, arithmetic and copies ran while one was open for 5% of the time, Pallas kernels for 0%

commit v1 on v0

v1 whole, which is shorter than its diff:
```python
import functools
import math

import jax
import jax.numpy as jnp
from jax import lax
from jax.experimental import pallas as pl
from jax.experimental.pallas import tpu as pltpu
from jax.sharding import PartitionSpec as P

BLK = 64
IMGW = 64
PIXB = 2 * IMGW
TILES = 64
CAP = 2
MESH = pl.DeviceIdType.MESH
ANY = pl.BlockSpec(memory_space=pl.ANY)
VMEM = pl.BlockSpec(memory_space=pltpu.VMEM)
SMEM = pl.BlockSpec(memory_space=pltpu.SMEM)
BF = jnp.bfloat16
F32 = jnp.float32


def coords():
    t = lax.axis_index("tile")
    return t // 16, (t // 8) % 2 * 2 + lax.axis_index("dp"), (t // 2) % 4, t % 2


def device(y, x, z, core):
    return (x % 2, ((y * 2 + x // 2) * 4 + z) * 2 + core)


def along(axis, step):
    y, x, z, core = coords()
    if axis == "y":
        y = (y + step) % 4
    elif axis == "x":
        x = (x + step) % 4
    elif axis == "z":
        z = (z + step) % 4
    else:
        core = 1 - core
    return device(y, x, z, core)


def bev_kernel(idx_ref, g_ref, lo_ref, hi_ref, w_ref, s_ref, frame, w, acc, bev, sems, out_sem):
    rows, cols = g_ref.shape[0], g_ref.shape[1]
    copies = [
        pltpu.make_async_copy(w_ref, w, sems.at[0]),
        pltpu.make_async_copy(g_ref, frame.at[pl.ds(1, rows)], sems.at[1]),
        pltpu.make_async_copy(lo_ref, frame.at[0], sems.at[2]),
        pltpu.make_async_copy(hi_ref, frame.at[rows + 1], sems.at[3]),
    ]
    for copy in copies:
        copy.start()
    for copy in copies:
        copy.wait()
    half = 256

    def step(s, carry):
        r, n = s // 2, s % 2
        lanes = pl.ds(pl.multiple_of(n * half, half), half)

        def tap(j):
            total = None
            for i in range(3):
                term = lax.dot_general(
                    frame[r + 2 - i],
                    w[i * 3 + j, lanes, :],
                    (((1,), (1,)), ((), ())),
                    preferred_element_type=F32,
                )
                total = term if total is None else total + term
            return total

        acc[pl.ds(8, cols), :] = tap(1)
        acc[pl.ds(7, cols), :] += tap(0)
        acc[pl.ds(9, cols), :] += tap(2)
        bev[pl.ds(pl.multiple_of(r * cols, cols), cols), lanes] = acc[pl.ds(8, cols), :].astype(BF)
        return carry

    lax.fori_loop(0, 2 * rows, step, 0)

    def send(s, carry):
        start = pl.multiple_of(idx_ref[s] * BLK, BLK)
        pltpu.make_async_copy(bev.at[pl.ds(start, BLK)], s_ref.at[s], out_sem).start()
        return carry

    lax.fori_loop(0, TILES * CAP, send, 0)
    pltpu.make_async_copy(s_ref, s_ref, out_sem).wait()


def bev_slots(idx, g, lo, hi, w):
    rows, cols, chans = g.shape
    return pl.pallas_call(
        bev_kernel,
        out_shape=jax.ShapeDtypeStruct((TILES * CAP, BLK, chans), BF),
        in_specs=[SMEM, ANY, ANY, ANY, ANY],
        out_specs=ANY,
        scratch_shapes=[
            pltpu.VMEM((rows + 2, cols, chans), BF),
            pltpu.VMEM(w.shape, BF),
            pltpu.VMEM((cols + 16, 256), F32),
            pltpu.VMEM((rows * cols, chans), BF),
            pltpu.SemaphoreType.DMA((4,)),
            pltpu.SemaphoreType.DMA,
        ],
        compiler_params=pltpu.CompilerParams(vmem_limit_bytes=40 << 20),
        cost_estimate=pl.CostEstimate(
            flops=2 * 9 * rows * cols * chans * chans, bytes_accessed=24 << 20, transcendentals=0
        ),
        name="bev_slots",
    )(idx, g, lo, hi, w)


ORDERS = (("y", "z", "x"), ("z", "x", "y"), ("x", "y", "z"))
BATCHES = 8


def exchange_kernel(
    scale, s_ref, m_ref, w_ref, r_ref, rm_ref, o_ref,
    recv0, acc0, recv1, acc1, recv2, acc2, recv3,
    slot_send, slot_recv, meta_send, meta_recv, own_sem, pair_send, pair_recv, st_send, st_recv,
):
    y, x, z, core = coords()
    dp = lax.axis_index("dp")
    tile = lax.axis_index("tile")
    place = {"y": y, "x": x, "z": z}

    barrier = pltpu.get_barrier_semaphore()

    def greet(n, carry):
        pl.semaphore_signal(
            barrier, inc=1, device_id=(dp, (tile + n) % TILES), device_id_type=MESH
        )
        return carry

    lax.fori_loop(1, TILES, greet, 0)
    for step in (1, 3):
        pl.semaphore_signal(barrier, inc=1, device_id=along("x", step), device_id_type=MESH)
    pl.semaphore_wait(barrier, TILES + 1)

    def shifted(b, e, sign):
        dc, h, g = b // 4, (b // 2) % 2, b % 2
        dy = e % 4
        dz = (dy + 2 * (e // 4) + h) % 4
        dx = (g + e) % 2
        x_hi = x // 2
        return (
            (((y + 4 + sign * dy) % 4 * 2 + (x_hi + dx) % 2) * 4 + (z + 4 + sign * dz) % 4) * 2
            + (core + dc) % 2
        )

    def slot_copy(b, e):
        peer = shifted(b, e, 1)
        n = b * 8 + e
        return pltpu.make_async_remote_copy(
            src_ref=s_ref.at[peer], dst_ref=r_ref.at[tile],
            send_sem=slot_send.at[n], recv_sem=slot_recv.at[n],
            device_id=(dp, peer), device_id_type=MESH,
        )

    def meta_copy(b, e):
        peer = shifted(b, e, 1)
        n = b * 8 + e
        return pltpu.make_async_remote_copy(
            src_ref=m_ref.at[peer], dst_ref=rm_ref.at[tile],
            send_sem=meta_send.at[n], recv_sem=meta_recv.at[n],
            device_id=(dp, peer), device_id_type=MESH,
        )

    def issue(b):
        def one(e, carry):
            slot_copy(b, e).start()
            meta_copy(b, e).start()
            return carry

        lax.fori_loop(1 if b == 0 else 0, 8, one, 0)

    own = [
        pltpu.make_async_copy(s_ref.at[tile], r_ref.at[tile], own_sem.at[0]),
        pltpu.make_async_copy(m_ref.at[tile], rm_ref.at[tile], own_sem.at[1]),
    ]
    for copy in own:
        copy.start()

    half = w_ref.shape[1] // 2
    mine = pl.ds(pl.multiple_of(core * half, half), half)
    other = pl.ds(pl.multiple_of((1 - core) * half, half), half)
    pair = pltpu.make_async_remote_copy(
        src_ref=w_ref.at[:, other], dst_ref=recv0,
        send_sem=pair_send.at[0], recv_sem=pair_recv.at[0],
        device_id=along("core", 1), device_id_type=MESH,
    )
    pair.start()
    issue(0)
    pair.wait()

    def add0(k, carry):
        acc0[k] = (w_ref[k, mine, :].astype(F32) + recv0[k].astype(F32)).astype(BF)
        return carry

    lax.fori_loop(0, w_ref.shape[0], add0, 0)

    def taps(i):
        return pl.ds(3 * i, 3)

    def exchange(stage, source, landing):
        copies = []
        for i, order in enumerate(ORDERS):
            axis = order[stage if stage < 3 else 5 - stage]
            for d in (1, 2, 3):
                src, dst = source(i, (place[axis] + d) % 4), landing(i, d - 1)
                copies.append(
                    pltpu.make_async_remote_copy(
                        src_ref=src, dst_ref=dst,
                        send_sem=st_send.at[stage, i, d - 1], recv_sem=st_recv.at[stage, i, d - 1],
                        device_id=along(axis, d), device_id_type=MESH,
                    )
                )
        for copy in copies:
            copy.start()
        return copies

    def sixteenth(i, q):
        return pl.ds(pl.multiple_of(q * 16, 16), 16)

    def quarter(i, q):
        return pl.ds(pl.multiple_of(q * 64, 64), 64)

    def lane_part(q):
        return pl.ds(pl.multiple_of(q * 128, 128), 128)

    copies = exchange(
        0, lambda i, q: acc0.at[taps(i), quarter(i, q)], lambda i, k: recv1.at[i, k]
    )
    issue(1)
    for copy in copies:
        copy.wait()
    for i, order in enumerate(ORDERS):
        q = place[order[0]]
        for j in range(3):
            total = acc0[3 * i + j, quarter(i, q), :].astype(F32)
            for k in range(3):
                total = total + recv1[i, k, j].astype(F32)
            acc1[i, j] = total.astype(BF)
    copies = exchange(1, lambda i, q: acc1.at[i, :, sixteenth(i, q)], lambda i, k: recv2.at[i, k])
    issue(2)
    for copy in copies:
        copy.wait()
    for i, order in enumerate(ORDERS):
        q = place[order[1]]
        for j in range(3):
            total = acc1[i, j, sixteenth(i, q), :].astype(F32)
            for k in range(3):
                total = total + recv2[i, k, j].astype(F32)
            acc2[i, j] = total.astype(BF)
    copies = exchange(2, lambda i, q: acc2.at[i, :, :, lane_part(q)], lambda i, k: recv3.at[i, k])
    issue(3)
    for copy in copies:
        copy.wait()

    def rows64(i):
        return pl.ds(pl.multiple_of(core * half + place[ORDERS[i][0]] * 64, 64), 64)

    def rows16(i):
        return pl.ds(
            pl.multiple_of(
                core * half + place[ORDERS[i][0]] * 64 + place[ORDERS[i][1]] * 16, 16
            ),
            16,
        )

    for i, order in enumerate(ORDERS):
        q = place[order[2]]
        for j in range(3):
            total = acc2[i, j, :, lane_part(q)].astype(F32)
            for k in range(3):
                total = total + recv3[i, k, j].astype(F32)
            o_ref[3 * i + j, rows16(i), lane_part(q)] = (total * scale).astype(BF)

    def finish(copies, stage, landed):
        for copy in copies:
            copy.wait_send()
        for i, order in enumerate(ORDERS):
            axis = order[5 - stage]
            for d in (1, 2, 3):
                part = landed(i, (place[axis] + 4 - d) % 4)
                pltpu.make_async_remote_copy(
                    src_ref=part, dst_ref=part,
                    send_sem=st_send.at[stage, i, d - 1], recv_sem=st_recv.at[stage, i, d - 1],
                    device_id=along(axis, d), device_id_type=MESH,
                ).wait_recv()

    def gather(stage, part, landed, batch):
        copies = []
        for i, order in enumerate(ORDERS):
            axis = order[5 - stage]
            for d in (1, 2, 3):
                copies.append(
                    pltpu.make_async_remote_copy(
                        src_ref=part(i), dst_ref=part(i),
                        send_sem=st_send.at[stage, i, d - 1], recv_sem=st_recv.at[stage, i, d - 1],
                        device_id=along(axis, d), device_id_type=MESH,
                    )
                )
        for copy in copies:
            copy.start()
        issue(batch)
        finish(copies, stage, landed)

    gather(
        3,
        lambda i: o_ref.at[taps(i), rows16(i), lane_part(place[ORDERS[i][2]])],
        lambda i, q: o_ref.at[taps(i), rows16(i), lane_part(q)],
        4,
    )
    gather(
        4,
        lambda i: o_ref.at[taps(i), rows16(i)],
        lambda i, q: o_ref.at[
            taps(i),
            pl.ds(pl.multiple_of(core * half + place[ORDERS[i][0]] * 64 + q * 16, 16), 16),
        ],
        5,
    )
    gather(
        5,
        lambda i: o_ref.at[taps(i), rows64(i)],
        lambda i, q: o_ref.at[taps(i), pl.ds(pl.multiple_of(core * half + q * 64, 64), 64)],
        6,
    )
    back = pltpu.make_async_remote_copy(
        src_ref=o_ref.at[:, mine], dst_ref=o_ref.at[:, mine],
        send_sem=pair_send.at[1], recv_sem=pair_recv.at[1],
        device_id=along("core", 1), device_id_type=MESH,
    )
    back.start()
    issue(7)
    back.wait_send()
    pltpu.make_async_remote_copy(
        src_ref=o_ref.at[:, other], dst_ref=o_ref.at[:, other],
        send_sem=pair_send.at[1], recv_sem=pair_recv.at[1],
        device_id=along("core", 1), device_id_type=MESH,
    ).wait_recv()

    for copy in own:
        copy.wait()

    def drain(n, carry):
        b, e = n // 8, n % 8
        slot_copy(b, e).wait_send()
        meta_copy(b, e).wait_send()
        source = shifted(b, e, -1)
        pltpu.make_async_remote_copy(
            src_ref=s_ref.at[source], dst_ref=r_ref.at[source],
            send_sem=slot_send.at[n], recv_sem=slot_recv.at[n],
            device_id=(dp, source), device_id_type=MESH,
        ).wait_recv()
        pltpu.make_async_remote_copy(
            src_ref=m_ref.at[source], dst_ref=rm_ref.at[source],
            send_sem=meta_send.at[n], recv_sem=meta_recv.at[n],
            device_id=(dp, source), device_id_type=MESH,
        ).wait_recv()
        return carry

    lax.fori_loop(1, 64, drain, 0)


def exchange_all(scale, slots, meta, w):
    taps, rows, chans = w.shape
    half = rows // 2
    return pl.pallas_call(
        functools.partial(exchange_kernel, scale),
        out_shape=[
            jax.ShapeDtypeStruct(slots.shape, BF),
            jax.ShapeDtypeStruct(meta.shape, BF),
            jax.ShapeDtypeStruct(w.shape, BF),
        ],
        in_specs=[ANY, ANY, VMEM],
        out_specs=[ANY, ANY, VMEM],
        scratch_shapes=[
            pltpu.VMEM((taps, half, chans), BF),
            pltpu.VMEM((taps, half, chans), BF),
            pltpu.VMEM((3, 3, 3, 64, chans), BF),
            pltpu.VMEM((3, 3, 64, chans), BF),
            pltpu.VMEM((3, 3, 3, 16, chans), BF),
            pltpu.VMEM((3, 3, 16, chans), BF),
            pltpu.VMEM((3, 3, 3, 16, 128), BF),
            pltpu.SemaphoreType.DMA((64,)),
            pltpu.SemaphoreType.DMA((64,)),
            pltpu.SemaphoreType.DMA((64,)),
            pltpu.SemaphoreType.DMA((64,)),
            pltpu.SemaphoreType.DMA((2,)),
            pltpu.SemaphoreType.DMA((2,)),
            pltpu.SemaphoreType.DMA((2,)),
            pltpu.SemaphoreType.DMA((6, 3, 3)),
            pltpu.SemaphoreType.DMA((6, 3, 3)),
        ],
        compiler_params=pltpu.CompilerParams(
            collective_id=0, has_side_effects=True, vmem_limit_bytes=32 << 20
        ),
        name="exchange_all",
    )(slots, meta, w)


def small_sum_kernel(scale, p_ref, o_ref, land, rs_send, rs_recv, ag_send, ag_recv):
    dp = lax.axis_index("dp")
    tile = lax.axis_index("tile")
    me = dp * TILES + tile
    count = 2 * TILES
    barrier = pltpu.get_barrier_semaphore()

    def target(n):
        d = (me + n) % count
        return d, (d // TILES, d % TILES)

    def greet(n, carry):
        pl.semaphore_signal(barrier, inc=1, device_id=target(n)[1], device_id_type=MESH)
        return carry

    lax.fori_loop(1, count, greet, 0)
    pl.semaphore_wait(barrier, count - 1)

    def part(ref, d):
        return ref.at[
            pl.ds(pl.multiple_of(d // 4 * 16, 16), 16),
            pl.ds(pl.multiple_of(d % 4 * 128, 128), 128),
        ]

    def scatter(n):
        d, where = target(n)
        return pltpu.make_async_remote_copy(
            src_ref=part(p_ref, d), dst_ref=land.at[me],
            send_sem=rs_send, recv_sem=rs_recv, device_id=where, device_id_type=MESH,
        )

    def spread(n):
        d, where = target(n)
        return pltpu.make_async_remote_copy(
            src_ref=part(o_ref, me), dst_ref=part(o_ref, me),
            send_sem=ag_send, recv_sem=ag_recv, device_id=where, device_id_type=MESH,
        )

    def start(make):
        def one(n, carry):
            make(n).start()
            return carry

        lax.fori_loop(1, count, one, 0)

    rows = pl.ds(pl.multiple_of(me // 4 * 16, 16), 16)
    lanes = pl.ds(pl.multiple_of(me % 4 * 128, 128), 128)
    land[me] = p_ref[rows, lanes]
    start(scatter)
    everything = land.at[pl.ds(0, count - 1)]
    pltpu.make_async_copy(everything, everything, rs_recv).wait()
    pltpu.make_async_copy(everything, everything, rs_send).wait()
    total = jnp.sum(land[...].astype(F32), axis=0)
    o_ref[rows, lanes] = (total * scale).astype(BF)
    start(spread)
    pltpu.make_async_copy(everything, everything, ag_recv).wait()
    pltpu.make_async_copy(everything, everything, ag_send).wait()


def small_sum(scale, part):
    return pl.pallas_call(
        functools.partial(small_sum_kernel, scale),
        out_shape=jax.ShapeDtypeStruct(part.shape, BF),
        in_specs=[VMEM],
        out_specs=VMEM,
        scratch_shapes=[
            pltpu.VMEM((2 * TILES, 16, 128), BF),
            pltpu.SemaphoreType.DMA,
            pltpu.SemaphoreType.DMA,
            pltpu.SemaphoreType.DMA,
            pltpu.SemaphoreType.DMA,
        ],
        compiler_params=pltpu.CompilerParams(
            collective_id=1, has_side_effects=True, vmem_limit_bytes=8 << 20
        ),
        name="small_sum",
    )(part)


def edge_rows(block):
    count = lax.axis_size("tile")
    forward = [(i, i + 1) for i in range(count - 1)]
    backward = [(target, source) for source, target in forward]
    return lax.ppermute(block[-1:], "tile", forward), lax.ppermute(block[:1], "tile", backward)


def silu_slope(value):
    sigma = jax.nn.sigmoid(value)
    return sigma * (1.0 + value * (1.0 - sigma))


def earlier_count(hits):
    size = hits.shape[-1]
    before = lax.broadcasted_iota(jnp.int32, (size, size), 0) < lax.broadcasted_iota(
        jnp.int32, (size, size), 1
    )
    return jnp.dot(hits.astype(BF), before.astype(BF), preferred_element_type=F32).astype(jnp.int32)


def body(grad_out, bev_act, conv_weight, img_in, backbone_weight, route, offsets, frac_x, frac_y):
    my_tile = lax.axis_index("tile")
    g, act, image = grad_out[0], bev_act[0], img_in[0]
    rows, cols, chans = g.shape
    g_lo, g_hi = edge_rows(g)
    a_lo, a_hi = edge_rows(act)
    blocks = rows * cols // BLK
    per_device = image.shape[0] // PIXB

    owners = (route[0] // per_device).reshape(TILES, blocks)
    local_ids = (route[0] % per_device).reshape(TILES, blocks)
    my_owners = lax.dynamic_index_in_dim(owners, my_tile, 0, keepdims=False)
    same = my_owners[:, None] == my_owners[None, :]
    before = lax.broadcasted_iota(jnp.int32, (blocks, blocks), 1) < lax.broadcasted_iota(
        jnp.int32, (blocks, blocks), 0
    )
    my_slots = my_owners * CAP + jnp.sum((same & before).astype(jnp.int32), axis=1)
    chosen = my_slots[None, :] == lax.broadcasted_iota(jnp.int32, (TILES * CAP, blocks), 0)
    idx = jnp.sum(
        jnp.where(chosen, lax.broadcasted_iota(jnp.int32, chosen.shape, 1), 0), axis=1
    )
    cells = jnp.stack([offsets[0], frac_x[0], frac_y[0]]).astype(BF).reshape(3, blocks, BLK)
    meta = jnp.einsum("sk,rkm->srm", chosen.astype(BF), cells, preferred_element_type=F32).astype(BF)
    meta = meta.reshape(TILES, CAP, 3, BLK).transpose(0, 2, 1, 3).reshape(TILES, 3, CAP * BLK)
    meta = jnp.pad(meta, ((0, 0), (0, 13), (0, 0)))

    weights = conv_weight.transpose(1, 2, 0, 3).reshape(9, chans, chans)
    slots = bev_slots(idx, g, g_lo[0], g_hi[0], weights)

    act_frame = jnp.pad(jnp.concatenate([a_lo, act, a_hi], axis=0), ((0, 0), (1, 1), (0, 0)))
    parts = []
    for row_tap in range(3):
        for col_tap in range(3):
            moved = act_frame[row_tap : row_tap + rows, col_tap : col_tap + cols]
            parts.append(jnp.einsum("rvc,rvo->co", moved, g, preferred_element_type=F32).astype(BF))
    conv_local = jnp.stack(parts)
    cell_scale = 1.0 / math.sqrt(2 * TILES * rows * cols)
    pixel_scale = 1.0 / math.sqrt(2 * TILES * image.shape[0])
    arrived, arrived_meta, conv_sum = exchange_all(
        cell_scale, slots.reshape(TILES, CAP * BLK, chans), meta, conv_local
    )
    conv_grad = conv_sum.reshape(3, 3, chans, chans).transpose(2, 0, 1, 3)

    mine = owners == my_tile
    rank = earlier_count(mine)
    rank_iota = lax.broadcasted_iota(jnp.int32, (1, 1, CAP), 2)
    picked = mine[:, :, None] & (rank[:, :, None] == rank_iota)
    held = jnp.sum(jnp.where(picked, local_ids[:, :, None] + 1, 0), axis=1) - 1
    base = jnp.where(held >= 0, held * PIXB, -4 * PIXB)
    base = jnp.broadcast_to(base[:, :, None], (TILES, CAP, BLK)).reshape(-1, 1)
    info = arrived_meta[:, :3].astype(F32)
    left = base + info[:, 0].reshape(-1, 1).astype(jnp.int32)
    right_w = info[:, 1].reshape(-1, 1) / 256.0
    lower_w = info[:, 2].reshape(-1, 1) / 256.0
    gap = lax.broadcasted_iota(jnp.int32, (1, per_device * PIXB), 1) - left
    across = jnp.where((gap == 0) | (gap == IMGW), 1.0 - right_w, 0.0) + jnp.where(
        (gap == 1) | (gap == IMGW + 1), right_w, 0.0
    )
    band = (jnp.where(gap >= IMGW, lower_w, 1.0 - lower_w) * across).astype(BF)
    feature_grad = lax.dot_general(
        band,
        arrived.reshape(-1, chans),
        (((0,), (0,)), ((), ())),
        preferred_element_type=F32,
    )
    pre_act = jnp.dot(image, backbone_weight, preferred_element_type=F32)
    scaled = (feature_grad * silu_slope(pre_act)).astype(BF)
    image_grad = lax.dot_general(
        scaled, backbone_weight, (((1,), (1,)), ((), ())), preferred_element_type=F32
    ).astype(BF)
    backbone_local = lax.dot_general(
        image, scaled, (((0,), (0,)), ((), ())), preferred_element_type=F32
    ).astype(BF)
    backbone_grad = small_sum(pixel_scale, backbone_local)
    return (image_grad[None], conv_grad, backbone_grad)


def solution(mesh):
    return jax.shard_map(
        body,
        mesh=mesh,
        in_specs=(
            P("dp", "tile", None, None),
            P("dp", "tile", None, None),
            P(),
            P("dp", "tile", None),
            P(),
            P("dp", None),
            P("dp", "tile"),
            P("dp", "tile"),
            P("dp", "tile"),
        ),
        out_specs=(P("dp", "tile", None), P(), P()),
        check_vma=False,
    )
```

time: 592 us -> 277 us (0.47)
  waiting for transfers between devices: 394 us -> 0.01 us
  Pallas kernels: 0 us -> 205 us
  matrix products: 88.5 us -> 35.7 us
  local copies, waits for them, and re-layouts: 45.9 us -> 16.1 us
  other arithmetic: 24.4 us -> 5.53 us
  between operations: 14.6 us -> 1.09 us
  starting transfers between devices: 20.8 us -> 12.4 us
    pallas_call x0 -> x3, Pallas kernels: none -> 205 us  [the longest x1 154 us: exchange_all(): pl.pallas_call(functools.partial(exchange_kernel, scale), out_shape=[jax....]
    all_to_all x1 -> x0, waiting for transfers between devices: 194 us -> none  [body(): lax.all_to_all(outgoing.reshape(tiles, capacity, 2 * IMGW, chans), 'tile'...]
    psum x1 -> x0, waiting for transfers between devices: 189 us -> none  [body(): lax.psum((conv_local, backbone_local), ('dp', 'tile'))]
    dot_general x21 -> x13, matrix products: 85.8 us -> 33.9 us  [the longest x9 16.2 us: body(): jnp.einsum('rvc,rvo->co', moved, g, preferred_element_type=F32).astype(BF)]
    scatter x1 -> x0, local copies, waits for them, and re-layouts: 14.1 us -> none  [body(): jnp.zeros((slot_total, 2 * IMGW, chans), jnp.bfloat16).at[my_slots]]
    all_to_all x1 -> x0, starting transfers between devices: 13.9 us -> none  [body(): lax.all_to_all(outgoing.reshape(tiles, capacity, 2 * IMGW, chans), 'tile'...]
    ppermute x2 -> x4, waiting for transfers between devices: 11.6 us -> 0.01 us  [the longest x2 0.01 us: edge_rows(): lax.ppermute(block[-1:], 'tile', forward)]
    another operation x4 -> x3, other arithmetic: 10.9 us -> 0.13 us  [the longest x3 6.56 us: body(): conv_local = jnp.stack(conv_parts, axis=1)]
  transfers between devices with their start and end apart: 4 -> 4, of which waited for: 4 -> 0; matrix products, arithmetic and copies ran while one was open for 5% -> 9% of each run, Pallas kernels for 0% -> 0%
where the time goes in v1:
time: 277 us; the launch traced here: 276 us
  Pallas kernels  205 us (74%)
  matrix products  35.7 us (13%)
  local copies, waits for them, and re-layouts  16.1 us (6%)
  starting transfers between devices  12.4 us (4%)
  other arithmetic  5.53 us (2%)
    pallas_call x1, Pallas kernels, exchange_all(): pl.pallas_call(functools.partial(exchange_kernel, scale), out_shape=[jax....  154 us
    pallas_call x1, Pallas kernels, small_sum(): pl.pallas_call(functools.partial(small_sum_kernel, scale), out_shape=jax....  31.6 us
    pallas_call x1, Pallas kernels, bev_slots(): pl.pallas_call(bev_kernel, out_shape=jax.ShapeDtypeStruct((TILES * CAP, B...  19.4 us
    dot_general x9, matrix products, body(): jnp.einsum('rvc,rvo->co', moved, g, preferred_element_type=F32).astype(BF)  16.2 us
    dot_general x1, matrix products, body(): lax.dot_general(band, arrived.reshape(-1, chans), (((0,), (0,)), ((), ())...  15.9 us
    unnamed x27, local copies, waits for them, and re-layouts  11.2 us
    ppermute x2, starting transfers between devices, edge_rows(): lax.ppermute(block[-1:], 'tile', forward)  8.54 us
  transfers between devices with their start and end apart: 4, of which 0 were waited for; matrix products, arithmetic and copies ran while one was open for 9% of the time, Pallas kernels for 0%

profile of v1, /device:TPU:1, one launch (start us, length us, event | category | flops | bytes accessed | tf_op | source)
XLA Modules:
  0.0 276.3 jit_solution(7605186458445014531)
XLA Ops:
  0.7 4.5 %copy.54 = bf16[1,4,640,512]{2,3,1,0:T(8,128)(2,1)} copy(bf16[1,4,640,512]{3,2,1,0:T(8,128)(2,1)} %param.10) | data formatting | bytes 5242880 | tf_op args[1]
  5.2 2.5 slice_bitcast_fusion.1
  7.7 4.9 %collective-permute-start.2 = (bf16[1,640,512]{1,2,0:T(8,128)(2,1)}, bf16[1,640,512]{1,2,0:T(8,128)(2,1)}, u32[]{:S(2)}, u32[]{:S(2)}) collective-permute-start(bf16[1,640,512]{1,2,0:T(8,128)(2,1)} %get-tuple-element.11), channel_id=1, source_target_pairs={{0,1},{1,2},{2,3},{3,4},{4,5},{5,6},{6,7},{7,8},{8,9},{9,10},{10,1... | collective-permute-start | bytes 1966088 | tf_op jit(solution)/shard_map/ppermute | solution.py:490
  12.6 1.9 collective-permute-start.3
  14.6 1.1 slice_bitcast_fusion.2
  15.7 3.6 %collective-permute-start = (bf16[1,640,512]{2,1,0:T(8,128)(2,1)}, bf16[1,640,512]{2,1,0:T(8,128)(2,1)}, u32[]{:S(2)}, u32[]{:S(2)}) collective-permute-start(bf16[1,640,512]{2,1,0:T(8,128)(2,1)} %get-tuple-element.14), channel_id=1, source_target_pairs={{0,1},{1,2},{2,3},{3,4},{4,5},{5,6},{6,7},{7,8},{8,9},{9,10},{10,1... | collective-permute-start | bytes 1966088 | tf_op jit(solution)/shard_map/ppermute | solution.py:490
  19.4 1.9 collective-permute-start.1
  22.0 0.2 add_reduce_fusion
  22.6 0.2 convolution_convert_fusion.3
  22.8 0.2 convolution_convert_fusion.2
  23.8 1.5 fusion.159
  25.3 4.7 %fusion.23 = bf16[6,642,512]{1,2,0:T(8,128)(2,1)S(1)} fusion(bf16[1,640,512]{1,2,0:T(8,128)(2,1)} %collective-permute-done.3, bf16[4,640,512]{1,2,0:T(8,128)(2,1)} %bitcast.191, bf16[1,640,512]{1,2,0:T(8,128)(2,1)} %collective-permute-done.2), kind=kLoop, calls=%fused_computation.27 | loop fusion | flops 23666688 | bytes 7876608 | tf_op jit(solution)/shard_map/concatenate | solution.py:535
  30.1 1.5 fusion.111
  31.6 0.2 copy-done.3
  31.8 2.6 fusion.153
  34.4 1.6 fusion.117
  36.0 1.5 fusion.123
  37.6 0.2 copy-done.4
  37.8 1.6 fusion.105
  39.3 1.6 fusion.129
  41.0 1.5 fusion.135
  42.5 2.7 fusion.147
  45.2 1.6 fusion.141.w_ref
  46.8 19.4 %bev_slots.1 = bf16[128,64,512]{2,1,0:T(8,128)(2,1)} custom-call(s32[128]{0:T(128)S(1)} %select_reduce_fusion.1.idx_ref, bf16[4,640,512]{2,1,0:T(8,128)(2,1)S(1)} %bitcast.186, bf16[640,512]{1,0:T(8,128)(2,1)} %bitcast.4.lo_ref, bf16[640,512]{1,0:T(8,128)(2,1)} %bitcast.6.hi_ref, bf16[9,512,512]{2,1,0:T(8,128)(2,1)S(1)} %bitcast.190), custom_call_target="tpu_custom_call" | custom-call | flops 12079595520 | bytes 25165824 | tf_op jit(solution)/shard_map/bev_slots/pallas_call | solution.py:95
  66.3 154.4 %exchange_all.1 = (bf16[64,128,512]{2,1,0:T(8,128)(2,1)S(1)}, bf16[64,16,128]{2,1,0:T(8,128)(2,1)S(1)}, bf16[9,512,512]{2,1,0:T(8,128)(2,1)S(1)}) custom-call(bf16[64,128,512]{2,1,0:T(8,128)(2,1)} %bitcast.194, bf16[64,16,128]{2,1,0:T(8,128)(2,1)S(1)} %pad.8.m_ref, bf16[9,512,512]{2,1,0:T(8,128)(2,1)S(1)} %fusion.141.w_ref), custom_call_target="tpu_custom_call" | custom-call | tf_op jit(solution)/shard_map/exchange_all/pallas_call | solution.py:373
  220.7 3.2 %copy-done.2 = bf16[64,128,512]{2,1,0:T(8,128)(2,1)} copy-done((bf16[64,128,512]{2,1,0:T(8,128)(2,1)}, bf16[64,128,512]{2,1,0:T(8,128)(2,1)S(1)}, u32[]{:S(2)}) %copy-start.2) | copy-done | bytes 8388632
  224.1 15.9 %fusion.101 = bf16[512,512]{1,0:T(8,128)(2,1)S(1)} fusion(bf16[8192,512]{1,0:T(8,128)(2,1)} %bitcast.187, f32[8192]{0:T(1024)S(1)} %bitcast.198, f32[8192]{0:T(1024)S(1)} %get-tuple-element.18, f32[8192]{0:T(1024)S(1)} %get-tuple-element.19, f32[8192]{0:T(1024)S(1)} %bitcast.200, s32[8192]{0:T(1024)S(1)} %add.64, f32[512,512]{1,0:T(8,128)S(1)} %fusion.159), kind=kOutput, calls=%fused_computation.71 | convolution fusion | flops 4356046848 | bytes 10125312 | tf_op jit(solution)/shard_map/dot_general | solution.py:565
  239.9 0.5 fusion.157.p_ref
  240.4 1.3 fusion.156
  241.7 31.6 %small_sum.1 = bf16[512,512]{1,0:T(8,128)(2,1)S(1)} custom-call(bf16[512,512]{1,0:T(8,128)(2,1)S(1)} %fusion.157.p_ref), custom_call_target="tpu_custom_call" | custom-call | tf_op jit(solution)/shard_map/small_sum/pallas_call | solution.py:467
  273.4 2.2 copy.69
  275.5 0.8 copy.70
  (54 shorter events, 2.0 us)
Async XLA Ops:
  0.6 23.2 %copy-start = (bf16[1,512,512]{2,1,0:T(8,128)(2,1)S(1)}, bf16[1,512,512]{2,1,0:T(8,128)(2,1)}, u32[]{:S(2)}) copy-start(bf16[1,512,512]{2,1,0:T(8,128)(2,1)} %param.12) | copy-start | bytes 1572868
  0.6 13.9 %copy-start.1 = (bf16[1,4,640,512]{3,2,1,0:T(8,128)(2,1)S(1)}, bf16[1,4,640,512]{3,2,1,0:T(8,128)(2,1)}, u32[]{:S(2)}) copy-start(bf16[1,4,640,512]{3,2,1,0:T(8,128)(2,1)} %param.9) | copy-start | bytes 7864324
  0.7 20.6 %copy-start.6 = (s32[1,2560]{1,0:T(1,128)S(1)}, s32[1,2560]{1,0:T(1,128)}, u32[]{:S(2)}) copy-start(s32[1,2560]{1,0:T(1,128)} %param.14) | copy-start | bytes 30724
  0.7 21.5 %copy-start.7 = (s32[1,2560]{1,0:T(1,128)S(1)}, s32[1,2560]{1,0:T(1,128)}, u32[]{:S(2)}) copy-start(s32[1,2560]{1,0:T(1,128)} %param.15) | copy-start | bytes 30724
  0.7 21.7 %copy-start.8 = (s32[1,2560]{1,0:T(1,128)S(1)}, s32[1,2560]{1,0:T(1,128)}, u32[]{:S(2)}) copy-start(s32[1,2560]{1,0:T(1,128)} %param.16) | copy-start | bytes 30724
  0.7 21.8 %copy-start.9 = (s32[1,2560]{1,0:T(1,128)S(1)}, s32[1,2560]{1,0:T(1,128)}, u32[]{:S(2)}) copy-start(s32[1,2560]{1,0:T(1,128)} %param.17) | copy-start | bytes 30724
  7.7 17.6 %collective-permute-start.2 = (bf16[1,640,512]{1,2,0:T(8,128)(2,1)}, bf16[1,640,512]{1,2,0:T(8,128)(2,1)}, u32[]{:S(2)}, u32[]{:S(2)}) collective-permute-start(bf16[1,640,512]{1,2,0:T(8,128)(2,1)} %get-tuple-element.11), channel_id=1, source_target_pairs={{0,1},{1,2},{2,3},{3,4},{4,5},{5,6},{6,7},{7,8},{8,9},{9,10},{10,1... | collective-permute-start | bytes 1966088 | tf_op jit(solution)/shard_map/ppermute | solution.py:490
  12.6 12.7 %collective-permute-start.3 = (bf16[1,640,512]{1,2,0:T(8,128)(2,1)}, bf16[1,640,512]{1,2,0:T(8,128)(2,1)}, u32[]{:S(2)}, u32[]{:S(2)}) collective-permute-start(bf16[1,640,512]{1,2,0:T(8,128)(2,1)} %get-tuple-element.12), channel_id=1, source_target_pairs={{1,0},{2,1},{3,2},{4,3},{5,4},{6,5},{7,6},{8,7},{9,8},{10,9},{11,1... | collective-permute-start | bytes 1966088 | tf_op jit(solution)/shard_map/ppermute | solution.py:490
  15.7 31.1 %collective-permute-start = (bf16[1,640,512]{2,1,0:T(8,128)(2,1)}, bf16[1,640,512]{2,1,0:T(8,128)(2,1)}, u32[]{:S(2)}, u32[]{:S(2)}) collective-permute-start(bf16[1,640,512]{2,1,0:T(8,128)(2,1)} %get-tuple-element.14), channel_id=1, source_target_pairs={{0,1},{1,2},{2,3},{3,4},{4,5},{5,6},{6,7},{7,8},{8,9},{9,10},{10,1... | collective-permute-start | bytes 1966088 | tf_op jit(solution)/shard_map/ppermute | solution.py:490
  19.4 27.4 %collective-permute-start.1 = (bf16[1,640,512]{2,1,0:T(8,128)(2,1)}, bf16[1,640,512]{2,1,0:T(8,128)(2,1)}, u32[]{:S(2)}, u32[]{:S(2)}) collective-permute-start(bf16[1,640,512]{2,1,0:T(8,128)(2,1)} %get-tuple-element.13), channel_id=1, source_target_pairs={{1,0},{2,1},{3,2},{4,3},{5,4},{6,5},{7,6},{8,7},{9,8},{10,9},{11,1... | collective-permute-start | bytes 1966088 | tf_op jit(solution)/shard_map/ppermute | solution.py:490
  30.1 1.7 copy-start.3
  36.0 1.7 copy-start.4
  40.9 5.8 %slice-start = ((s8[4718592]{0:T(1024)(128)(4,1)}), s8[4194304]{0:T(1024)(128)(4,1)S(1)}, s32[]{:S(2)}) async-start(s8[4718592]{0:T(1024)(128)(4,1)} %bitcast.188), calls=%async_computation | async-start | bytes 8388608
  42.5 4.3 %slice-start.1 = ((s8[4718592]{0:T(1024)(128)(4,1)}), s8[524288]{0:T(1024)(128)(4,1)S(1)}, s32[]{:S(2)}) async-start(s8[4718592]{0:T(1024)(128)(4,1)} %bitcast.188), calls=%async_computation.1 | async-start | bytes 1048576
  220.7 3.2 %copy-start.2 = (bf16[64,128,512]{2,1,0:T(8,128)(2,1)}, bf16[64,128,512]{2,1,0:T(8,128)(2,1)S(1)}, u32[]{:S(2)}) copy-start(bf16[64,128,512]{2,1,0:T(8,128)(2,1)S(1)} %get-tuple-element.7) | copy-start | bytes 25165828
  224.1 16.4 %copy-start.5 = (bf16[512,512]{1,0:T(8,128)(2,1)S(1)}, bf16[512,512]{1,0:T(8,128)(2,1)}, u32[]{:S(2)}) copy-start(bf16[512,512]{1,0:T(8,128)(2,1)} %param.13) | copy-start | bytes 1572868

commit v2 on v1

v2 whole, which is shorter than its diff:
```python
import functools
import math

import jax
import jax.numpy as jnp
from jax import lax
from jax.experimental import pallas as pl
from jax.experimental.pallas import tpu as pltpu
from jax.sharding import PartitionSpec as P

BLK = 64
IMGW = 64
PIXB = 2 * IMGW
TILES = 64
CAP = 2
MESH = pl.DeviceIdType.MESH
ANY = pl.BlockSpec(memory_space=pl.ANY)
VMEM = pl.BlockSpec(memory_space=pltpu.VMEM)
SMEM = pl.BlockSpec(memory_space=pltpu.SMEM)
BF = jnp.bfloat16
F32 = jnp.float32


def coords():
    t = lax.axis_index("tile")
    return t // 16, (t // 8) % 2 * 2 + lax.axis_index("dp"), (t // 2) % 4, t % 2


def device(y, x, z, core):
    return (x % 2, ((y * 2 + x // 2) * 4 + z) * 2 + core)


def along(axis, step):
    y, x, z, core = coords()
    if axis == "y":
        y = (y + step) % 4
    elif axis == "x":
        x = (x + step) % 4
    elif axis == "z":
        z = (z + step) % 4
    else:
        core = 1 - core
    return device(y, x, z, core)


def bev_kernel(idx_ref, g_ref, lo_ref, hi_ref, w_ref, sa_ref, sb_ref, frame, w, acc, bev, sems, out_sem):
    rows, cols = g_ref.shape[0], g_ref.shape[1]
    copies = [
        pltpu.make_async_copy(w_ref, w, sems.at[0]),
        pltpu.make_async_copy(g_ref, frame.at[pl.ds(1, rows)], sems.at[1]),
        pltpu.make_async_copy(lo_ref, frame.at[0], sems.at[2]),
        pltpu.make_async_copy(hi_ref, frame.at[rows + 1], sems.at[3]),
    ]
    for copy in copies:
        copy.start()
    for copy in copies:
        copy.wait()
    half = 256

    def step(s, carry):
        r, n = s // 2, s % 2
        lanes = pl.ds(pl.multiple_of(n * half, half), half)

        def tap(j):
            total = None
            for i in range(3):
                term = lax.dot_general(
                    frame[r + 2 - i],
                    w[i * 3 + j, lanes, :],
                    (((1,), (1,)), ((), ())),
                    preferred_element_type=F32,
                )
                total = term if total is None else total + term
            return total

        acc[pl.ds(8, cols), :] = tap(1)
        acc[pl.ds(7, cols), :] += tap(0)
        acc[pl.ds(9, cols), :] += tap(2)
        bev[n, pl.ds(pl.multiple_of(r * cols, cols), cols), :] = acc[pl.ds(8, cols), :].astype(BF)
        return carry

    lax.fori_loop(0, 2 * rows, step, 0)

    def send(s, carry):
        start = pl.multiple_of(idx_ref[s] * BLK, BLK)
        rows_of = pl.ds(start, BLK)
        pltpu.make_async_copy(bev.at[0, rows_of], sa_ref.at[s], out_sem.at[0]).start()
        pltpu.make_async_copy(bev.at[1, rows_of], sb_ref.at[s], out_sem.at[1]).start()
        return carry

    lax.fori_loop(0, TILES * CAP, send, 0)
    pltpu.make_async_copy(sa_ref, sa_ref, out_sem.at[0]).wait()
    pltpu.make_async_copy(sb_ref, sb_ref, out_sem.at[1]).wait()


def bev_slots(idx, g, lo, hi, w):
    rows, cols, chans = g.shape
    return pl.pallas_call(
        bev_kernel,
        out_shape=[jax.ShapeDtypeStruct((TILES * CAP, BLK, chans // 2), BF)] * 2,
        in_specs=[SMEM, ANY, ANY, ANY, ANY],
        out_specs=[ANY, ANY],
        scratch_shapes=[
            pltpu.VMEM((rows + 2, cols, chans), BF),
            pltpu.VMEM(w.shape, BF),
            pltpu.VMEM((cols + 16, 256), F32),
            pltpu.VMEM((2, rows * cols, chans // 2), BF),
            pltpu.SemaphoreType.DMA((4,)),
            pltpu.SemaphoreType.DMA((2,)),
        ],
        compiler_params=pltpu.CompilerParams(vmem_limit_bytes=40 << 20),
        cost_estimate=pl.CostEstimate(
            flops=2 * 9 * rows * cols * chans * chans, bytes_accessed=24 << 20, transcendentals=0
        ),
        name="bev_slots",
    )(idx, g, lo, hi, w)


NPIX = 4 * PIXB
CELLS = CAP * BLK
GROUP = 8


def exchange_kernel(
    scale, sa_ref, sb_ref, m_ref, w_ref, f_ref, o_ref,
    land, meta, band, dense, land2, sums, land3, recv0, acc0, recv1, acc1, recv2,
    m_send, m_recv, p1_send, p1_recv, own_sem, p2_send, p2_recv, p3_send, p3_recv,
    pair_send, pair_recv, x_send, x_recv, yz_send, yz_recv,
):
    y, x, z, core = coords()
    x_hi = x // 2

    def remote(src, dst, sends, recvs, where):
        return pltpu.make_async_remote_copy(
            src_ref=src, dst_ref=dst, send_sem=sends, recv_sem=recvs,
            device_id=where, device_id_type=MESH,
        )

    plane = [(dy, dz) for dy in range(4) for dz in range(4) if dy or dz]

    def at(dy, dz, dc):
        return device((y + dy) % 4, x, (z + dz) % 4, (core + dc) % 2)

    barrier = pltpu.get_barrier_semaphore()
    greeted = [at(0, 0, 1)] + [at(dy, dz, 0) for dy, dz in plane]
    greeted += [at(dy, dz, 1) for dy, dz in plane if not (dy and dz)]
    greeted += [along("x", d) for d in (1, 2, 3)]
    for where in greeted:
        pl.semaphore_signal(barrier, inc=1, device_id=where, device_id_type=MESH)
    pl.semaphore_wait(barrier, len(greeted))

    line = (z, y)
    here = [line[h] * 2 + core for h in range(2)]

    def slots_of(h, member):
        return sa_ref.at[:, member] if h == 0 else sb_ref.at[member // 2, :, member % 2]

    steps = [(d, dc) for d in range(4) for dc in range(2) if d or dc]

    def member_at(h, d, dc):
        return (line[h] + d) % 4 * 2 + (core + dc) % 2

    def group_copy(h, k, sign, which):
        d, dc = steps[k]
        member = member_at(h, d if sign > 0 else 4 - d, dc)
        where = at(0, d, dc) if h == 0 else at(d, 0, dc)
        place = here[h] if sign > 0 else member
        if which == "meta":
            return remote(
                mb(h, member), meta.at[h, place], m_send.at[h, k], m_recv.at[h, k], where
            )
        return remote(
            slots_of(h, member), land.at[h, place], p1_send.at[h, k], p1_recv.at[h, k], where
        )

    def mb(h, member):
        return m_ref.at[0, :, member] if h == 0 else m_ref.at[1, :, member]

    own = []
    for h in range(2):
        own.append(pltpu.make_async_copy(mb(h, here[h]), meta.at[h, here[h]], own_sem.at[h, 0]))
        own.append(
            pltpu.make_async_copy(slots_of(h, here[h]), land.at[h, here[h]], own_sem.at[h, 1])
        )
    for copy in own:
        copy.start()
    for k in range(7):
        for h in range(2):
            group_copy(h, k, 1, "meta").start()

    half = w_ref.shape[1] // 2
    mine = pl.ds(pl.multiple_of(core * half, half), half)
    other = pl.ds(pl.multiple_of((1 - core) * half, half), half)
    pair = remote(
        w_ref.at[:, other], recv0, pair_send.at[0], pair_recv.at[0], at(0, 0, 1)
    )
    pair.start()
    for k in range(7):
        for h in range(2):
            group_copy(h, k, 1, "slots").start()
    pair.wait()

    def add0(k, carry):
        acc0[k] = (w_ref[k, mine, :].astype(F32) + recv0[k].astype(F32)).astype(BF)
        return carry

    lax.fori_loop(0, w_ref.shape[0], add0, 0)

    def rows64(q):
        return pl.ds(pl.multiple_of(q * 64, 64), 64)

    along_x = [
        remote(
            acc0.at[:, rows64((x + d) % 4)], recv1.at[d - 1],
            x_send.at[0, d - 1], x_recv.at[0, d - 1], along("x", d),
        )
        for d in (1, 2, 3)
    ]
    for copy in along_x:
        copy.start()

    for k in range(7):
        for h in range(2):
            group_copy(h, k, 1, "meta").wait_send()
            group_copy(h, k, -1, "meta").wait_recv()
    own[0].wait()
    own[2].wait()

    def make_band(n, carry):
        h, owner, member = n // 64, n // 8 % 8, n % 8
        info = meta[h, member, owner].astype(F32)
        q = lax.broadcasted_iota(jnp.int32, (IMGW, CELLS), 0).astype(F32)
        left, right = q == info[0:1], q == info[0:1] + 1.0
        zero = jnp.zeros((IMGW, CELLS), F32)
        upper = jnp.where(left, info[2:3], jnp.where(right, info[3:4], zero))
        lower = jnp.where(left, info[4:5], jnp.where(right, info[5:6], zero))
        whole = jnp.concatenate([upper, lower], axis=0)
        lanes = pl.ds(pl.multiple_of(member * CELLS, CELLS), CELLS)
        for block in range(4):
            kept = jnp.where(info[1:2] == float(block), whole, 0.0)
            band[h, owner, pl.ds(block * PIXB, PIXB), lanes] = kept.astype(BF)
        return carry

    lax.fori_loop(0, 128, make_band, 0)

    for copy in along_x:
        copy.wait()

    def add1(k, carry):
        total = acc0[k, rows64(x), :].astype(F32)
        for d in range(3):
            total = total + recv1[d, k].astype(F32)
        acc1[k] = total.astype(BF)
        return carry

    lax.fori_loop(0, w_ref.shape[0], add1, 0)

    def rows16(ref, base, q_y, q_z):
        return ref.at[
            :,
            pl.ds(pl.multiple_of(base + q_y * 16, 16), 16),
            pl.ds(pl.multiple_of(q_z * 128, 128), 128),
        ]

    to_plane = [
        remote(
            rows16(acc1, 0, (y + dy) % 4, (z + dz) % 4), recv2.at[k],
            yz_send.at[0, k], yz_recv.at[0, k], at(dy, dz, 0),
        )
        for k, (dy, dz) in enumerate(plane)
    ]
    for copy in to_plane:
        copy.start()

    def reduce_half(h):
        for k in range(7):
            group_copy(h, k, 1, "slots").wait_send()
            group_copy(h, k, -1, "slots").wait_recv()
        own[2 * h + 1].wait()

        def one(owner, carry):
            cells = land[h, :, owner].reshape(GROUP * CELLS, land.shape[-1])
            dense[h, owner] = jnp.dot(
                band[h, owner], cells, preferred_element_type=F32
            ).astype(BF)
            return carry

        lax.fori_loop(0, GROUP, one, 0)

    def dense_part(h, x_part, q):
        return dense.at[h, q * 2 + x_part] if h == 0 else dense.at[h, x_part * 4 + q]

    cross = (y, z)

    def second(h):
        return [
            remote(
                dense_part(h, x_part, (cross[h] + d) % 4), land2.at[h, x_part, d - 1],
                p2_send.at[h, x_part, d - 1], p2_recv.at[h, x_part, d - 1],
                at(d, 0, 0) if h == 0 else at(0, d, 0),
            )
            for x_part in range(2)
            for d in (1, 2, 3)
        ]

    reduce_half(0)
    for copy in to_plane:
        copy.wait()

    def add2(k, carry):
        total = acc1[
            k, pl.ds(pl.multiple_of(y * 16, 16), 16), pl.ds(pl.multiple_of(z * 128, 128), 128)
        ].astype(F32)
        for p in range(15):
            total = total + recv2[p, k].astype(F32)
        o_ref[
            k,
            pl.ds(pl.multiple_of(core * half + x * 64 + y * 16, 16), 16),
            pl.ds(pl.multiple_of(z * 128, 128), 128),
        ] = (total * scale).astype(BF)
        return carry

    lax.fori_loop(0, w_ref.shape[0], add2, 0)
    base = core * half + x * 64

    def spread(k, sign):
        dy, dz = plane[k]
        part = rows16(o_ref, base, (y + sign * dy + 4) % 4, (z + sign * dz + 4) % 4)
        if sign == 0:
            part = rows16(o_ref, base, y, z)
        return remote(part, part, yz_send.at[1, k], yz_recv.at[1, k], at(dy, dz, 0))

    for k in range(15):
        spread(k, 0).start()
    second0 = second(0)
    for copy in second0:
        copy.start()
    reduce_half(1)
    second1 = second(1)
    for copy in second1:
        copy.start()
    for k in range(15):
        spread(k, 0).wait_send()
        spread(k, -1).wait_recv()

    def strip(d, sign):
        part = o_ref.at[:, rows64(core * 4 + (x + sign * d + 4) % 4)]
        return remote(part, part, x_send.at[1, d - 1], x_recv.at[1, d - 1], along("x", d))

    for d in (1, 2, 3):
        strip(d, 0).start()

    for copy in second0 + second1:
        copy.wait()

    def add3(h, x_part):
        start = dense[h, cross[h] * 2 + x_part] if h == 0 else dense[h, x_part * 4 + cross[h]]
        total = start.astype(F32)
        for d in range(3):
            total = total + land2[h, x_part, d].astype(F32)
        return total

    third = []
    for h in range(2):
        sums[h] = add3(h, 1 - x_hi).astype(BF)
        third.append(
            remote(sums.at[h], land3.at[h], p3_send.at[h], p3_recv.at[h], along("x", 2))
        )
        third[h].start()
    lanes_of = (pl.ds(0, 256), pl.ds(256, 256))
    for h in range(2):
        f_ref[:, lanes_of[h]] = add3(h, x_hi)

    for d in (1, 2, 3):
        strip(d, 0).wait_send()
        strip(d, -1).wait_recv()
    back = remote(
        o_ref.at[:, mine], o_ref.at[:, mine], pair_send.at[1], pair_recv.at[1], at(0, 0, 1)
    )
    back.start()
    for h in range(2):
        third[h].wait()
        f_ref[:, lanes_of[h]] += land3[h].astype(F32)
    back.wait_send()
    remote(
        o_ref.at[:, other], o_ref.at[:, other], pair_send.at[1], pair_recv.at[1], at(0, 0, 1)
    ).wait_recv()


def exchange_all(scale, slots, meta, w):
    taps, rows, chans = w.shape
    half = rows // 2
    wide = chans // 2
    dma = pltpu.SemaphoreType.DMA
    return pl.pallas_call(
        functools.partial(exchange_kernel, scale),
        out_shape=[
            jax.ShapeDtypeStruct((NPIX, chans), F32),
            jax.ShapeDtypeStruct(w.shape, BF),
        ],
        in_specs=[ANY, ANY, ANY, VMEM],
        out_specs=[VMEM, VMEM],
        scratch_shapes=[
            pltpu.VMEM((2, GROUP, GROUP, CELLS, wide), BF),
            pltpu.VMEM((2, GROUP, GROUP, 16, CELLS), BF),
            pltpu.VMEM((2, GROUP, NPIX, GROUP * CELLS), BF),
            pltpu.VMEM((2, GROUP, NPIX, wide), BF),
            pltpu.VMEM((2, 2, 3, NPIX, wide), BF),
            pltpu.VMEM((2, NPIX, wide), BF),
            pltpu.VMEM((2, NPIX, wide), BF),
            pltpu.VMEM((taps, half, chans), BF),
            pltpu.VMEM((taps, half, chans), BF),
            pltpu.VMEM((3, taps, 64, chans), BF),
            pltpu.VMEM((taps, 64, chans), BF),
            pltpu.VMEM((15, taps, 16, 128), BF),
            dma((2, 7)), dma((2, 7)), dma((2, 7)), dma((2, 7)), dma((2, 2)),
            dma((2, 2, 3)), dma((2, 2, 3)), dma((2,)), dma((2,)),
            dma((2,)), dma((2,)), dma((2, 3)), dma((2, 3)), dma((2, 15)), dma((2, 15)),
        ],
        compiler_params=pltpu.CompilerParams(
            collective_id=0, has_side_effects=True, vmem_limit_bytes=60 << 20
        ),
        name="exchange_all",
    )(*slots, meta, w)


def small_sum_kernel(scale, p_ref, o_ref, land, rs_send, rs_recv, ag_send, ag_recv):
    dp = lax.axis_index("dp")
    tile = lax.axis_index("tile")
    me = dp * TILES + tile
    count = 2 * TILES
    barrier = pltpu.get_barrier_semaphore()

    def target(n):
        d = (me + n) % count
        return d, (d // TILES, d % TILES)

    def greet(n, carry):
        pl.semaphore_signal(barrier, inc=1, device_id=target(n)[1], device_id_type=MESH)
        return carry

    lax.fori_loop(1, count, greet, 0)
    pl.semaphore_wait(barrier, count - 1)

    def part(ref, d):
        return ref.at[
            pl.ds(pl.multiple_of(d // 4 * 16, 16), 16),
            pl.ds(pl.multiple_of(d % 4 * 128, 128), 128),
        ]

    def scatter(n):
        d, where = target(n)
        return pltpu.make_async_remote_copy(
            src_ref=part(p_ref, d), dst_ref=land.at[me],
            send_sem=rs_send, recv_sem=rs_recv, device_id=where, device_id_type=MESH,
        )

    def spread(n):
        d, where = target(n)
        return pltpu.make_async_remote_copy(
            src_ref=part(o_ref, me), dst_ref=part(o_ref, me),
            send_sem=ag_send, recv_sem=ag_recv, device_id=where, device_id_type=MESH,
        )

    def start(make):
        def one(n, carry):
            make(n).start()
            return carry

        lax.fori_loop(1, count, one, 0)

    rows = pl.ds(pl.multiple_of(me // 4 * 16, 16), 16)
    lanes = pl.ds(pl.multiple_of(me % 4 * 128, 128), 128)
    land[me] = p_ref[rows, lanes]
    start(scatter)
    everything = land.at[pl.ds(0, count - 1)]
    pltpu.make_async_copy(everything, everything, rs_recv).wait()
    pltpu.make_async_copy(everything, everything, rs_send).wait()
    total = jnp.sum(land[...].astype(F32), axis=0)
    o_ref[rows, lanes] = (total * scale).astype(BF)
    start(spread)
    pltpu.make_async_copy(everything, everything, ag_recv).wait()
    pltpu.make_async_copy(everything, everything, ag_send).wait()


def small_sum(scale, part):
    return pl.pallas_call(
        functools.partial(small_sum_kernel, scale),
        out_shape=jax.ShapeDtypeStruct(part.shape, BF),
        in_specs=[VMEM],
        out_specs=VMEM,
        scratch_shapes=[
            pltpu.VMEM((2 * TILES, 16, 128), BF),
            pltpu.SemaphoreType.DMA,
            pltpu.SemaphoreType.DMA,
            pltpu.SemaphoreType.DMA,
            pltpu.SemaphoreType.DMA,
        ],
        compiler_params=pltpu.CompilerParams(
            collective_id=1, has_side_effects=True, vmem_limit_bytes=8 << 20
        ),
        name="small_sum",
    )(part)


def edge_rows(block):
    count = lax.axis_size("tile")
    forward = [(i, i + 1) for i in range(count - 1)]
    backward = [(target, source) for source, target in forward]
    return lax.ppermute(block[-1:], "tile", forward), lax.ppermute(block[:1], "tile", backward)


def silu_slope(value):
    sigma = jax.nn.sigmoid(value)
    return sigma * (1.0 + value * (1.0 - sigma))


def body(grad_out, bev_act, conv_weight, img_in, backbone_weight, route, offsets, frac_x, frac_y):
    my_tile = lax.axis_index("tile")
    g, act, image = grad_out[0], bev_act[0], img_in[0]
    rows, cols, chans = g.shape
    g_lo, g_hi = edge_rows(g)
    a_lo, a_hi = edge_rows(act)
    blocks = rows * cols // BLK
    per_device = image.shape[0] // PIXB

    owners = (route[0] // per_device).reshape(TILES, blocks)
    local_ids = (route[0] % per_device).reshape(TILES, blocks)
    my_owners = lax.dynamic_index_in_dim(owners, my_tile, 0, keepdims=False)
    same = my_owners[:, None] == my_owners[None, :]
    before = lax.broadcasted_iota(jnp.int32, (blocks, blocks), 1) < lax.broadcasted_iota(
        jnp.int32, (blocks, blocks), 0
    )
    my_slots = my_owners * CAP + jnp.sum((same & before).astype(jnp.int32), axis=1)
    chosen = my_slots[None, :] == lax.broadcasted_iota(jnp.int32, (TILES * CAP, blocks), 0)
    idx = jnp.sum(
        jnp.where(chosen, lax.broadcasted_iota(jnp.int32, chosen.shape, 1), 0), axis=1
    )
    right_w = frac_x[0].astype(F32) / 256.0
    lower_w = frac_y[0].astype(F32) / 256.0
    cells = jnp.stack(
        [
            offsets[0].astype(F32),
            (1.0 - lower_w) * (1.0 - right_w),
            (1.0 - lower_w) * right_w,
            lower_w * (1.0 - right_w),
            lower_w * right_w,
        ]
    )
    cells = cells.astype(BF).reshape(5, blocks, BLK)
    info = jnp.einsum("sk,rkm->srm", chosen.astype(BF), cells, preferred_element_type=F32)
    my_local = lax.dynamic_index_in_dim(local_ids, my_tile, 0, keepdims=False)
    held = jnp.sum(jnp.where(chosen, my_local[None, :] + 1, 0), axis=1) - 1
    held = jnp.broadcast_to(held.astype(F32)[:, None, None], (TILES * CAP, 1, BLK))
    info = jnp.concatenate([info[:, :1], held, info[:, 1:]], axis=1).astype(BF)
    info = info.reshape(TILES, CAP, 6, BLK).transpose(0, 2, 1, 3).reshape(TILES, 6, CELLS)
    info = jnp.pad(info, ((0, 0), (0, 10), (0, 0)))
    by_z = info.reshape(8, 8, 16, CELLS)
    by_y = info.reshape(4, 8, 2, 16, CELLS).transpose(1, 0, 2, 3, 4).reshape(8, 8, 16, CELLS)
    meta = jnp.stack([by_z, by_y])

    weights = conv_weight.transpose(1, 2, 0, 3).reshape(9, chans, chans)
    slot_z, slot_y = bev_slots(idx, g, g_lo[0], g_hi[0], weights)
    slot_z = slot_z.reshape(8, 8, CELLS, chans // 2)
    slot_y = slot_y.reshape(4, 8, 2, CELLS, chans // 2)

    act_frame = jnp.pad(jnp.concatenate([a_lo, act, a_hi], axis=0), ((0, 0), (1, 1), (0, 0)))
    parts = []
    for row_tap in range(3):
        for col_tap in range(3):
            moved = act_frame[row_tap : row_tap + rows, col_tap : col_tap + cols]
            parts.append(jnp.einsum("rvc,rvo->co", moved, g, preferred_element_type=F32).astype(BF))
    conv_local = jnp.stack(parts)
    cell_scale = 1.0 / math.sqrt(2 * TILES * rows * cols)
    pixel_scale = 1.0 / math.sqrt(2 * TILES * image.shape[0])
    feature_grad, conv_sum = exchange_all(cell_scale, (slot_z, slot_y), meta, conv_local)
    conv_grad = conv_sum.reshape(3, 3, chans, chans).transpose(2, 0, 1, 3)

    pre_act = jnp.dot(image, backbone_weight, preferred_element_type=F32)
    scaled = (feature_grad * silu_slope(pre_act)).astype(BF)
    image_grad = lax.dot_general(
        scaled, backbone_weight, (((1,), (1,)), ((), ())), preferred_element_type=F32
    ).astype(BF)
    backbone_local = lax.dot_general(
        image, scaled, (((0,), (0,)), ((), ())), preferred_element_type=F32
    ).astype(BF)
    backbone_grad = small_sum(pixel_scale, backbone_local)
    return (image_grad[None], conv_grad, backbone_grad)


def solution(mesh):
    return jax.shard_map(
        body,
        mesh=mesh,
        in_specs=(
            P("dp", "tile", None, None),
            P("dp", "tile", None, None),
            P(),
            P("dp", "tile", None),
            P(),
            P("dp", None),
            P("dp", "tile"),
            P("dp", "tile"),
            P("dp", "tile"),
        ),
        out_specs=(P("dp", "tile", None), P(), P()),
        check_vma=False,
    )
```

time: 277 us -> 247 us (0.89)
  Pallas kernels: 205 us -> 185 us
  matrix products: 35.7 us -> 20.6 us
  local copies, waits for them, and re-layouts: 16.1 us -> 18.9 us
    pallas_call x1, Pallas kernels: 154 us -> 124 us  [exchange_all(): pl.pallas_call(functools.partial(exchange_kernel, scale), out_shape=[jax....]
    dot_general x2 -> x0, matrix products: 16.1 us -> none  [the longest x1 15.9 us: body(): lax.dot_general(band, arrived.reshape(-1, chans), (((0,), (0,)), ((), ())...]
    pallas_call x1, Pallas kernels: 19.4 us -> 29.3 us  [bev_slots(): pl.pallas_call(bev_kernel, out_shape=[jax.ShapeDtypeStruct((TILES * CAP,...]
    unnamed x27 -> x36, local copies, waits for them, and re-layouts: 11.2 us -> 14 us
  transfers between devices with their start and end apart: 4 -> 4, of which waited for: 0 -> 0; matrix products, arithmetic and copies ran while one was open for 9% -> 11% of each run, Pallas kernels for 0% -> 0%
where the time goes in v2:
time: 247 us; the launch traced here: 246 us
  Pallas kernels  185 us (75%)
  matrix products  20.6 us (8%)
  local copies, waits for them, and re-layouts  18.9 us (8%)
  starting transfers between devices  12.4 us (5%)
  other arithmetic  7.98 us (3%)
    pallas_call x1, Pallas kernels, exchange_all(): pl.pallas_call(functools.partial(exchange_kernel, scale), out_shape=[jax....  124 us
    pallas_call x1, Pallas kernels, small_sum(): pl.pallas_call(functools.partial(small_sum_kernel, scale), out_shape=jax....  32.1 us
    pallas_call x1, Pallas kernels, bev_slots(): pl.pallas_call(bev_kernel, out_shape=[jax.ShapeDtypeStruct((TILES * CAP,...  29.3 us
    dot_general x9, matrix products, body(): jnp.einsum('rvc,rvo->co', moved, g, preferred_element_type=F32).astype(BF)  16.1 us
    unnamed x36, local copies, waits for them, and re-layouts  14 us
    ppermute x2, starting transfers between devices, edge_rows(): lax.ppermute(block[-1:], 'tile', forward)  8.54 us
  transfers between devices with their start and end apart: 4, of which 0 were waited for; matrix products, arithmetic and copies ran while one was open for 11% of the time, Pallas kernels for 0%

profile of v2, /device:TPU:1, one launch (start us, length us, event | category | flops | bytes accessed | tf_op | source)
XLA Modules:
  0.0 246.4 jit_solution(11772905334030954955)
XLA Ops:
  0.7 4.5 %copy.31 = bf16[1,4,640,512]{2,3,1,0:T(8,128)(2,1)} copy(bf16[1,4,640,512]{3,2,1,0:T(8,128)(2,1)} %param.10) | data formatting | bytes 5242880 | tf_op args[1]
  5.2 2.5 %slice_bitcast_fusion.1 = (bf16[1,640,512]{1,2,0:T(8,128)(2,1)}, bf16[1,640,512]{1,2,0:T(8,128)(2,1)}) fusion(bf16[1,4,640,512]{2,3,1,0:T(8,128)(2,1)} %copy.31), kind=kLoop, calls=%fused_computation.73 | loop fusion | bytes 2621440 | tf_op jit(solution)/shard_map/slice | solution.py:510
  7.7 4.9 %collective-permute-start.2 = (bf16[1,640,512]{1,2,0:T(8,128)(2,1)}, bf16[1,640,512]{1,2,0:T(8,128)(2,1)}, u32[]{:S(2)}, u32[]{:S(2)}) collective-permute-start(bf16[1,640,512]{1,2,0:T(8,128)(2,1)} %get-tuple-element.21), channel_id=1, source_target_pairs={{0,1},{1,2},{2,3},{3,4},{4,5},{5,6},{6,7},{7,8},{8,9},{9,10},{10,1... | collective-permute-start | bytes 1966088 | tf_op jit(solution)/shard_map/ppermute | solution.py:510
  12.6 1.9 collective-permute-start.3
  14.6 1.1 slice_bitcast_fusion.2
  15.7 3.6 %collective-permute-start = (bf16[1,640,512]{2,1,0:T(8,128)(2,1)}, bf16[1,640,512]{2,1,0:T(8,128)(2,1)}, u32[]{:S(2)}, u32[]{:S(2)}) collective-permute-start(bf16[1,640,512]{2,1,0:T(8,128)(2,1)} %get-tuple-element.24), channel_id=1, source_target_pairs={{0,1},{1,2},{2,3},{3,4},{4,5},{5,6},{6,7},{7,8},{8,9},{9,10},{10,1... | collective-permute-start | bytes 1966088 | tf_op jit(solution)/shard_map/ppermute | solution.py:510
  19.4 1.9 collective-permute-start.1
  22.4 0.2 convolution_convert_fusion.2
  23.3 0.3 maximum_bitcast_fusion
  23.9 0.8 pad_maximum_fusion.m_ref
  24.8 2.5 %fusion.139 = f32[512,512]{1,0:T(8,128)} fusion(bf16[512,512]{1,0:T(8,128)(2,1)} %param.13, bf16[1,512,512]{2,1,0:T(8,128)(2,1)S(1)} %copy-done), kind=kOutput, calls=%fused_computation.78 | convolution fusion | flops 268435456 | bytes 2097152 | tf_op jit(solution)/shard_map/dot_general | solution.py:579
  27.3 4.5 %fusion.5 = bf16[6,642,512]{1,2,0:T(8,128)(2,1)S(1)} fusion(bf16[1,640,512]{1,2,0:T(8,128)(2,1)} %collective-permute-done.3, bf16[4,640,512]{1,2,0:T(8,128)(2,1)S(1)} %bitcast.198, bf16[1,640,512]{1,2,0:T(8,128)(2,1)} %collective-permute-done.2), kind=kLoop, calls=%fused_computation.7 | loop fusion | flops 23666688 | bytes 7876608 | tf_op jit(solution)/shard_map/concatenate | solution.py:567
  31.8 1.5 fusion.91
  33.3 2.6 %fusion.133 = bf16[9,512,512]{2,1,0:T(8,128)(2,1)S(1)} fusion(bf16[9,512,512]{2,1,0:T(8,128)(2,1)S(1)} %fusion.91, bf16[4,640,512]{1,2,0:T(8,128)(2,1)S(1)} %bitcast.199, bf16[1,640,512]{1,2,0:T(8,128)(2,1)} %collective-permute-done.2, bf16[1,4,640,512]{3,2,1,0:T(8,128)(2,1)S(1)} %copy-done.3), kind=kOutput, calls=%fused_computation.67 | convolution fusion | flops 1348993024 | bytes 6422528 | tf_op jit(solution)/shard_map/rvc,rvo->co/dot_general | solution.py:572
  35.9 1.6 fusion.97
  37.6 1.5 fusion.103
  39.3 1.6 fusion.85
  40.9 1.6 fusion.109
  42.5 1.5 fusion.115
  44.0 2.6 %fusion.127 = bf16[9,512,512]{2,1,0:T(8,128)(2,1)S(1)} fusion(bf16[9,512,512]{2,1,0:T(8,128)(2,1)S(1)} %fusion.115, bf16[1,640,512]{1,2,0:T(8,128)(2,1)} %collective-permute-done.3, bf16[4,640,512]{1,2,0:T(8,128)(2,1)S(1)} %bitcast.200, bf16[1,4,640,512]{3,2,1,0:T(8,128)(2,1)S(1)} %copy-done.3), kind=kOutput, calls=%fused_computation.65 | convolution fusion | flops 1348993024 | bytes 6422528 | tf_op jit(solution)/shard_map/rvc,rvo->co/dot_general | solution.py:572
  46.6 1.6 fusion.121.w_ref
  48.3 2.2 copy-done.6
  50.4 29.3 %bev_slots.1 = (bf16[128,64,256]{2,1,0:T(8,128)(2,1)S(1)}, bf16[128,64,256]{2,1,0:T(8,128)(2,1)S(1)}) custom-call(s32[128]{0:T(128)S(1)} %get-tuple-element.16.idx_ref, bf16[4,640,512]{2,1,0:T(8,128)(2,1)S(1)} %bitcast.197, bf16[640,512]{1,0:T(8,128)(2,1)} %bitcast.6.lo_ref, bf16[640,512]{1,0:T(8,128)(2,1)} %bitcast.8.hi_ref, bf16[9,512,512]{2,1,0:T(8,128)(2,1)} %bitcast.208), custom_call_target="tpu_custom_call" | custom-call | flops 12079595520 | bytes 25165824 | tf_op jit(solution)/shard_map/bev_slots/pallas_call | solution.py:98
  79.8 2.0 copy-done.1
  81.8 2.0 copy-done.2
  83.8 124.1 %exchange_all.1 = (f32[512,512]{1,0:T(8,128)}, bf16[9,512,512]{2,1,0:T(8,128)(2,1)}) custom-call(bf16[8,8,128,256]{3,2,1,0:T(8,128)(2,1)} %bitcast.195, bf16[4,8,2,128,256]{4,3,2,1,0:T(8,128)(2,1)} %bitcast.196, bf16[2,8,8,16,128]{4,3,2,1,0:T(8,128)(2,1)} %pad_maximum_fusion.m_ref, bf16[9,512,512]{2,1,0:T(8,128)(2,1)} %copy-done.6), custom_call_target="tpu_custom_call" | custom-call | tf_op jit(solution)/shard_map/exchange_all/pallas_call | solution.py:395
  207.9 1.7 multiply_convert_fusion
  209.6 0.5 fusion.137.p_ref
  210.1 1.3 fusion.136
  211.4 32.1 %small_sum.1 = bf16[512,512]{1,0:T(8,128)(2,1)S(1)} custom-call(bf16[512,512]{1,0:T(8,128)(2,1)S(1)} %fusion.137.p_ref), custom_call_target="tpu_custom_call" | custom-call | tf_op jit(solution)/shard_map/small_sum/pallas_call | solution.py:487
  243.5 2.2 copy.51
  245.7 0.8 copy.52
  (59 shorter events, 2.2 us)
Async XLA Ops:
  0.6 24.1 %copy-start = (bf16[1,512,512]{2,1,0:T(8,128)(2,1)S(1)}, bf16[1,512,512]{2,1,0:T(8,128)(2,1)}, u32[]{:S(2)}) copy-start(bf16[1,512,512]{2,1,0:T(8,128)(2,1)} %param.12) | copy-start | bytes 1572868
  0.6 13.9 %copy-start.3 = (bf16[1,4,640,512]{3,2,1,0:T(8,128)(2,1)S(1)}, bf16[1,4,640,512]{3,2,1,0:T(8,128)(2,1)}, u32[]{:S(2)}) copy-start(bf16[1,4,640,512]{3,2,1,0:T(8,128)(2,1)} %param.9) | copy-start | bytes 7864324
  0.7 20.6 %copy-start.10 = (s32[1,2560]{1,0:T(1,128)S(1)}, s32[1,2560]{1,0:T(1,128)}, u32[]{:S(2)}) copy-start(s32[1,2560]{1,0:T(1,128)} %param.14) | copy-start | bytes 30724
  0.7 21.0 %copy-start.13 = (s32[1,2560]{1,0:T(1,128)S(1)}, s32[1,2560]{1,0:T(1,128)}, u32[]{:S(2)}) copy-start(s32[1,2560]{1,0:T(1,128)} %param.16) | copy-start | bytes 30724
  0.7 21.0 %copy-start.12 = (s32[1,2560]{1,0:T(1,128)S(1)}, s32[1,2560]{1,0:T(1,128)}, u32[]{:S(2)}) copy-start(s32[1,2560]{1,0:T(1,128)} %param.17) | copy-start | bytes 30724
  0.7 21.2 %copy-start.11 = (s32[1,2560]{1,0:T(1,128)S(1)}, s32[1,2560]{1,0:T(1,128)}, u32[]{:S(2)}) copy-start(s32[1,2560]{1,0:T(1,128)} %param.15) | copy-start | bytes 30724
  7.7 19.5 %collective-permute-start.2 = (bf16[1,640,512]{1,2,0:T(8,128)(2,1)}, bf16[1,640,512]{1,2,0:T(8,128)(2,1)}, u32[]{:S(2)}, u32[]{:S(2)}) collective-permute-start(bf16[1,640,512]{1,2,0:T(8,128)(2,1)} %get-tuple-element.21), channel_id=1, source_target_pairs={{0,1},{1,2},{2,3},{3,4},{4,5},{5,6},{6,7},{7,8},{8,9},{9,10},{10,1... | collective-permute-start | bytes 1966088 | tf_op jit(solution)/shard_map/ppermute | solution.py:510
  12.6 14.6 %collective-permute-start.3 = (bf16[1,640,512]{1,2,0:T(8,128)(2,1)}, bf16[1,640,512]{1,2,0:T(8,128)(2,1)}, u32[]{:S(2)}, u32[]{:S(2)}) collective-permute-start(bf16[1,640,512]{1,2,0:T(8,128)(2,1)} %get-tuple-element.22), channel_id=1, source_target_pairs={{1,0},{2,1},{3,2},{4,3},{5,4},{6,5},{7,6},{8,7},{9,8},{10,9},{11,1... | collective-permute-start | bytes 1966088 | tf_op jit(solution)/shard_map/ppermute | solution.py:510
  15.7 32.5 %collective-permute-start = (bf16[1,640,512]{2,1,0:T(8,128)(2,1)}, bf16[1,640,512]{2,1,0:T(8,128)(2,1)}, u32[]{:S(2)}, u32[]{:S(2)}) collective-permute-start(bf16[1,640,512]{2,1,0:T(8,128)(2,1)} %get-tuple-element.24), channel_id=1, source_target_pairs={{0,1},{1,2},{2,3},{3,4},{4,5},{5,6},{6,7},{7,8},{8,9},{9,10},{10,1... | collective-permute-start | bytes 1966088 | tf_op jit(solution)/shard_map/ppermute | solution.py:510
  19.4 28.9 %collective-permute-start.1 = (bf16[1,640,512]{2,1,0:T(8,128)(2,1)}, bf16[1,640,512]{2,1,0:T(8,128)(2,1)}, u32[]{:S(2)}, u32[]{:S(2)}) collective-permute-start(bf16[1,640,512]{2,1,0:T(8,128)(2,1)} %get-tuple-element.23), channel_id=1, source_target_pairs={{1,0},{2,1},{3,2},{4,3},{5,4},{6,5},{7,6},{8,7},{9,8},{10,9},{11,1... | collective-permute-start | bytes 1966088 | tf_op jit(solution)/shard_map/ppermute | solution.py:510
  23.8 3.5 %copy-start.4 = (bf16[1,4,640,512]{2,3,1,0:T(8,128)(2,1)S(1)}, bf16[1,4,640,512]{2,3,1,0:T(8,128)(2,1)}, u32[]{:S(2)}) copy-start(bf16[1,4,640,512]{2,3,1,0:T(8,128)(2,1)} %copy.31) | copy-start | bytes 7864324
  37.6 1.7 copy-start.8
  48.2 2.2 copy-start.6
  79.8 2.0 copy-start.1
  81.8 2.0 copy-start.2
  83.8 124.1 %copy-start.7 = (f32[512,512]{1,0:T(8,128)S(1)}, f32[512,512]{1,0:T(8,128)}, u32[]{:S(2)}) copy-start(f32[512,512]{1,0:T(8,128)} %fusion.139) | copy-start | bytes 3145732
  83.8 126.3 %copy-start.9 = (bf16[512,512]{1,0:T(8,128)(2,1)S(1)}, bf16[512,512]{1,0:T(8,128)(2,1)}, u32[]{:S(2)}) copy-start(bf16[512,512]{1,0:T(8,128)(2,1)} %param.13) | copy-start | bytes 1572868
  207.8 35.6 %copy-start.5 = (bf16[9,512,512]{2,1,0:T(8,128)(2,1)S(1)}, bf16[9,512,512]{2,1,0:T(8,128)(2,1)}, u32[]{:S(2)}) copy-start(bf16[9,512,512]{2,1,0:T(8,128)(2,1)} %get-tuple-element.10) | copy-start | bytes 14155780

commit v3 on v2

v3 whole, which is shorter than its diff:
```python
import functools
import math

import jax
import jax.numpy as jnp
from jax import lax
from jax.experimental import pallas as pl
from jax.experimental.pallas import tpu as pltpu
from jax.sharding import PartitionSpec as P

BLK = 64
IMGW = 64
PIXB = 2 * IMGW
TILES = 64
CAP = 2
MESH = pl.DeviceIdType.MESH
ANY = pl.BlockSpec(memory_space=pl.ANY)
VMEM = pl.BlockSpec(memory_space=pltpu.VMEM)
SMEM = pl.BlockSpec(memory_space=pltpu.SMEM)
HBM = pl.BlockSpec(memory_space=pltpu.HBM)
BF = jnp.bfloat16
F32 = jnp.float32


def coords():
    t = lax.axis_index("tile")
    return t // 16, (t // 8) % 2 * 2 + lax.axis_index("dp"), (t // 2) % 4, t % 2


def device(y, x, z, core):
    return (x % 2, ((y * 2 + x // 2) * 4 + z) * 2 + core)


def along(axis, step):
    y, x, z, core = coords()
    if axis == "y":
        y = (y + step) % 4
    elif axis == "x":
        x = (x + step) % 4
    elif axis == "z":
        z = (z + step) % 4
    else:
        core = 1 - core
    return device(y, x, z, core)


def bev_kernel(idx_ref, g_ref, lo_ref, hi_ref, w_ref, sa_ref, sb_ref, frame, w, acc, bev, sems, out_sem):
    rows, cols = g_ref.shape[0], g_ref.shape[1]
    copies = [
        pltpu.make_async_copy(w_ref, w, sems.at[0]),
        pltpu.make_async_copy(g_ref, frame.at[pl.ds(1, rows)], sems.at[1]),
        pltpu.make_async_copy(lo_ref, frame.at[0], sems.at[2]),
        pltpu.make_async_copy(hi_ref, frame.at[rows + 1], sems.at[3]),
    ]
    for copy in copies:
        copy.start()
    for copy in copies:
        copy.wait()
    half = 256

    def step(s, carry):
        r, n = s // 2, s % 2
        lanes = pl.ds(pl.multiple_of(n * half, half), half)

        def tap(j):
            total = None
            for i in range(3):
                term = lax.dot_general(
                    frame[r + 2 - i],
                    w[i * 3 + j, lanes, :],
                    (((1,), (1,)), ((), ())),
                    preferred_element_type=F32,
                )
                total = term if total is None else total + term
            return total

        acc[pl.ds(8, cols), :] = tap(1)
        acc[pl.ds(7, cols), :] += tap(0)
        acc[pl.ds(9, cols), :] += tap(2)
        bev[n, pl.ds(pl.multiple_of(r * cols, cols), cols), :] = acc[pl.ds(8, cols), :].astype(BF)
        return carry

    lax.fori_loop(0, 2 * rows, step, 0)

    def send(s, carry):
        start = pl.multiple_of(idx_ref[s] * BLK, BLK)
        rows_of = pl.ds(start, BLK)
        pltpu.make_async_copy(bev.at[0, rows_of], sa_ref.at[s], out_sem.at[0]).start()
        pltpu.make_async_copy(bev.at[1, rows_of], sb_ref.at[s], out_sem.at[1]).start()
        return carry

    lax.fori_loop(0, TILES * CAP, send, 0)
    pltpu.make_async_copy(sa_ref, sa_ref, out_sem.at[0]).wait()
    pltpu.make_async_copy(sb_ref, sb_ref, out_sem.at[1]).wait()


def bev_slots(idx, g, lo, hi, w):
    rows, cols, chans = g.shape
    return pl.pallas_call(
        bev_kernel,
        out_shape=[jax.ShapeDtypeStruct((TILES * CAP, BLK, chans // 2), BF)] * 2,
        in_specs=[SMEM, ANY, ANY, ANY, ANY],
        out_specs=[HBM, HBM],
        scratch_shapes=[
            pltpu.VMEM((rows + 2, cols, chans), BF),
            pltpu.VMEM(w.shape, BF),
            pltpu.VMEM((cols + 16, 256), F32),
            pltpu.VMEM((2, rows * cols, chans // 2), BF),
            pltpu.SemaphoreType.DMA((4,)),
            pltpu.SemaphoreType.DMA((2,)),
        ],
        compiler_params=pltpu.CompilerParams(vmem_limit_bytes=40 << 20),
        cost_estimate=pl.CostEstimate(
            flops=2 * 9 * rows * cols * chans * chans, bytes_accessed=24 << 20, transcendentals=0
        ),
        name="bev_slots",
    )(idx, g, lo, hi, w)


NPIX = 4 * PIXB
CELLS = CAP * BLK
GROUP = 8


def silu_slope(value):
    sigma = jax.nn.sigmoid(value)
    return sigma * (1.0 + value * (1.0 - sigma))


def exchange_kernel(
    cell_scale, pixel_scale,
    sa_ref, sb_ref, m_ref, g_ref, a_ref, alo_ref, ahi_ref, img_ref, bw_ref,
    ig_ref, o_ref, bb_ref,
    land, meta, band, dense, land2, sums, land3, w_ref, recv0, acc0, recv1, acc1, recv2,
    shift, feature, slope, img_t, bb, bb0, bb0_acc, bb1, bb1_acc, bb2,
    in_sem, m_send, m_recv, p1_send, p1_recv, own_sem, p2_send, p2_recv, p3_send, p3_recv,
    pair_send, pair_recv, x_send, x_recv, yz_send, yz_recv, ag_send, ag_recv, far_send, far_recv,
    by_send, by_recv, bx_send, bx_recv,
):
    y, x, z, core = coords()
    x_hi = x // 2
    taps, chans = w_ref.shape[0], w_ref.shape[1]
    rows, cols = a_ref.shape[0] // alo_ref.shape[0], alo_ref.shape[0] * 64

    def remote(src, dst, sends, recvs, where):
        return pltpu.make_async_remote_copy(
            src_ref=src, dst_ref=dst, send_sem=sends, recv_sem=recvs,
            device_id=where, device_id_type=MESH,
        )

    plane = [(p, q) for p in range(4) for q in range(4) if p or q]
    corner = [(p, q) for p, q in plane if p and q]

    def at(dy, dz, dc, dx=0):
        return device((y + dy) % 4, (x + dx) % 4, (z + dz) % 4, (core + dc) % 2)

    barrier = pltpu.get_barrier_semaphore()
    greeted = [at(0, 0, 1)] + [at(dy, dz, 0) for dy, dz in plane]
    greeted += [at(dy, dz, 1) for dy, dz in plane if not (dy and dz)]
    greeted += [at(0, 0, 0, d) for d in (1, 2, 3)]
    greeted += [at(p, 0, 0, q) for p, q in corner] + [at(0, p, 0, q) for p, q in corner]
    for where in greeted:
        pl.semaphore_signal(barrier, inc=1, device_id=where, device_id_type=MESH)

    loads = [
        pltpu.make_async_copy(g_ref.at[pl.ds(p * 512, 512)], w_ref.at[p], in_sem.at[p])
        for p in range(5)
    ]
    loads += [
        pltpu.make_async_copy(
            a_ref.at[pl.ds(4 * u, 4)], o_ref.at[u // 2, u % 2], in_sem.at[5 + u]
        )
        for u in range(10)
    ]
    for k, ref in enumerate((alo_ref, ahi_ref)):
        for u in range(3):
            size = 4 if u < 2 else 2
            loads.append(
                pltpu.make_async_copy(
                    ref.at[pl.ds(4 * u, size)],
                    o_ref.at[5 + 2 * k + u // 2, u % 2, pl.ds(0, size)],
                    in_sem.at[15 + 3 * k + u],
                )
            )
    for copy in loads:
        copy.start()
    pl.semaphore_wait(barrier, len(greeted))

    line = (z, y)
    here = [line[h] * 2 + core for h in range(2)]

    def slots_of(h, member):
        return sa_ref.at[:, member] if h == 0 else sb_ref.at[member // 2, :, member % 2]

    def info_of(h, member):
        return m_ref.at[h, :, member]

    steps = [(d, dc) for d in range(4) for dc in range(2) if d or dc]

    def group_copy(h, k, sign, which):
        d, dc = steps[k]
        member = (line[h] + (d if sign > 0 else 4 - d)) % 4 * 2 + (core + dc) % 2
        where = at(0, d, dc) if h == 0 else at(d, 0, dc)
        place = here[h] if sign > 0 else member
        if which == "meta":
            return remote(
                info_of(h, member), meta.at[h, place], m_send.at[h, k], m_recv.at[h, k], where
            )
        return remote(
            slots_of(h, member), land.at[h, place], p1_send.at[h, k], p1_recv.at[h, k], where
        )

    own = []
    for h in range(2):
        own.append(
            pltpu.make_async_copy(info_of(h, here[h]), meta.at[h, here[h]], own_sem.at[h, 0])
        )
        own.append(
            pltpu.make_async_copy(slots_of(h, here[h]), land.at[h, here[h]], own_sem.at[h, 1])
        )
    for copy in own:
        copy.start()
    for which in ("meta", "slots"):
        for k in range(7):
            for h in range(2):
                group_copy(h, k, 1, which).start()

    for copy in loads:
        copy.wait()

    def turn(r, piece, start, column):
        block = o_ref[piece, start // 256, pl.ds(start // 64 % 4, 2)]
        band[r, :, column] = block.reshape(128, chans).T

    def turn_inner(n, carry):
        column = pl.ds(pl.multiple_of(n % 5 * 128, 128), 128)
        turn(n // 5 + 1, n // 4, n % 4 * 128, column)
        return carry

    lax.fori_loop(0, 20, turn_inner, 0)
    for k, r in ((0, 0), (1, rows + 1)):
        for n in range(5):
            turn(r, 5 + 2 * k + n // 4, n % 4 * 128, pl.ds(n * 128, 128))

    def store_moved(j, n, value):
        p = j * 5 + n // 4
        band[
            6 + p // 2,
            pl.ds(pl.multiple_of(n % 4 * 128, 128), 128),
            pl.ds(pl.multiple_of(p % 2 * 512, 512), 512),
        ] = value.astype(BF)

    edge = jnp.zeros((8, chans), F32)
    shift[pl.ds(0, 8), :] = edge
    shift[pl.ds(cols + 8, 8), :] = edge

    def move(r, carry):
        for n in range(5):
            b = r * 5 + n
            block = w_ref[b // 4, pl.ds(pl.multiple_of(b % 4 * 128, 128), 128), :]
            store_moved(1, b, block)
            shift[pl.ds(8 + n * 128, 128), :] = block.astype(F32)
        for n in range(5):
            store_moved(0, r * 5 + n, shift[pl.ds(9 + n * 128, 128), :])
            store_moved(2, r * 5 + n, shift[pl.ds(7 + n * 128, 128), :])
        return carry

    lax.fori_loop(0, rows, move, 0)

    def tap(n, carry):
        i, j = n // 3, n % 3
        left = jnp.concatenate([band[r + i, :, 0:cols] for r in range(rows)], axis=1)
        parts = []
        for k in range(5):
            p = j * 5 + k
            parts.append(
                band[6 + p // 2, :, pl.ds(pl.multiple_of(p % 2 * 512, 512), 512)]
            )
        right = jnp.concatenate(parts, axis=0)
        w_ref[n] = jnp.dot(left, right, preferred_element_type=F32).astype(BF)
        return carry

    lax.fori_loop(0, taps, tap, 0)

    half = chans // 2
    mine = pl.ds(pl.multiple_of(core * half, half), half)
    other = pl.ds(pl.multiple_of((1 - core) * half, half), half)
    pair = remote(w_ref.at[:, other], recv0, pair_send.at[0], pair_recv.at[0], at(0, 0, 1))
    pair.start()

    image = img_ref[...]
    slope[...] = silu_slope(jnp.dot(image, bw_ref[...], preferred_element_type=F32))
    img_t[...] = image.T
    pair.wait()

    def add0(k, carry):
        acc0[k] = (w_ref[k, mine, :].astype(F32) + recv0[k].astype(F32)).astype(BF)
        return carry

    lax.fori_loop(0, taps, add0, 0)

    def rows64(q):
        return pl.ds(pl.multiple_of(q * 64, 64), 64)

    along_x = [
        remote(
            acc0.at[:, rows64((x + d) % 4)], recv1.at[d - 1],
            x_send.at[d - 1], x_recv.at[d - 1], at(0, 0, 0, d),
        )
        for d in (1, 2, 3)
    ]
    for copy in along_x:
        copy.start()

    for k in range(7):
        for h in range(2):
            group_copy(h, k, 1, "meta").wait_send()
            group_copy(h, k, -1, "meta").wait_recv()
    own[0].wait()
    own[2].wait()

    def make_band(n, carry):
        h, owner, member = n // 64, n // 8 % 8, n % 8
        info = meta[h, member, owner].astype(F32)
        q = lax.broadcasted_iota(jnp.int32, (IMGW, CELLS), 0).astype(F32)
        left, right = q == info[0:1], q == info[0:1] + 1.0
        zero = jnp.zeros((IMGW, CELLS), F32)
        upper = jnp.where(left, info[2:3], jnp.where(right, info[3:4], zero))
        lower = jnp.where(left, info[4:5], jnp.where(right, info[5:6], zero))
        whole = jnp.concatenate([upper, lower], axis=0)
        lanes = pl.ds(pl.multiple_of(member * CELLS, CELLS), CELLS)
        for block in range(4):
            kept = jnp.where(info[1:2] == float(block), whole, 0.0)
            band[h * 8 + owner, pl.ds(block * PIXB, PIXB), lanes] = kept.astype(BF)
        return carry

    lax.fori_loop(0, 128, make_band, 0)
    for k in range(7):
        for h in range(2):
            group_copy(h, k, 1, "slots").wait_send()
            group_copy(h, k, -1, "slots").wait_recv()
    own[1].wait()
    own[3].wait()

    def owner_of(h, x_part, d):
        q = (y + h * (z - y) + d) % 4
        return (1 - h) * (q * 2 + x_part) + h * (x_part * 4 + q)

    def second(h, x_part, d):
        far = (x_part + x_hi) % 2
        return remote(
            dense.at[h, owner_of(h, x_part, d)], land2.at[h, far, d - 1],
            p2_send.at[h, far, d - 1], p2_recv.at[h, far, d - 1],
            at((1 - h) * d, h * d, 0),
        )

    def form(x_part):
        def one(n, carry):
            h, d = n % 2, n // 2 + 1
            owner = owner_of(h, x_part, d)
            cells = land[h, :, owner].reshape(GROUP * CELLS, half)
            dense[h, owner] = jnp.dot(
                band[h * 8 + owner], cells, preferred_element_type=F32
            ).astype(BF)

            @pl.when(d < 4)
            def _():
                second(h, x_part, d).start()

            return carry

        lax.fori_loop(0, 8, one, 0)

    form(1 - x_hi)

    for copy in along_x:
        copy.wait()

    def add1(k, carry):
        total = acc0[k, rows64(x), :].astype(F32)
        for d in range(3):
            total = total + recv1[d, k].astype(F32)
        acc1[k] = total.astype(BF)
        return carry

    lax.fori_loop(0, taps, add1, 0)

    def lanes128(q):
        return pl.ds(pl.multiple_of(q * 128, 128), 128)

    def rows16(q):
        return pl.ds(pl.multiple_of(q * 16, 16), 16)

    to_plane = [
        remote(
            acc1.at[:, rows16((y + dy) % 4), lanes128((z + dz) % 4)], recv2.at[k],
            yz_send.at[k], yz_recv.at[k], at(dy, dz, 0),
        )
        for k, (dy, dz) in enumerate(plane)
    ]
    for copy in to_plane:
        copy.start()
    form(x_hi)

    def settle(far):
        for h in range(2):
            for d in (1, 2, 3):
                second(h, (far + x_hi) % 2, d).wait()

    def gathered(h, x_part, far):
        total = dense[h, owner_of(h, x_part, 0)].astype(F32)
        for d in range(3):
            total = total + land2[h, far, d].astype(F32)
        return total

    settle(1)
    third = []
    for h in range(2):
        sums[h] = gathered(h, 1 - x_hi, 1).astype(BF)
        third.append(
            remote(sums.at[h], land3.at[h], p3_send.at[h], p3_recv.at[h], at(0, 0, 0, 2))
        )
        third[h].start()

    for copy in to_plane:
        copy.wait()

    def add2(k, carry):
        total = acc1[k, rows16(y), lanes128(z)].astype(F32)
        for p in range(15):
            total = total + recv2[p, k].astype(F32)
        o_ref[k, core, x, y, :, lanes128(z)] = (total * cell_scale).astype(BF)
        return carry

    lax.fori_loop(0, taps, add2, 0)

    def spread(s, k, sign):
        p, q = plane[k]
        dy, dx, dz = ((p, 0, q), (0, p, q), (p, q, 0))[s]
        part = o_ref.at[
            pl.ds(3 * s, 3), core, (x + sign * dx + 4) % 4, (y + sign * dy + 4) % 4, :,
            lanes128((z + sign * dz + 4) % 4),
        ]
        return remote(part, part, ag_send.at[s, k], ag_recv.at[s, k], at(dy, dz, 0, dx))

    def strip(s, d, sign):
        t = pl.ds(3 * s, 3)
        if s == 0:
            part, where = o_ref.at[t, core, (x + sign * d + 4) % 4], at(0, 0, 0, d)
        elif s == 1:
            part, where = o_ref.at[t, core, :, (y + sign * d + 4) % 4], at(d, 0, 0)
        else:
            part = o_ref.at[t, core, :, :, :, lanes128((z + sign * d + 4) % 4)]
            where = at(0, d, 0)
        return remote(part, part, far_send.at[s, d - 1], far_recv.at[s, d - 1], where)

    for k in range(15):
        for s in range(3):
            spread(s, k, 0).start()

    settle(0)
    lanes_of = (pl.ds(0, 256), pl.ds(256, 256))
    for h in range(2):
        feature[:, lanes_of[h]] = gathered(h, x_hi, 0)
    for k in range(15):
        for s in range(3):
            spread(s, k, 0).wait_send()
            spread(s, k, -1).wait_recv()
    for d in (1, 2, 3):
        for s in range(3):
            strip(s, d, 0).start()

    for h in range(2):
        third[h].wait()
        feature[:, lanes_of[h]] += land3[h].astype(F32)
    scaled = (feature[...] * slope[...]).astype(BF)
    bb[...] = jnp.dot(img_t[...], scaled, preferred_element_type=F32).astype(BF)
    bb_pair = remote(bb.at[other], bb0, pair_send.at[1], pair_recv.at[1], at(0, 0, 1))
    bb_pair.start()
    ig_ref[...] = lax.dot_general(
        scaled, bw_ref[...], (((1,), (1,)), ((), ())), preferred_element_type=F32
    ).astype(BF)
    bb_pair.wait()
    bb0_acc[...] = (bb[mine, :].astype(F32) + bb0[...].astype(F32)).astype(BF)

    def place(dy, dz):
        return (y + dy + 4) % 4 * 4 + (z + dz + 4) % 4

    bb_plane = [
        remote(
            bb0_acc.at[rows16(place(dy, dz))], bb1.at[k],
            by_send.at[0, k], by_recv.at[0, k], at(dy, dz, 0),
        )
        for k, (dy, dz) in enumerate(plane)
    ]
    for copy in bb_plane:
        copy.start()
    for copy in bb_plane:
        copy.wait()
    total = bb0_acc[rows16(place(0, 0)), :].astype(F32)
    for k in range(15):
        total = total + bb1[k].astype(F32)
    bb1_acc[...] = total.astype(BF)
    bb_line = [
        remote(
            bb1_acc.at[:, lanes128((x + d) % 4)], bb2.at[d - 1],
            bx_send.at[0, d - 1], bx_recv.at[0, d - 1], at(0, 0, 0, d),
        )
        for d in (1, 2, 3)
    ]
    for copy in bb_line:
        copy.start()

    for d in (1, 2, 3):
        for s in range(3):
            strip(s, d, 0).wait_send()
            strip(s, d, -1).wait_recv()

    def back(c):
        return remote(
            o_ref.at[:, c], o_ref.at[:, c], pair_send.at[2], pair_recv.at[2], at(0, 0, 1)
        )

    back(core).start()
    for copy in bb_line:
        copy.wait()
    total = bb1_acc[:, lanes128(x)].astype(F32)
    for d in range(3):
        total = total + bb2[d].astype(F32)

    def bb_rows(dy, dz):
        return pl.ds(pl.multiple_of(core * half + place(dy, dz) * 16, 16), 16)

    bb_ref[bb_rows(0, 0), lanes128(x)] = (total * pixel_scale).astype(BF)

    def bb_strip(d, sign):
        part = bb_ref.at[bb_rows(0, 0), lanes128((x + sign * d + 4) % 4)]
        return remote(part, part, bx_send.at[1, d - 1], bx_recv.at[1, d - 1], at(0, 0, 0, d))

    def bb_spread(k, sign):
        dy, dz = plane[k]
        part = bb_ref.at[bb_rows(sign * dy, sign * dz)]
        return remote(part, part, by_send.at[1, k], by_recv.at[1, k], at(dy, dz, 0))

    def bb_back(which):
        part = bb_ref.at[which]
        return remote(part, part, pair_send.at[3], pair_recv.at[3], at(0, 0, 1))

    for d in (1, 2, 3):
        bb_strip(d, 0).start()
    for d in (1, 2, 3):
        bb_strip(d, 0).wait_send()
        bb_strip(d, -1).wait_recv()
    for k in range(15):
        bb_spread(k, 0).start()
    for k in range(15):
        bb_spread(k, 0).wait_send()
        bb_spread(k, -1).wait_recv()
    bb_back(mine).start()
    back(core).wait_send()
    back(1 - core).wait_recv()
    bb_back(mine).wait_send()
    bb_back(other).wait_recv()


def exchange_all(cell_scale, pixel_scale, slots, meta, g, act, a_lo, a_hi, image, weight):
    chans = image.shape[1]
    half = chans // 2
    wide = chans // 2
    taps = 9
    dma = pltpu.SemaphoreType.DMA
    vmem = pltpu.VMEM
    pixels = image.shape[0]
    return pl.pallas_call(
        functools.partial(exchange_kernel, cell_scale, pixel_scale),
        out_shape=[
            jax.ShapeDtypeStruct((pixels, chans), BF),
            jax.ShapeDtypeStruct((taps, 2, 4, 4, 16, chans), BF),
            jax.ShapeDtypeStruct((chans, chans), BF),
        ],
        in_specs=[HBM] * 7 + [VMEM, VMEM],
        out_specs=[VMEM, VMEM, VMEM],
        scratch_shapes=[
            vmem((2, GROUP, GROUP, CELLS, wide), BF),
            vmem((2, GROUP, GROUP, 16, CELLS), BF),
            vmem((2 * GROUP, NPIX, GROUP * CELLS), BF),
            vmem((2, GROUP, NPIX, wide), BF),
            vmem((2, 2, 3, NPIX, wide), BF),
            vmem((2, NPIX, wide), BF),
            vmem((2, NPIX, wide), BF),
            vmem((taps, chans, chans), BF),
            vmem((taps, half, chans), BF),
            vmem((taps, half, chans), BF),
            vmem((3, taps, 64, chans), BF),
            vmem((taps, 64, chans), BF),
            vmem((15, taps, 16, 128), BF),
            vmem((a_lo.shape[0] * 64 + 16, chans), F32),
            vmem((pixels, chans), F32),
            vmem((pixels, chans), F32),
            vmem((chans, pixels), BF),
            vmem((chans, chans), BF),
            vmem((half, chans), BF),
            vmem((half, chans), BF),
            vmem((15, 16, chans), BF),
            vmem((16, chans), BF),
            vmem((3, 16, 128), BF),
            dma((21,)), dma((2, 7)), dma((2, 7)), dma((2, 7)), dma((2, 7)), dma((2, 2)),
            dma((2, 2, 3)), dma((2, 2, 3)), dma((2,)), dma((2,)),
            dma((4,)), dma((4,)), dma((3,)), dma((3,)), dma((15,)), dma((15,)),
            dma((3, 15)), dma((3, 15)), dma((3, 3)), dma((3, 3)),
            dma((2, 15)), dma((2, 15)), dma((2, 3)), dma((2, 3)),
        ],
        compiler_params=pltpu.CompilerParams(
            collective_id=0, has_side_effects=True, vmem_limit_bytes=63 << 20
        ),
        name="exchange_all",
    )(*slots, meta, g, act, a_lo, a_hi, image, weight)


def edge_rows(block):
    count = lax.axis_size("tile")
    forward = [(i, i + 1) for i in range(count - 1)]
    backward = [(target, source) for source, target in forward]
    return lax.ppermute(block[-1:], "tile", forward), lax.ppermute(block[:1], "tile", backward)


def body(grad_out, bev_act, conv_weight, img_in, backbone_weight, route, offsets, frac_x, frac_y):
    my_tile = lax.axis_index("tile")
    g, act, image = grad_out[0], bev_act[0], img_in[0]
    rows, cols, chans = g.shape
    g_lo, g_hi = edge_rows(g)
    a_lo, a_hi = edge_rows(act)
    blocks = rows * cols // BLK
    per_device = image.shape[0] // PIXB

    owners = (route[0] // per_device).reshape(TILES, blocks)
    local_ids = (route[0] % per_device).reshape(TILES, blocks)
    my_owners = lax.dynamic_index_in_dim(owners, my_tile, 0, keepdims=False)
    same = my_owners[:, None] == my_owners[None, :]
    before = lax.broadcasted_iota(jnp.int32, (blocks, blocks), 1) < lax.broadcasted_iota(
        jnp.int32, (blocks, blocks), 0
    )
    my_slots = my_owners * CAP + jnp.sum((same & before).astype(jnp.int32), axis=1)
    chosen = my_slots[None, :] == lax.broadcasted_iota(jnp.int32, (TILES * CAP, blocks), 0)
    idx = jnp.sum(
        jnp.where(chosen, lax.broadcasted_iota(jnp.int32, chosen.shape, 1), 0), axis=1
    )
    right_w = frac_x[0].astype(F32) / 256.0
    lower_w = frac_y[0].astype(F32) / 256.0
    cells = jnp.stack(
        [
            offsets[0].astype(F32),
            (1.0 - lower_w) * (1.0 - right_w),
            (1.0 - lower_w) * right_w,
            lower_w * (1.0 - right_w),
            lower_w * right_w,
        ]
    )
    cells = cells.astype(BF).reshape(5, blocks, BLK)
    info = jnp.einsum("sk,rkm->srm", chosen.astype(BF), cells, preferred_element_type=F32)
    my_local = lax.dynamic_index_in_dim(local_ids, my_tile, 0, keepdims=False)
    held = jnp.sum(jnp.where(chosen, my_local[None, :] + 1, 0), axis=1) - 1
    held = jnp.broadcast_to(held.astype(F32)[:, None, None], (TILES * CAP, 1, BLK))
    info = jnp.concatenate([info[:, :1], held, info[:, 1:]], axis=1).astype(BF)
    info = info.reshape(TILES, CAP, 6, BLK).transpose(0, 2, 1, 3).reshape(TILES, 6, CELLS)
    info = jnp.pad(info, ((0, 0), (0, 10), (0, 0)))
    by_z = info.reshape(8, 8, 16, CELLS)
    by_y = info.reshape(4, 8, 2, 16, CELLS).transpose(1, 0, 2, 3, 4).reshape(8, 8, 16, CELLS)
    meta = jnp.stack([by_z, by_y])

    weights = conv_weight.transpose(1, 2, 0, 3).reshape(9, chans, chans)
    slot_z, slot_y = bev_slots(idx, g, g_lo[0], g_hi[0], weights)
    slot_z = slot_z.reshape(8, 8, CELLS, chans // 2)
    slot_y = slot_y.reshape(4, 8, 2, CELLS, chans // 2)

    cell_scale = 1.0 / math.sqrt(2 * TILES * rows * cols)
    pixel_scale = 1.0 / math.sqrt(2 * TILES * image.shape[0])
    image_grad, conv_sum, backbone_grad = exchange_all(
        cell_scale,
        pixel_scale,
        (slot_z, slot_y),
        meta,
        g.reshape(rows * cols, chans),
        act.reshape(-1, 4, 16, chans),
        a_lo.reshape(-1, 4, 16, chans),
        a_hi.reshape(-1, 4, 16, chans),
        image,
        backbone_weight,
    )
    conv_grad = conv_sum.reshape(3, 3, chans, chans).transpose(2, 0, 1, 3)
    return (image_grad[None], conv_grad, backbone_grad)


def solution(mesh):
    return jax.shard_map(
        body,
        mesh=mesh,
        in_specs=(
            P("dp", "tile", None, None),
            P("dp", "tile", None, None),
            P(),
            P("dp", "tile", None),
            P(),
            P("dp", None),
            P("dp", "tile"),
            P("dp", "tile"),
            P("dp", "tile"),
        ),
        out_specs=(P("dp", "tile", None), P(), P()),
        check_vma=False,
    )
```

time: 247 us -> 210 us (0.85)
  matrix products: 20.6 us -> 0.24 us
  Pallas kernels: 185 us -> 172 us
  other arithmetic: 7.98 us -> 2.6 us
    dot_general x12 -> x0, matrix products: 20.4 us -> none  [the longest x9 16.1 us: body(): jnp.einsum('rvc,rvo->co', moved, g, preferred_element_type=F32).astype(BF)]
    pallas_call x2 -> x1, Pallas kernels: 156 us -> 143 us  [exchange_all(): pl.pallas_call(functools.partial(exchange_kernel, cell_scale, pixel_scale...]
    concatenate x1 -> x0, other arithmetic: 4.54 us -> none  [body(): jnp.concatenate([a_lo, act, a_hi], axis=0)]
    slice x1 -> x2, local copies, waits for them, and re-layouts: 1.15 us -> 5.04 us  [edge_rows(): block[:1]]
    slice x1 -> x0, local copies, waits for them, and re-layouts: 2.48 us -> none  [edge_rows(): block[-1:]]
    unnamed x36 -> x24, local copies, waits for them, and re-layouts: 14 us -> 12.6 us
  transfers between devices with their start and end apart: 4 -> 4, of which waited for: 0 -> 1; matrix products, arithmetic and copies ran while one was open for 11% -> 4% of each run, Pallas kernels for 0% -> 14%
where the time goes in v3:
time: 210 us; the launch traced here: 209 us
  Pallas kernels  172 us (82%)
  local copies, waits for them, and re-layouts  20.2 us (10%)
  starting transfers between devices  12.4 us (6%)
  other arithmetic  2.6 us (1%)
    pallas_call x1, Pallas kernels, exchange_all(): pl.pallas_call(functools.partial(exchange_kernel, cell_scale, pixel_scale...  143 us
    pallas_call x1, Pallas kernels, bev_slots(): pl.pallas_call(bev_kernel, out_shape=[jax.ShapeDtypeStruct((TILES * CAP,...  28.9 us
    unnamed x24, local copies, waits for them, and re-layouts  12.6 us
    ppermute x2, starting transfers between devices, edge_rows(): lax.ppermute(block[-1:], 'tile', forward)  7.2 us
    ppermute x2, starting transfers between devices, edge_rows(): lax.ppermute(block[:1], 'tile', backward)  5.19 us
    slice x2, local copies, waits for them, and re-layouts, edge_rows(): block[:1]  5.04 us
  transfers between devices with their start and end apart: 4, of which 1 were waited for; matrix products, arithmetic and copies ran while one was open for 4% of the time, Pallas kernels for 14%

profile of v3, /device:TPU:1, one launch (start us, length us, event | category | flops | bytes accessed | tf_op | source)
XLA Modules:
  0.0 209.5 jit_solution(2306933218040278038)
XLA Ops:
  0.7 2.6 %slice_bitcast_fusion = (bf16[1,640,512]{2,1,0:T(8,128)(2,1)}, bf16[1,640,512]{2,1,0:T(8,128)(2,1)}) fusion(bf16[1,4,640,512]{3,2,1,0:T(8,128)(2,1)} %param.10), kind=kLoop, calls=%fused_computation.1 | loop fusion | bytes 2621440 | tf_op jit(solution)/shard_map/slice | solution.py:624
  3.3 3.3 %collective-permute-start.3 = (bf16[1,640,512]{2,1,0:T(8,128)(2,1)}, bf16[1,640,512]{2,1,0:T(8,128)(2,1)}, u32[]{:S(2)}, u32[]{:S(2)}) collective-permute-start(bf16[1,640,512]{2,1,0:T(8,128)(2,1)} %get-tuple-element.23), channel_id=1, source_target_pairs={{1,0},{2,1},{3,2},{4,3},{5,4},{6,5},{7,6},{8,7},{9,8},{10,9},{11,1... | collective-permute-start | bytes 1966088 | tf_op jit(solution)/shard_map/ppermute | solution.py:624
  6.6 3.6 %collective-permute-start.2 = (bf16[1,640,512]{2,1,0:T(8,128)(2,1)}, bf16[1,640,512]{2,1,0:T(8,128)(2,1)}, u32[]{:S(2)}, u32[]{:S(2)}) collective-permute-start(bf16[1,640,512]{2,1,0:T(8,128)(2,1)} %get-tuple-element.24), channel_id=1, source_target_pairs={{0,1},{1,2},{2,3},{3,4},{4,5},{5,6},{6,7},{7,8},{8,9},{9,10},{10,1... | collective-permute-start | bytes 1966088 | tf_op jit(solution)/shard_map/ppermute | solution.py:624
  10.1 2.5 %slice_bitcast_fusion.2 = (bf16[1,640,512]{2,1,0:T(8,128)(2,1)}, bf16[1,640,512]{2,1,0:T(8,128)(2,1)}) fusion(bf16[1,4,640,512]{3,2,1,0:T(8,128)(2,1)} %param.9), kind=kLoop, calls=%fused_computation.3 | loop fusion | bytes 2621440 | tf_op jit(solution)/shard_map/slice | solution.py:624
  12.6 1.9 collective-permute-start.1
  14.5 3.6 %collective-permute-start = (bf16[1,640,512]{2,1,0:T(8,128)(2,1)}, bf16[1,640,512]{2,1,0:T(8,128)(2,1)}, u32[]{:S(2)}, u32[]{:S(2)}) collective-permute-start(bf16[1,640,512]{2,1,0:T(8,128)(2,1)} %get-tuple-element.26), channel_id=1, source_target_pairs={{0,1},{1,2},{2,3},{3,4},{4,5},{5,6},{6,7},{7,8},{8,9},{9,10},{10,1... | collective-permute-start | bytes 1966088 | tf_op jit(solution)/shard_map/ppermute | solution.py:624
  18.2 0.1 stack.21
  18.3 0.1 squeeze.23
  18.4 0.1 convert_reduce_fusion.1
  18.6 0.1 stack.25
  18.6 0.1 stack.24
  18.7 0.1 stack.23
  18.8 0.1 stack.22
  19.0 0.2 convert_reduce_fusion
  19.2 0.2 convolution_convert_fusion
  19.5 0.1 select_reduce_fusion
  19.6 0.1 reshape.78
  19.7 0.1 copy.18
  19.8 0.8 copy.19
  20.6 0.1 broadcast_in_dim.32
  20.8 1.2 maximum_bitcast_fusion
  22.0 0.8 reshape.73
  22.8 1.0 copy.23
  23.8 0.8 pad_maximum_fusion.m_ref
  24.7 1.3 collective-permute-done
  26.0 28.9 %bev_slots.1 = (bf16[128,64,256]{2,1,0:T(8,128)(2,1)S(1)}, bf16[128,64,256]{2,1,0:T(8,128)(2,1)S(1)}) custom-call(s32[128]{0:T(128)S(1)} %get-tuple-element.18.idx_ref, bf16[4,640,512]{2,1,0:T(8,128)(2,1)S(1)} %bitcast.51, bf16[640,512]{1,0:T(8,128)(2,1)} %bitcast.6.lo_ref, bf16[640,512]{1,0:T(8,128)(2,1)S(1)} %bitcast.54, bf16[9,512,512]{2,1,0:T(8,128)(2,1)} %bitcast.65), custom_call_target="tpu_custom_call" | custom-call | flops 12079595520 | bytes 25165824 | tf_op jit(solution)/shard_map/bev_slots/pallas_call | solution.py:99
  54.9 2.0 copy-done.1
  56.9 2.0 copy-done.2
  58.9 143.0 %exchange_all.1 = (bf16[512,512]{1,0:T(8,128)(2,1)}, bf16[9,2,4,4,16,512]{5,4,3,2,1,0:T(8,128)(2,1)}, bf16[512,512]{1,0:T(8,128)(2,1)}) custom-call(bf16[8,8,128,256]{3,2,1,0:T(8,128)(2,1)} %bitcast.52, bf16[4,8,2,128,256]{4,3,2,1,0:T(8,128)(2,1)} %bitcast.53, bf16[2,8,8,16,128]{4,3,2,1,0:T(8,128)(2,1)} %pad_maximum_fusion.m_ref, ...), custom_call_target="tpu_custom_call" | custom-call | tf_op jit(solution)/shard_map/exchange_all/pallas_call | solution.py:574
  201.9 1.9 copy.31
  203.8 4.9 %copy.32 = bf16[512,3,3,512]{3,0,2,1:T(8,128)(2,1)} copy(bf16[512,3,3,512]{3,0,2,1:T(8,128)(2,1)} %bitcast.56) | data formatting | bytes 9437184
  208.7 0.8 copy.33
  (32 shorter events, 0.3 us)
Async XLA Ops:
  0.6 25.3 %copy-start = (bf16[1,4,640,512]{3,2,1,0:T(8,128)(2,1)S(1)}, bf16[1,4,640,512]{3,2,1,0:T(8,128)(2,1)}, u32[]{:S(2)}) copy-start(bf16[1,4,640,512]{3,2,1,0:T(8,128)(2,1)} %param.9) | copy-start | bytes 7864324
  0.6 17.5 %copy-start.5 = (s32[1,2560]{1,0:T(1,128)S(1)}, s32[1,2560]{1,0:T(1,128)}, u32[]{:S(2)}) copy-start(s32[1,2560]{1,0:T(1,128)} %param.15) | copy-start | bytes 30724
  0.7 17.6 %copy-start.4 = (s32[1,2560]{1,0:T(1,128)S(1)}, s32[1,2560]{1,0:T(1,128)}, u32[]{:S(2)}) copy-start(s32[1,2560]{1,0:T(1,128)} %param.14) | copy-start | bytes 30724
  0.7 17.7 %copy-start.6 = (s32[1,2560]{1,0:T(1,128)S(1)}, s32[1,2560]{1,0:T(1,128)}, u32[]{:S(2)}) copy-start(s32[1,2560]{1,0:T(1,128)} %param.17) | copy-start | bytes 30724
  0.7 17.7 %copy-start.7 = (s32[1,2560]{1,0:T(1,128)S(1)}, s32[1,2560]{1,0:T(1,128)}, u32[]{:S(2)}) copy-start(s32[1,2560]{1,0:T(1,128)} %param.16) | copy-start | bytes 30724
  3.3 55.7 %collective-permute-start.3 = (bf16[1,640,512]{2,1,0:T(8,128)(2,1)}, bf16[1,640,512]{2,1,0:T(8,128)(2,1)}, u32[]{:S(2)}, u32[]{:S(2)}) collective-permute-start(bf16[1,640,512]{2,1,0:T(8,128)(2,1)} %get-tuple-element.23), channel_id=1, source_target_pairs={{1,0},{2,1},{3,2},{4,3},{5,4},{6,5},{7,6},{8,7},{9,8},{10,9},{11,1... | collective-permute-start | bytes 1966088 | tf_op jit(solution)/shard_map/ppermute | solution.py:624
  6.6 52.4 %collective-permute-start.2 = (bf16[1,640,512]{2,1,0:T(8,128)(2,1)}, bf16[1,640,512]{2,1,0:T(8,128)(2,1)}, u32[]{:S(2)}, u32[]{:S(2)}) collective-permute-start(bf16[1,640,512]{2,1,0:T(8,128)(2,1)} %get-tuple-element.24), channel_id=1, source_target_pairs={{0,1},{1,2},{2,3},{3,4},{4,5},{5,6},{6,7},{7,8},{8,9},{9,10},{10,1... | collective-permute-start | bytes 1966088 | tf_op jit(solution)/shard_map/ppermute | solution.py:624
  12.6 12.1 %collective-permute-start.1 = (bf16[1,640,512]{2,1,0:T(8,128)(2,1)}, bf16[1,640,512]{2,1,0:T(8,128)(2,1)S(1)}, u32[]{:S(2)}, u32[]{:S(2)}) collective-permute-start(bf16[1,640,512]{2,1,0:T(8,128)(2,1)} %get-tuple-element.25), channel_id=1, source_target_pairs={{1,0},{2,1},{3,2},{4,3},{5,4},{6,5},{7,6},{8,7},{9,8},{10,9},{11,1... | collective-permute-start | bytes 1966088 | tf_op jit(solution)/shard_map/ppermute | solution.py:624
  14.5 11.5 %collective-permute-start = (bf16[1,640,512]{2,1,0:T(8,128)(2,1)}, bf16[1,640,512]{2,1,0:T(8,128)(2,1)}, u32[]{:S(2)}, u32[]{:S(2)}) collective-permute-start(bf16[1,640,512]{2,1,0:T(8,128)(2,1)} %get-tuple-element.26), channel_id=1, source_target_pairs={{0,1},{1,2},{2,3},{3,4},{4,5},{5,6},{6,7},{7,8},{8,9},{9,10},{10,1... | collective-permute-start | bytes 1966088 | tf_op jit(solution)/shard_map/ppermute | solution.py:624
  54.9 2.0 copy-start.1
  56.9 2.0 copy-start.2
  203.8 4.9 %copy-start.3 = (bf16[512,512]{1,0:T(8,128)(2,1)S(1)}, bf16[512,512]{1,0:T(8,128)(2,1)}, u32[]{:S(2)}) copy-start(bf16[512,512]{1,0:T(8,128)(2,1)} %get-tuple-element.34) | copy-start | bytes 1572868

commit v4 on v3

v4 whole, which is shorter than its diff:
```python
import functools
import math

import jax
import jax.numpy as jnp
from jax import lax
from jax.experimental import pallas as pl
from jax.experimental.pallas import tpu as pltpu
from jax.sharding import PartitionSpec as P

BLK = 64
IMGW = 64
PIXB = 2 * IMGW
TILES = 64
CAP = 2
MESH = pl.DeviceIdType.MESH
ANY = pl.BlockSpec(memory_space=pl.ANY)
VMEM = pl.BlockSpec(memory_space=pltpu.VMEM)
SMEM = pl.BlockSpec(memory_space=pltpu.SMEM)
HBM = pl.BlockSpec(memory_space=pltpu.HBM)
BF = jnp.bfloat16
F32 = jnp.float32


def coords():
    t = lax.axis_index("tile")
    return t // 16, (t // 8) % 2 * 2 + lax.axis_index("dp"), (t // 2) % 4, t % 2


def device(y, x, z, core):
    return (x % 2, ((y * 2 + x // 2) * 4 + z) * 2 + core)


def along(axis, step):
    y, x, z, core = coords()
    if axis == "y":
        y = (y + step) % 4
    elif axis == "x":
        x = (x + step) % 4
    elif axis == "z":
        z = (z + step) % 4
    else:
        core = 1 - core
    return device(y, x, z, core)


NPIX = 4 * PIXB
CELLS = CAP * BLK
GROUP = 8


def silu_slope(value):
    sigma = jax.nn.sigmoid(value)
    return sigma * (1.0 + value * (1.0 - sigma))


def exchange_kernel(
    cell_scale, pixel_scale,
    idx_ref, m_ref, g_ref, a_ref, cw_ref, img_ref, bw_ref,
    ig_ref, o_ref, bb_ref,
    land, meta, band, dense, slots1, land2, sums, land3, w_ref, recv0, recv1, acc1, recv2,
    edges, shift, slope, img_t, bb0, bb1, bb1_acc, bb2,
    in_sem, e_send, e_recv, m_send, m_recv, p1_send, p1_recv, own_sem, p2_send, p2_recv, p3_send, p3_recv,
    pair_send, pair_recv, x_send, x_recv, yz_send, yz_recv, ag_send, ag_recv, far_send, far_recv,
    by_send, by_recv, bx_send, bx_recv,
):
    y, x, z, core = coords()
    x_hi = x // 2
    taps, chans = w_ref.shape[0], w_ref.shape[3]
    cols = edges.shape[1]
    rows = g_ref.shape[0] // cols
    half = chans // 2
    dp, tile = lax.axis_index("dp"), lax.axis_index("tile")

    def remote(src, dst, sends, recvs, where):
        return pltpu.make_async_remote_copy(
            src_ref=src, dst_ref=dst, send_sem=sends, recv_sem=recvs,
            device_id=where, device_id_type=MESH,
        )

    plane = [(p, q) for p in range(4) for q in range(4) if p or q]
    corner = [(p, q) for p, q in plane if p and q]

    def at(dy, dz, dc, dx=0):
        return device((y + dy) % 4, (x + dx) % 4, (z + dz) % 4, (core + dc) % 2)

    barrier = pltpu.get_barrier_semaphore()
    greeted = [at(0, 0, 1)] + [at(dy, dz, 0) for dy, dz in plane]
    greeted += [at(dy, dz, 1) for dy, dz in plane if not (dy and dz)]
    greeted += [at(0, 0, 0, d) for d in (1, 2, 3)]
    greeted += [at(p, 0, 0, q) for p, q in corner] + [at(0, p, 0, q) for p, q in corner]
    below, above = (dp, (tile + TILES - 1) % TILES), (dp, (tile + 1) % TILES)
    has_below, has_above = tile > 0, tile < TILES - 1
    greeted += [below, above]
    for where in greeted:
        pl.semaphore_signal(barrier, inc=1, device_id=where, device_id_type=MESH)

    def unit(n):
        return n // 2, pl.ds(pl.multiple_of(n % 2 * 512, 512), 512)

    def moved(j, r, n):
        b = j * 5 * (rows + 2) + r * 5 + n
        slot, lanes = unit(b // 4)
        return slot, pl.ds(pl.multiple_of(b % 4 * 128, 128), 128), lanes

    first_weight = 23

    loads = []
    for k in range(taps):
        slot, lanes = unit(first_weight + k)
        loads.append(pltpu.make_async_copy(cw_ref.at[k], band.at[slot, :, lanes], in_sem.at[k]))
    loads += [
        pltpu.make_async_copy(
            a_ref.at[pl.ds(4 * u, 4)], o_ref.at[u // 2, u % 2], in_sem.at[taps + u]
        )
        for u in range(10)
    ]

    def load_gradient(b, carry):
        pltpu.make_async_copy(
            g_ref.at[pl.ds(pl.multiple_of(b * 128, 128), 128)],
            band.at[moved(1, 1 + b // 5, b % 5)], in_sem.at[19],
        ).start()
        return carry

    lax.fori_loop(0, 5 * rows, load_gradient, 0)
    for copy in loads:
        copy.start()

    pl.semaphore_wait(barrier, len(greeted))

    def edge_copies(up, where):
        side = 0 if up else 1
        row = pl.ds((rows - 1) * cols if up else 0, cols)
        copies = [
            remote(g_ref.at[row], edges.at[side], e_send.at[side, 0], e_recv.at[side, 0], where)
        ]
        for u in range(3):
            size = 4 if u < 2 else 2
            copies.append(
                remote(
                    a_ref.at[pl.ds((10 * (rows - 1) if up else 0) + 4 * u, size)],
                    o_ref.at[5 + 2 * side + u // 2, u % 2, pl.ds(0, size)],
                    e_send.at[side, 1 + u], e_recv.at[side, 1 + u], where,
                )
            )
        return copies

    @pl.when(has_above)
    def _():
        for copy in edge_copies(True, above):
            copy.start()

    @pl.when(has_below)
    def _():
        for copy in edge_copies(False, below):
            copy.start()

    edge = jnp.zeros((8, half), F32)
    shift[pl.ds(0, 8), :] = edge
    shift[pl.ds(cols + 8, 8), :] = edge

    def move(r, carry):
        for part in (slice(0, half), slice(half, chans)):

            def block(j, n):
                slot, places, lanes = moved(j, r, n)
                start = pl.multiple_of(lanes.start + part.start, half)
                return slot, places, pl.ds(start, half)

            for n in range(5):
                shift[pl.ds(8 + n * 128, 128), :] = band[block(1, n)].astype(F32)
            for n in range(5):
                band[block(0, n)] = shift[pl.ds(9 + n * 128, 128), :].astype(BF)
                band[block(2, n)] = shift[pl.ds(7 + n * 128, 128), :].astype(BF)
        return carry

    pltpu.make_async_copy(g_ref, g_ref, in_sem.at[19]).wait()
    lax.fori_loop(1, rows + 1, move, 0)

    def arrive(side, up, present):
        @pl.when(present)
        def _():
            for copy in edge_copies(up, below if up else above):
                copy.wait_recv()

        @pl.when(jnp.logical_not(present))
        def _():
            edges[side] = jnp.zeros((cols, chans), BF)
            nothing = jnp.zeros((4, 16, chans), BF)
            for u in range(10):
                o_ref[5 + 2 * side + u // 8, u // 4 % 2, u % 4] = nothing

        r = 0 if side == 0 else rows + 1
        for n in range(5):
            band[moved(1, r, n)] = edges[side, pl.ds(n * 128, 128), :]
        move(r, 0)

    arrive(0, True, has_below)
    arrive(1, False, has_above)
    for copy in loads:
        copy.wait()

    def ground(s, carry):
        r, n = s // 2, s % 2
        out = None
        for i in range(3):
            left, right = [], []
            for j in range(3):
                left.append(
                    jnp.concatenate([band[moved(j, r + 2 - i, m)] for m in range(5)], axis=0)
                )
                slot, lanes = unit(first_weight + 3 * i + j)
                right.append(band[slot, pl.ds(pl.multiple_of(n * half, half), half), lanes])
            term = lax.dot_general(
                jnp.concatenate(left, axis=1), jnp.concatenate(right, axis=1),
                (((1,), (1,)), ((), ())), preferred_element_type=F32,
            )
            out = term if out is None else out + term
        out = out.astype(BF)
        lanes = pl.ds(pl.multiple_of(n * half, half), half)
        for m in range(10):
            k = r * 10 + m
            w_ref[k // 8, k % 8, :, lanes] = out[m * BLK : (m + 1) * BLK]
        return carry

    lax.fori_loop(0, 2 * rows, ground, 0)

    def fill(s, carry):
        block = w_ref[idx_ref[0, s], idx_ref[1, s]]
        place = pl.ds(pl.multiple_of(s % CAP * BLK, BLK), BLK)
        o = s // CAP
        dense[o // 8, o % 8, place, :] = block[:, :half]
        slots1[o // 16, o // 2 % 8, o % 2, place, :] = block[:, half:]
        return carry

    lax.fori_loop(0, TILES * CAP, fill, 0)

    line = (z, y)
    here = [line[h] * 2 + core for h in range(2)]

    def slots_of(h, member):
        if h == 0:
            return dense.at[:, member]
        return slots1.at[member // 2, :, member % 2]

    def info_of(h, member):
        return m_ref.at[h, :, member]

    steps = [(d, dc) for d in range(4) for dc in range(2) if d or dc]

    def group_copy(h, k, sign, which):
        d, dc = steps[k]
        member = (line[h] + (d if sign > 0 else 4 - d)) % 4 * 2 + (core + dc) % 2
        where = at(0, d, dc) if h == 0 else at(d, 0, dc)
        place = here[h] if sign > 0 else member
        if which == "meta":
            return remote(
                info_of(h, member), meta.at[h, place], m_send.at[h, k], m_recv.at[h, k], where
            )
        return remote(
            slots_of(h, member), land.at[h, place], p1_send.at[h, k], p1_recv.at[h, k], where
        )

    own = []
    for h in range(2):
        own.append(
            pltpu.make_async_copy(info_of(h, here[h]), meta.at[h, here[h]], own_sem.at[h, 0])
        )
        own.append(
            pltpu.make_async_copy(slots_of(h, here[h]), land.at[h, here[h]], own_sem.at[h, 1])
        )
    for copy in own:
        copy.start()
    for which in ("meta", "slots"):
        for k in range(7):
            for h in range(2):
                group_copy(h, k, 1, which).start()

    def column(u):
        n = first_weight + u // 4
        return n // 2, pl.ds(pl.multiple_of(n % 2 * 512 + u % 4 * 128, 128), 128)

    def turn(u, piece, start):
        block = o_ref[piece, start // 256, pl.ds(start // 64 % 4, 2)].reshape(128, chans)
        slot, lanes = column(u)
        band[slot, :, lanes] = block.T

    def turn_inner(n, carry):
        turn(5 + n, n // 4, n % 4 * 128)
        return carry

    lax.fori_loop(0, 5 * rows, turn_inner, 0)
    for side in range(2):
        for n in range(5):
            turn(5 * (rows + 1) * side + n, 5 + 2 * side + n // 4, n % 4 * 128)

    def tap(n, carry):
        i, j = n // 3, n % 3
        left = []
        for m in range(5 * rows):
            slot, lanes = column(5 * i + m)
            left.append(band[slot, :, lanes])
        right = [band[moved(j, 1 + m // 5, m % 5)] for m in range(5 * rows)]
        w_ref[n] = jnp.dot(
            jnp.concatenate(left, axis=1), jnp.concatenate(right, axis=0),
            preferred_element_type=F32,
        ).astype(BF).reshape(w_ref.shape[1:])
        return carry

    mine, other = pl.ds(core * 4, 4), pl.ds((1 - core) * 4, 4)

    def pair(k):
        t = pl.ds(3 * k, 3)
        return remote(
            w_ref.at[t, other], recv0.at[t], pair_send.at[4 + k], pair_recv.at[4 + k], at(0, 0, 1)
        )

    def along_x(k, d):
        t = pl.ds(3 * k, 3)
        return remote(
            w_ref.at[t, core * 4 + (x + d) % 4], recv1.at[d - 1, t],
            x_send.at[k, d - 1], x_recv.at[k, d - 1], at(0, 0, 0, d),
        )

    def add0(k, carry):
        w_ref[k, mine] = (w_ref[k, mine].astype(F32) + recv0[k].astype(F32)).astype(BF)
        return carry

    def pass_on(k):
        pair(k).wait()
        lax.fori_loop(3 * k, 3 * k + 3, add0, 0)
        for d in (1, 2, 3):
            along_x(k, d).start()

    for k in range(3):
        lax.fori_loop(3 * k, 3 * k + 3, tap, 0)
        pair(k).start()
        if k > 0:
            pass_on(k - 1)

    image = img_ref[...]
    slope[...] = silu_slope(jnp.dot(image, bw_ref[...], preferred_element_type=F32))
    img_t[...] = image.T
    pass_on(2)

    for k in range(7):
        for h in range(2):
            group_copy(h, k, 1, "meta").wait_send()
            group_copy(h, k, -1, "meta").wait_recv()
    own[0].wait()
    own[2].wait()

    def make_band(n, carry):
        h, owner, member = n // 64, n // 8 % 8, n % 8
        info = meta[h, member, owner].astype(F32)
        q = lax.broadcasted_iota(jnp.int32, (IMGW, CELLS), 0).astype(F32)
        left, right = q == info[0:1], q == info[0:1] + 1.0
        zero = jnp.zeros((IMGW, CELLS), F32)
        upper = jnp.where(left, info[2:3], jnp.where(right, info[3:4], zero))
        lower = jnp.where(left, info[4:5], jnp.where(right, info[5:6], zero))
        whole = jnp.concatenate([upper, lower], axis=0)
        lanes = pl.ds(pl.multiple_of(member * CELLS, CELLS), CELLS)
        for block in range(4):
            kept = jnp.where(info[1:2] == float(block), whole, 0.0)
            band[h * 8 + owner, pl.ds(block * PIXB, PIXB), lanes] = kept.astype(BF)
        return carry

    lax.fori_loop(0, 128, make_band, 0)

    for k in range(3):
        for d in (1, 2, 3):
            along_x(k, d).wait()

    def add1(k, carry):
        total = w_ref[k, core * 4 + x].astype(F32)
        for d in range(3):
            total = total + recv1[d, k].astype(F32)
        acc1[k] = total.astype(BF)
        return carry

    lax.fori_loop(0, taps, add1, 0)

    def lanes128(q):
        return pl.ds(pl.multiple_of(q * 128, 128), 128)

    def rows16(q):
        return pl.ds(pl.multiple_of(q * 16, 16), 16)

    to_plane = [
        remote(
            acc1.at[:, rows16((y + dy) % 4), lanes128((z + dz) % 4)], recv2.at[k],
            yz_send.at[k], yz_recv.at[k], at(dy, dz, 0),
        )
        for k, (dy, dz) in enumerate(plane)
    ]
    for copy in to_plane:
        copy.start()
    for k in range(7):
        for h in range(2):
            group_copy(h, k, 1, "slots").wait_send()
            group_copy(h, k, -1, "slots").wait_recv()
    own[1].wait()
    own[3].wait()

    def owner_of(h, x_part, d):
        q = (y + h * (z - y) + d) % 4
        return (1 - h) * (q * 2 + x_part) + h * (x_part * 4 + q)

    def owner_part(h, x_part, d):
        owner = owner_of(h, x_part, d)
        return h * 4 + owner // 2, pl.ds(owner % 2 * 4, 4)

    def second(h, x_part, d):
        far = (x_part + x_hi) % 2
        return remote(
            dense.at[owner_part(h, x_part, d)], land2.at[h, far, d - 1],
            p2_send.at[h, far, d - 1], p2_recv.at[h, far, d - 1],
            at((1 - h) * d, h * d, 0),
        )

    def form(x_part):
        def one(n, carry):
            h, d = n % 2, n // 2 + 1
            owner = owner_of(h, x_part, d)
            cells = land[h, :, owner].reshape(GROUP * CELLS, half)
            dense[owner_part(h, x_part, d)] = (
                jnp.dot(band[h * 8 + owner], cells, preferred_element_type=F32)
                .astype(BF)
                .reshape(4, PIXB, half)
            )

            @pl.when(d < 4)
            def _():
                second(h, x_part, d).start()

            return carry

        lax.fori_loop(0, 8, one, 0)

    form(1 - x_hi)

    for copy in to_plane:
        copy.wait()

    def add2(k, carry):
        total = acc1[k, rows16(y), lanes128(z)].astype(F32)
        for p in range(15):
            total = total + recv2[p, k].astype(F32)
        o_ref[k, core, x, y, :, lanes128(z)] = (total * cell_scale).astype(BF)
        return carry

    lax.fori_loop(0, taps, add2, 0)

    def spread(s, k, sign):
        p, q = plane[k]
        dy, dx, dz = ((p, 0, q), (0, p, q), (p, q, 0))[s]
        part = o_ref.at[
            pl.ds(3 * s, 3), core, (x + sign * dx + 4) % 4, (y + sign * dy + 4) % 4, :,
            lanes128((z + sign * dz + 4) % 4),
        ]
        return remote(part, part, ag_send.at[s, k], ag_recv.at[s, k], at(dy, dz, 0, dx))

    def strip(s, d, sign):
        t = pl.ds(3 * s, 3)
        if s == 0:
            part, where = o_ref.at[t, core, (x + sign * d + 4) % 4], at(0, 0, 0, d)
        elif s == 1:
            part, where = o_ref.at[t, core, :, (y + sign * d + 4) % 4], at(d, 0, 0)
        else:
            part = o_ref.at[t, core, :, :, :, lanes128((z + sign * d + 4) % 4)]
            where = at(0, d, 0)
        return remote(part, part, far_send.at[s, d - 1], far_recv.at[s, d - 1], where)

    for k in range(15):
        for s in range(3):
            spread(s, k, 0).start()

    form(x_hi)

    def settle(far):
        for h in range(2):
            for d in (1, 2, 3):
                second(h, (far + x_hi) % 2, d).wait()

    def gathered(h, x_part, far):
        total = dense[owner_part(h, x_part, 0)].astype(F32)
        for d in range(3):
            total = total + land2[h, far, d].astype(F32)
        return total.reshape(NPIX, half)

    settle(1)
    third = []
    for h in range(2):
        sums[h] = gathered(h, 1 - x_hi, 1).astype(BF)
        third.append(
            remote(sums.at[h], land3.at[h], p3_send.at[h], p3_recv.at[h], at(0, 0, 0, 2))
        )
        third[h].start()

    for k in range(15):
        for s in range(3):
            spread(s, k, 0).wait_send()
            spread(s, k, -1).wait_recv()
    for d in (1, 2, 3):
        for s in range(3):
            strip(s, d, 0).start()

    settle(0)

    scaled = []
    for h in range(2):
        third[h].wait()
        feature = gathered(h, x_hi, 0) + land3[h].astype(F32)
        scaled.append((feature * slope[:, h * half : (h + 1) * half]).astype(BF))
    scaled = jnp.concatenate(scaled, axis=1)
    part = jnp.dot(img_t[...], scaled, preferred_element_type=F32).astype(BF)
    w_ref[0] = part.reshape(w_ref.shape[1:])
    bb_pair = remote(w_ref.at[0, other], bb0, pair_send.at[1], pair_recv.at[1], at(0, 0, 1))
    bb_pair.start()
    ig_ref[...] = lax.dot_general(
        scaled, bw_ref[...], (((1,), (1,)), ((), ())), preferred_element_type=F32
    ).astype(BF)
    bb_pair.wait()
    w_ref[1, pl.ds(0, 4)] = (w_ref[0, mine].astype(F32) + bb0[...].astype(F32)).astype(BF)

    def place(dy, dz):
        return (y + dy + 4) % 4 * 4 + (z + dz + 4) % 4

    bb_plane = [
        remote(
            w_ref.at[1, place(dy, dz) // 4, rows16(place(dy, dz) % 4)], bb1.at[k],
            by_send.at[0, k], by_recv.at[0, k], at(dy, dz, 0),
        )
        for k, (dy, dz) in enumerate(plane)
    ]
    for copy in bb_plane:
        copy.start()
    for copy in bb_plane:
        copy.wait()
    total = w_ref[1, y, rows16(z), :].astype(F32)
    for k in range(15):
        total = total + bb1[k].astype(F32)
    bb1_acc[...] = total.astype(BF)
    bb_line = [
        remote(
            bb1_acc.at[:, lanes128((x + d) % 4)], bb2.at[d - 1],
            bx_send.at[0, d - 1], bx_recv.at[0, d - 1], at(0, 0, 0, d),
        )
        for d in (1, 2, 3)
    ]
    for copy in bb_line:
        copy.start()

    for d in (1, 2, 3):
        for s in range(3):
            strip(s, d, 0).wait_send()
            strip(s, d, -1).wait_recv()

    def back(c):
        return remote(
            o_ref.at[:, c], o_ref.at[:, c], pair_send.at[2], pair_recv.at[2], at(0, 0, 1)
        )

    back(core).start()
    for copy in bb_line:
        copy.wait()
    total = bb1_acc[:, lanes128(x)].astype(F32)
    for d in range(3):
        total = total + bb2[d].astype(F32)

    def bb_rows(dy, dz):
        return pl.ds(pl.multiple_of(core * half + place(dy, dz) * 16, 16), 16)

    bb_ref[bb_rows(0, 0), lanes128(x)] = (total * pixel_scale).astype(BF)

    def bb_strip(d, sign):
        part = bb_ref.at[bb_rows(0, 0), lanes128((x + sign * d + 4) % 4)]
        return remote(part, part, bx_send.at[1, d - 1], bx_recv.at[1, d - 1], at(0, 0, 0, d))

    def bb_spread(k, sign):
        dy, dz = plane[k]
        part = bb_ref.at[bb_rows(sign * dy, sign * dz)]
        return remote(part, part, by_send.at[1, k], by_recv.at[1, k], at(dy, dz, 0))

    def bb_half(c):
        return pl.ds(pl.multiple_of(c * half, half), half)

    def bb_back(which):
        part = bb_ref.at[which]
        return remote(part, part, pair_send.at[3], pair_recv.at[3], at(0, 0, 1))

    for d in (1, 2, 3):
        bb_strip(d, 0).start()
    for d in (1, 2, 3):
        bb_strip(d, 0).wait_send()
        bb_strip(d, -1).wait_recv()
    for k in range(15):
        bb_spread(k, 0).start()
    for k in range(15):
        bb_spread(k, 0).wait_send()
        bb_spread(k, -1).wait_recv()
    bb_back(bb_half(core)).start()
    back(core).wait_send()
    back(1 - core).wait_recv()
    bb_back(bb_half(core)).wait_send()
    bb_back(bb_half(1 - core)).wait_recv()

    @pl.when(has_above)
    def _():
        for copy in edge_copies(True, above):
            copy.wait_send()

    @pl.when(has_below)
    def _():
        for copy in edge_copies(False, below):
            copy.wait_send()


def exchange_all(cell_scale, pixel_scale, idx, meta, g, act, kernel, image, weight):
    chans = image.shape[1]
    half = chans // 2
    taps = kernel.shape[0]
    cols = 640
    dma = pltpu.SemaphoreType.DMA
    vmem = pltpu.VMEM
    pixels = image.shape[0]
    return pl.pallas_call(
        functools.partial(exchange_kernel, cell_scale, pixel_scale),
        out_shape=[
            jax.ShapeDtypeStruct((pixels, chans), BF),
            jax.ShapeDtypeStruct((taps, 2, 4, 4, 16, chans), BF),
            jax.ShapeDtypeStruct((chans, chans), BF),
        ],
        in_specs=[SMEM] + [HBM] * 4 + [VMEM, VMEM],
        out_specs=[VMEM, VMEM, VMEM],
        scratch_shapes=[
            vmem((2, GROUP, GROUP, CELLS, half), BF),
            vmem((2, GROUP, GROUP, 16, CELLS), BF),
            vmem((2 * GROUP, NPIX, GROUP * CELLS), BF),
            vmem((8, 8, CELLS, half), BF),
            vmem((4, 8, 2, CELLS, half), BF),
            vmem((2, 2, 3, 4, PIXB, half), BF),
            vmem((2, NPIX, half), BF),
            vmem((2, NPIX, half), BF),
            vmem((taps, 8, BLK, chans), BF),
            vmem((taps, 4, BLK, chans), BF),
            vmem((3, taps, 64, chans), BF),
            vmem((taps, 64, chans), BF),
            vmem((15, taps, 16, 128), BF),
            vmem((2, cols, chans), BF),
            vmem((cols + 16, half), F32),
            vmem((pixels, chans), F32),
            vmem((chans, pixels), BF),
            vmem((4, BLK, chans), BF),
            vmem((15, 16, chans), BF),
            vmem((16, chans), BF),
            vmem((3, 16, 128), BF),
            dma((20,)), dma((2, 4)), dma((2, 4)),
            dma((2, 7)), dma((2, 7)), dma((2, 7)), dma((2, 7)), dma((2, 2)),
            dma((2, 2, 3)), dma((2, 2, 3)), dma((2,)), dma((2,)),
            dma((7,)), dma((7,)), dma((3, 3)), dma((3, 3)), dma((15,)), dma((15,)),
            dma((3, 15)), dma((3, 15)), dma((3, 3)), dma((3, 3)),
            dma((2, 15)), dma((2, 15)), dma((2, 3)), dma((2, 3)),
        ],
        compiler_params=pltpu.CompilerParams(
            collective_id=0, has_side_effects=True, vmem_limit_bytes=67043328
        ),
        name="exchange_all",
    )(idx, meta, g, act, kernel, image, weight)


def body(grad_out, bev_act, conv_weight, img_in, backbone_weight, route, offsets, frac_x, frac_y):
    my_tile = lax.axis_index("tile")
    g, act, image = grad_out[0], bev_act[0], img_in[0]
    rows, cols, chans = g.shape
    blocks = rows * cols // BLK
    per_device = image.shape[0] // PIXB

    owners = (route[0] // per_device).reshape(TILES, blocks)
    local_ids = (route[0] % per_device).reshape(TILES, blocks)
    my_owners = lax.dynamic_index_in_dim(owners, my_tile, 0, keepdims=False)
    same = my_owners[:, None] == my_owners[None, :]
    before = lax.broadcasted_iota(jnp.int32, (blocks, blocks), 1) < lax.broadcasted_iota(
        jnp.int32, (blocks, blocks), 0
    )
    my_slots = my_owners * CAP + jnp.sum((same & before).astype(jnp.int32), axis=1)
    chosen = my_slots[None, :] == lax.broadcasted_iota(jnp.int32, (TILES * CAP, blocks), 0)
    idx = jnp.sum(
        jnp.where(chosen, lax.broadcasted_iota(jnp.int32, chosen.shape, 1), 0), axis=1
    )
    right_w = frac_x[0].astype(F32) / 256.0
    lower_w = frac_y[0].astype(F32) / 256.0
    cells = jnp.stack(
        [
            offsets[0].astype(F32),
            (1.0 - lower_w) * (1.0 - right_w),
            (1.0 - lower_w) * right_w,
            lower_w * (1.0 - right_w),
            lower_w * right_w,
        ]
    )
    cells = cells.astype(BF).reshape(5, blocks, BLK)
    info = jnp.einsum("sk,rkm->srm", chosen.astype(BF), cells, preferred_element_type=F32)
    my_local = lax.dynamic_index_in_dim(local_ids, my_tile, 0, keepdims=False)
    held = jnp.sum(jnp.where(chosen, my_local[None, :] + 1, 0), axis=1) - 1
    held = jnp.broadcast_to(held.astype(F32)[:, None, None], (TILES * CAP, 1, BLK))
    info = jnp.concatenate([info[:, :1], held, info[:, 1:]], axis=1).astype(BF)
    info = info.reshape(TILES, CAP, 6, BLK).transpose(0, 2, 1, 3).reshape(TILES, 6, CELLS)
    info = jnp.pad(info, ((0, 0), (0, 10), (0, 0)))
    by_z = info.reshape(8, 8, 16, CELLS)
    by_y = info.reshape(4, 8, 2, 16, CELLS).transpose(1, 0, 2, 3, 4).reshape(8, 8, 16, CELLS)
    meta = jnp.stack([by_z, by_y])

    weights = conv_weight.transpose(1, 2, 0, 3).reshape(9, chans, chans)
    cell_scale = 1.0 / math.sqrt(2 * TILES * rows * cols)
    pixel_scale = 1.0 / math.sqrt(2 * TILES * image.shape[0])
    image_grad, conv_sum, backbone_grad = exchange_all(
        cell_scale,
        pixel_scale,
        jnp.stack([idx // 8, idx % 8]),
        meta,
        g.reshape(rows * cols, chans),
        act.reshape(-1, 4, 16, chans),
        weights,
        image,
        backbone_weight,
    )
    conv_grad = conv_sum.reshape(3, 3, chans, chans).transpose(2, 0, 1, 3)
    return (image_grad[None], conv_grad, backbone_grad)


def solution(mesh):
    return jax.shard_map(
        body,
        mesh=mesh,
        in_specs=(
            P("dp", "tile", None, None),
            P("dp", "tile", None, None),
            P(),
            P("dp", "tile", None),
            P(),
            P("dp", None),
            P("dp", "tile"),
            P("dp", "tile"),
            P("dp", "tile"),
        ),
        out_specs=(P("dp", "tile", None), P(), P()),
        check_vma=False,
    )
```

time: 210 us -> 179 us (0.85)
  starting transfers between devices: 12.4 us -> 0 us
  local copies, waits for them, and re-layouts: 20.2 us -> 8.9 us
  Pallas kernels: 172 us -> 164 us
    pallas_call x1 -> x0, Pallas kernels: 28.9 us -> none  [bev_slots(): pl.pallas_call(bev_kernel, out_shape=[jax.ShapeDtypeStruct((TILES * CAP,...]
    pallas_call x1, Pallas kernels: 143 us -> 164 us  [exchange_all(): pl.pallas_call(functools.partial(exchange_kernel, cell_scale, pixel_scale...]
    ppermute x4 -> x0, starting transfers between devices: 12.4 us -> none  [the longest x2 7.2 us: edge_rows(): lax.ppermute(block[-1:], 'tile', forward)]
    slice x2 -> x0, local copies, waits for them, and re-layouts: 5.04 us -> none  [edge_rows(): block[:1]]
    unnamed x24 -> x10, local copies, waits for them, and re-layouts: 12.6 us -> 7.65 us
  transfers between devices with their start and end apart: 4 -> 0, of which waited for: 1 -> 0; matrix products, arithmetic and copies ran while one was open for 4% -> 0% of each run, Pallas kernels for 14% -> 0%
where the time goes in v4:
time: 179 us; the launch traced here: 178 us
  Pallas kernels  164 us (92%)
  local copies, waits for them, and re-layouts  8.9 us (5%)
  other arithmetic  4.4 us (2%)
    pallas_call x1, Pallas kernels, exchange_all(): pl.pallas_call(functools.partial(exchange_kernel, cell_scale, pixel_scale...  164 us
    unnamed x10, local copies, waits for them, and re-layouts  7.65 us

profile of v4, /device:TPU:1, one launch (start us, length us, event | category | flops | bytes accessed | tf_op | source)
XLA Modules:
  0.0 178.4 jit_solution(13721399332798033003)
XLA Ops:
  0.6 0.7 convert_reduce_fusion.5
  1.4 0.1 stack.27
  1.5 0.7 reduce
  2.2 0.1 squeeze.7
  2.3 0.8 convert_reduce_fusion.1
  3.1 0.1 stack.31
  3.2 0.1 stack.30
  3.3 0.1 stack.29
  3.4 0.1 stack.28
  3.6 0.2 convert_reduce_fusion
  3.8 0.1 select_reduce_fusion
  3.9 0.6 pad_add_fusion.idx_ref
  4.5 0.1 reshape.130
  4.6 0.1 broadcast_in_dim.32
  4.8 0.2 convolution_convert_fusion
  5.0 0.1 copy.18
  5.2 0.1 copy.19
  5.3 0.3 maximum_bitcast_fusion
  5.6 0.1 reshape.126
  5.8 0.1 copy.23
  5.9 0.8 pad_maximum_fusion.m_ref
  6.8 164.1 %exchange_all.1 = (bf16[512,512]{1,0:T(8,128)(2,1)}, bf16[9,2,4,4,16,512]{5,4,3,2,1,0:T(8,128)(2,1)}, bf16[512,512]{1,0:T(8,128)(2,1)}) custom-call(s32[2,128]{1,0:T(2,128)} %pad_add_fusion.idx_ref, bf16[2,8,8,16,128]{4,3,2,1,0:T(8,128)(2,1)} %pad_maximum_fusion.m_ref, bf16[2560,512]{1,0:T(8,128)(2,1)} %bitcast.52, bf16[40,4,16,512]{3,2,1,0:T(8,128)(2,1)} %bitcast.53, ...), custom_call_target="tpu_custom_call" | custom-call | tf_op jit(solution)/shard_map/exchange_all/pallas_call | solution.py:628
  170.8 1.9 %copy.31 = bf16[1,512,512]{2,1,0:T(8,128)(2,1)} copy(bf16[1,512,512]{2,1,0:T(8,128)(2,1)} %bitcast.59) | data formatting | bytes 1048576
  172.7 0.0 copy-start
  172.7 4.9 %copy.32 = bf16[512,3,3,512]{3,0,2,1:T(8,128)(2,1)} copy(bf16[512,3,3,512]{3,0,2,1:T(8,128)(2,1)} %bitcast.51) | data formatting | bytes 9437184
  177.6 0.0 copy-done
  177.6 0.8 copy.33
  (14 shorter events, 0.2 us)
Async XLA Ops:
  172.7 4.9 %copy-start = (bf16[512,512]{1,0:T(8,128)(2,1)S(1)}, bf16[512,512]{1,0:T(8,128)(2,1)}, u32[]{:S(2)}) copy-start(bf16[512,512]{1,0:T(8,128)(2,1)} %get-tuple-element.28) | copy-start | bytes 1572868

commit v5 on v4

--- a/solution.py
+++ b/solution.py
@@ -13,6 +13,7 @@
 PIXB = 2 * IMGW
 TILES = 64
 CAP = 2
+UP = 256.0
 MESH = pl.DeviceIdType.MESH
 ANY = pl.BlockSpec(memory_space=pl.ANY)
 VMEM = pl.BlockSpec(memory_space=pltpu.VMEM)
@@ -129,12 +130,16 @@
 
     pl.semaphore_wait(barrier, len(greeted))
 
-    def edge_copies(up, where):
+    def edge_gradient(up, where):
         side = 0 if up else 1
         row = pl.ds((rows - 1) * cols if up else 0, cols)
-        copies = [
+        return [
             remote(g_ref.at[row], edges.at[side], e_send.at[side, 0], e_recv.at[side, 0], where)
         ]
+
+    def edge_features(up, where):
+        side = 0 if up else 1
+        copies = []
         for u in range(3):
             size = 4 if u < 2 else 2
             copies.append(
@@ -146,15 +151,17 @@
             )
         return copies
 
-    @pl.when(has_above)
-    def _():
-        for copy in edge_copies(True, above):
-            copy.start()
-
-    @pl.when(has_below)
-    def _():
-        for copy in edge_copies(False, below):
-            copy.start()
+    for edge_copies in (edge_gradient, edge_features):
+
+        @pl.when(has_above)
+        def _():
+            for copy in edge_copies(True, above):
+                copy.start()
+
+        @pl.when(has_below)
+        def _():
+            for copy in edge_copies(False, below):
+                copy.start()
 
     edge = jnp.zeros((8, half), F32)
     shift[pl.ds(0, 8), :] = edge
@@ -178,7 +185,9 @@
     pltpu.make_async_copy(g_ref, g_ref, in_sem.at[19]).wait()
     lax.fori_loop(1, rows + 1, move, 0)
 
-    def arrive(side, up, present):
+    def arrive(side, edge_copies, clear):
+        up, present = side == 0, has_below if side == 0 else has_above
+
         @pl.when(present)
         def _():
             for copy in edge_copies(up, below if up else above):
@@ -186,23 +195,40 @@
 
         @pl.when(jnp.logical_not(present))
         def _():
-            edges[side] = jnp.zeros((cols, chans), BF)
-            nothing = jnp.zeros((4, 16, chans), BF)
-            for u in range(10):
-                o_ref[5 + 2 * side + u // 8, u // 4 % 2, u % 4] = nothing
-
-        r = 0 if side == 0 else rows + 1
-        for n in range(5):
-            band[moved(1, r, n)] = edges[side, pl.ds(n * 128, 128), :]
-        move(r, 0)
-
-    arrive(0, True, has_below)
-    arrive(1, False, has_above)
+            clear()
+
+    def arrive_gradient():
+        for side in range(2):
+
+            def clear():
+                edges[side] = jnp.zeros((cols, chans), BF)
+
+            arrive(side, edge_gradient, clear)
+            r = 0 if side == 0 else rows + 1
+            for n in range(5):
+                band[moved(1, r, n)] = edges[side, pl.ds(n * 128, 128), :]
+            move(r, 0)
+
+    def arrive_features():
+        for side in range(2):
+
+            def clear():
+                nothing = jnp.zeros((4, 16, chans), BF)
+                for u in range(10):
+                    o_ref[5 + 2 * side + u // 8, u // 4 % 2, u % 4] = nothing
+
+            arrive(side, edge_features, clear)
+
     for copy in loads:
         copy.wait()
 
     def ground(s, carry):
-        r, n = s // 2, s % 2
+        r, n = (s // 2 + 1) % 3 + s // 6 * 2, s % 2
+
+        @pl.when(s == 4)
+        def _():
+            arrive_gradient()
+
         out = None
         for i in range(3):
             left, right = [], []
@@ -226,15 +252,18 @@
 
     lax.fori_loop(0, 2 * rows, ground, 0)
 
-    def fill(s, carry):
-        block = w_ref[idx_ref[0, s], idx_ref[1, s]]
-        place = pl.ds(pl.multiple_of(s % CAP * BLK, BLK), BLK)
-        o = s // CAP
-        dense[o // 8, o % 8, place, :] = block[:, :half]
-        slots1[o // 16, o // 2 % 8, o % 2, place, :] = block[:, half:]
-        return carry
-
-    lax.fori_loop(0, TILES * CAP, fill, 0)
+    def fill(h):
+        def one(s, carry):
+            o = s // CAP
+            place = pl.ds(pl.multiple_of(s % CAP * BLK, BLK), BLK)
+            block = w_ref[idx_ref[0, s], idx_ref[1, s]]
+            if h == 0:
+                dense[o // 8, o % 8, place, :] = block[:, :half]
+            else:
+                slots1[o // 16, o // 2 % 8, o % 2, place, :] = block[:, half:]
+            return carry
+
+        lax.fori_loop(0, TILES * CAP, one, 0, unroll=4)
 
     line = (z, y)
     here = [line[h] * 2 + core for h in range(2)]
@@ -262,19 +291,19 @@
             slots_of(h, member), land.at[h, place], p1_send.at[h, k], p1_recv.at[h, k], where
         )
 
-    own = []
+    own = [
+        pltpu.make_async_copy(src, dst.at[h, here[h]], own_sem.at[h, k])
+        for h in range(2)
+        for k, (src, dst) in enumerate(
+            ((info_of(h, here[h]), meta), (slots_of(h, here[h]), land))
+        )
+    ]
     for h in range(2):
-        own.append(
-            pltpu.make_async_copy(info_of(h, here[h]), meta.at[h, here[h]], own_sem.at[h, 0])
-        )
-        own.append(
-            pltpu.make_async_copy(slots_of(h, here[h]), land.at[h, here[h]], own_sem.at[h, 1])
-        )
-    for copy in own:
-        copy.start()
-    for which in ("meta", "slots"):
-        for k in range(7):
-            for h in range(2):
+        fill(h)
+        for copy in own[2 * h : 2 * h + 2]:
+            copy.start()
+        for which in ("meta", "slots"):
+            for k in range(7):
                 group_copy(h, k, 1, which).start()
 
     def column(u):
@@ -291,6 +320,7 @@
         return carry
 
     lax.fori_loop(0, 5 * rows, turn_inner, 0)
+    arrive_features()
     for side in range(2):
         for n in range(5):
             turn(5 * (rows + 1) * side + n, 5 + 2 * side + n // 4, n % 4 * 128)
@@ -447,7 +477,7 @@
         total = acc1[k, rows16(y), lanes128(z)].astype(F32)
         for p in range(15):
             total = total + recv2[p, k].astype(F32)
-        o_ref[k, core, x, y, :, lanes128(z)] = (total * cell_scale).astype(BF)
+        o_ref[k, core, x, y, :, lanes128(z)] = (total * (cell_scale * UP)).astype(BF)
         return carry
 
     lax.fori_loop(0, taps, add2, 0)
@@ -518,9 +548,10 @@
     w_ref[0] = part.reshape(w_ref.shape[1:])
     bb_pair = remote(w_ref.at[0, other], bb0, pair_send.at[1], pair_recv.at[1], at(0, 0, 1))
     bb_pair.start()
-    ig_ref[...] = lax.dot_general(
+    image_grad = lax.dot_general(
         scaled, bw_ref[...], (((1,), (1,)), ((), ())), preferred_element_type=F32
-    ).astype(BF)
+    )
+    ig_ref[...] = (image_grad * UP).astype(BF)
     bb_pair.wait()
     w_ref[1, pl.ds(0, 4)] = (w_ref[0, mine].astype(F32) + bb0[...].astype(F32)).astype(BF)
 
@@ -572,7 +603,7 @@
     def bb_rows(dy, dz):
         return pl.ds(pl.multiple_of(core * half + place(dy, dz) * 16, 16), 16)
 
-    bb_ref[bb_rows(0, 0), lanes128(x)] = (total * pixel_scale).astype(BF)
+    bb_ref[bb_rows(0, 0), lanes128(x)] = (total * (pixel_scale * UP)).astype(BF)
 
     def bb_strip(d, sign):
         part = bb_ref.at[bb_rows(0, 0), lanes128((x + sign * d + 4) % 4)]
@@ -608,12 +639,12 @@
 
     @pl.when(has_above)
     def _():
-        for copy in edge_copies(True, above):
+        for copy in edge_gradient(True, above) + edge_features(True, above):
             copy.wait_send()
 
     @pl.when(has_below)
     def _():
-        for copy in edge_copies(False, below):
+        for copy in edge_gradient(False, below) + edge_features(False, below):
             copy.wait_send()
 
 
@@ -726,6 +757,9 @@
         image,
         backbone_weight,
     )
+    image_grad, conv_sum, backbone_grad = (
+        (part * jnp.asarray(1.0 / UP, BF)) for part in (image_grad, conv_sum, backbone_grad)
+    )
     conv_grad = conv_sum.reshape(3, 3, chans, chans).transpose(2, 0, 1, 3)
     return (image_grad[None], conv_grad, backbone_grad)
 

time: 179 us -> 165 us (0.922)
  Pallas kernels: 164 us -> 149 us
  other arithmetic: 4.4 us -> 13.1 us
  local copies, waits for them, and re-layouts: 8.9 us -> 1.35 us
    pallas_call x1, Pallas kernels: 164 us -> 149 us  [exchange_all(): pl.pallas_call(functools.partial(exchange_kernel, cell_scale, pixel_scale...]
    unnamed x10 -> x5, local copies, waits for them, and re-layouts: 7.65 us -> 0.1 us
    mul x0 -> x2, other arithmetic: none -> 6.81 us  [body(): part * jnp.asarray(1.0 / UP, BF)]
    broadcast_in_dim x0 -> x1, other arithmetic: none -> 1.88 us  [body(): return (image_grad[None], conv_grad, backbone_grad)]
where the time goes in v5:
time: 165 us; the launch traced here: 164 us
  Pallas kernels  149 us (90%)
  other arithmetic  13.1 us (8%)
    pallas_call x1, Pallas kernels, exchange_all(): pl.pallas_call(functools.partial(exchange_kernel, cell_scale, pixel_scale...  149 us
    mul x2, other arithmetic, body(): part * jnp.asarray(1.0 / UP, BF)  6.81 us

profile of v5, /device:TPU:1, one launch (start us, length us, event | category | flops | bytes accessed | tf_op | source)
XLA Modules:
  0.0 164.5 jit_solution(16286332338746047598)
XLA Ops:
  0.6 0.7 convert_reduce_fusion.5
  1.4 0.1 stack.27
  1.5 0.7 reduce
  2.2 0.1 squeeze.7
  2.3 0.8 convert_reduce_fusion.1
  3.1 0.1 stack.31
  3.2 0.1 stack.30
  3.3 0.1 stack.29
  3.4 0.1 stack.28
  3.6 0.2 convert_reduce_fusion
  3.8 0.1 select_reduce_fusion
  3.9 0.6 pad_add_fusion.idx_ref
  4.5 0.1 reshape.130
  4.6 0.1 broadcast_in_dim.32
  4.8 0.2 convolution_convert_fusion
  5.0 0.1 copy.18
  5.2 0.1 copy.19
  5.3 0.3 maximum_bitcast_fusion
  5.6 0.1 reshape.126
  5.8 0.1 copy.23
  5.9 0.8 pad_maximum_fusion.m_ref
  6.8 149.0 %exchange_all.1 = (bf16[512,512]{1,0:T(8,128)(2,1)}, bf16[9,2,4,4,16,512]{5,4,3,2,1,0:T(8,128)(2,1)}, bf16[512,512]{1,0:T(8,128)(2,1)}) custom-call(s32[2,128]{1,0:T(2,128)} %pad_add_fusion.idx_ref, bf16[2,8,8,16,128]{4,3,2,1,0:T(8,128)(2,1)} %pad_maximum_fusion.m_ref, bf16[2560,512]{1,0:T(8,128)(2,1)} %bitcast.53, bf16[40,4,16,512]{3,2,1,0:T(8,128)(2,1)} %bitcast.54, ...), custom_call_target="tpu_custom_call" | custom-call | tf_op jit(solution)/shard_map/exchange_all/pallas_call | solution.py:659
  155.8 1.9 %multiply_bitcast_fusion = bf16[1,512,512]{2,1,0:T(8,128)(2,1)} fusion(bf16[512,512]{1,0:T(8,128)(2,1)} %get-tuple-element.6), kind=kLoop, calls=%fused_computation.3 | loop fusion | flops 262144 | bytes 1048576 | tf_op jit(solution)/shard_map/broadcast_in_dim | solution.py:764
  157.7 1.9 %broadcast_multiply_fusion.1 = bf16[512,512]{1,0:T(8,128)(2,1)} fusion(bf16[512,512]{1,0:T(8,128)(2,1)} %get-tuple-element.8), kind=kLoop, calls=%fused_computation.4 | loop fusion | flops 262144 | bytes 1048576 | tf_op jit(solution)/shard_map/mul | solution.py:761
  159.6 4.9 %broadcast_multiply_fusion = bf16[9,2,4,4,16,512]{5,4,3,2,1,0:T(8,128)(2,1)} fusion(bf16[9,2,4,4,16,512]{5,4,3,2,1,0:T(8,128)(2,1)} %get-tuple-element.7), kind=kLoop, calls=%fused_computation | loop fusion | flops 2359296 | bytes 9437184 | tf_op jit(solution)/shard_map/mul | solution.py:761
  (14 shorter events, 0.2 us)

commit v6 on v5

--- a/solution.py
+++ b/solution.py
@@ -13,7 +13,6 @@
 PIXB = 2 * IMGW
 TILES = 64
 CAP = 2
-UP = 256.0
 MESH = pl.DeviceIdType.MESH
 ANY = pl.BlockSpec(memory_space=pl.ANY)
 VMEM = pl.BlockSpec(memory_space=pltpu.VMEM)
@@ -252,18 +251,15 @@
 
     lax.fori_loop(0, 2 * rows, ground, 0)
 
-    def fill(h):
-        def one(s, carry):
-            o = s // CAP
-            place = pl.ds(pl.multiple_of(s % CAP * BLK, BLK), BLK)
-            block = w_ref[idx_ref[0, s], idx_ref[1, s]]
-            if h == 0:
-                dense[o // 8, o % 8, place, :] = block[:, :half]
-            else:
-                slots1[o // 16, o // 2 % 8, o % 2, place, :] = block[:, half:]
-            return carry
-
-        lax.fori_loop(0, TILES * CAP, one, 0, unroll=4)
+    def fill(s, carry):
+        o = s // CAP
+        place = pl.ds(pl.multiple_of(s % CAP * BLK, BLK), BLK)
+        block = w_ref[idx_ref[0, s], idx_ref[1, s]]
+        dense[o // 8, o % 8, place, :] = block[:, :half]
+        slots1[o // 16, o // 2 % 8, o % 2, place, :] = block[:, half:]
+        return carry
+
+    lax.fori_loop(0, TILES * CAP, fill, 0)
 
     line = (z, y)
     here = [line[h] * 2 + core for h in range(2)]
@@ -298,12 +294,11 @@
             ((info_of(h, here[h]), meta), (slots_of(h, here[h]), land))
         )
     ]
-    for h in range(2):
-        fill(h)
-        for copy in own[2 * h : 2 * h + 2]:
-            copy.start()
-        for which in ("meta", "slots"):
-            for k in range(7):
+    for copy in own:
+        copy.start()
+    for which in ("meta", "slots"):
+        for k in range(7):
+            for h in range(2):
                 group_copy(h, k, 1, which).start()
 
     def column(u):
@@ -477,33 +472,41 @@
         total = acc1[k, rows16(y), lanes128(z)].astype(F32)
         for p in range(15):
             total = total + recv2[p, k].astype(F32)
-        o_ref[k, core, x, y, :, lanes128(z)] = (total * (cell_scale * UP)).astype(BF)
+        o_ref[k, core, x, y, :, lanes128(z)] = (total * cell_scale).astype(BF)
         return carry
 
     lax.fori_loop(0, taps, add2, 0)
 
+    sets = (("x", 0, 3), ("y", 3, 2), ("z", 5, 2), ("x", 7, 2))
+
     def spread(s, k, sign):
+        axis, first, count = sets[s]
         p, q = plane[k]
-        dy, dx, dz = ((p, 0, q), (0, p, q), (p, q, 0))[s]
+        dy, dx, dz = {"x": (p, 0, q), "y": (0, p, q), "z": (p, q, 0)}[axis]
         part = o_ref.at[
-            pl.ds(3 * s, 3), core, (x + sign * dx + 4) % 4, (y + sign * dy + 4) % 4, :,
+            pl.ds(first, count), core, (x + sign * dx + 4) % 4, (y + sign * dy + 4) % 4, :,
             lanes128((z + sign * dz + 4) % 4),
         ]
         return remote(part, part, ag_send.at[s, k], ag_recv.at[s, k], at(dy, dz, 0, dx))
 
     def strip(s, d, sign):
-        t = pl.ds(3 * s, 3)
-        if s == 0:
+        axis, first, count = sets[s]
+        t = pl.ds(first, count)
+        if axis == "x":
             part, where = o_ref.at[t, core, (x + sign * d + 4) % 4], at(0, 0, 0, d)
-        elif s == 1:
+        elif axis == "y":
             part, where = o_ref.at[t, core, :, (y + sign * d + 4) % 4], at(d, 0, 0)
         else:
             part = o_ref.at[t, core, :, :, :, lanes128((z + sign * d + 4) % 4)]
             where = at(0, d, 0)
         return remote(part, part, far_send.at[s, d - 1], far_recv.at[s, d - 1], where)
 
+    def strips(s):
+        for d in (1, 2, 3):
+            strip(s, d, 0).start()
+
     for k in range(15):
-        for s in range(3):
+        for s in range(4):
             spread(s, k, 0).start()
 
     form(x_hi)
@@ -529,13 +532,11 @@
         third[h].start()
 
     for k in range(15):
-        for s in range(3):
+        for s in range(4):
             spread(s, k, 0).wait_send()
             spread(s, k, -1).wait_recv()
-    for d in (1, 2, 3):
-        for s in range(3):
-            strip(s, d, 0).start()
-
+    strips(0)
+    strips(3)
     settle(0)
 
     scaled = []
@@ -551,7 +552,7 @@
     image_grad = lax.dot_general(
         scaled, bw_ref[...], (((1,), (1,)), ((), ())), preferred_element_type=F32
     )
-    ig_ref[...] = (image_grad * UP).astype(BF)
+    ig_ref[...] = image_grad.astype(BF)
     bb_pair.wait()
     w_ref[1, pl.ds(0, 4)] = (w_ref[0, mine].astype(F32) + bb0[...].astype(F32)).astype(BF)
 
@@ -567,6 +568,8 @@
     ]
     for copy in bb_plane:
         copy.start()
+    strips(1)
+    strips(2)
     for copy in bb_plane:
         copy.wait()
     total = w_ref[1, y, rows16(z), :].astype(F32)
@@ -583,17 +586,11 @@
     for copy in bb_line:
         copy.start()
 
-    for d in (1, 2, 3):
-        for s in range(3):
-            strip(s, d, 0).wait_send()
-            strip(s, d, -1).wait_recv()
-
     def back(c):
         return remote(
             o_ref.at[:, c], o_ref.at[:, c], pair_send.at[2], pair_recv.at[2], at(0, 0, 1)
         )
 
-    back(core).start()
     for copy in bb_line:
         copy.wait()
     total = bb1_acc[:, lanes128(x)].astype(F32)
@@ -603,7 +600,7 @@
     def bb_rows(dy, dz):
         return pl.ds(pl.multiple_of(core * half + place(dy, dz) * 16, 16), 16)
 
-    bb_ref[bb_rows(0, 0), lanes128(x)] = (total * (pixel_scale * UP)).astype(BF)
+    bb_ref[bb_rows(0, 0), lanes128(x)] = (total * pixel_scale).astype(BF)
 
     def bb_strip(d, sign):
         part = bb_ref.at[bb_rows(0, 0), lanes128((x + sign * d + 4) % 4)]
@@ -623,6 +620,12 @@
 
     for d in (1, 2, 3):
         bb_strip(d, 0).start()
+
+    for s in (0, 3, 1, 2):
+        for d in (1, 2, 3):
+            strip(s, d, 0).wait_send()
+            strip(s, d, -1).wait_recv()
+    back(core).start()
     for d in (1, 2, 3):
         bb_strip(d, 0).wait_send()
         bb_strip(d, -1).wait_recv()
@@ -691,7 +694,7 @@
             dma((2, 7)), dma((2, 7)), dma((2, 7)), dma((2, 7)), dma((2, 2)),
             dma((2, 2, 3)), dma((2, 2, 3)), dma((2,)), dma((2,)),
             dma((7,)), dma((7,)), dma((3, 3)), dma((3, 3)), dma((15,)), dma((15,)),
-            dma((3, 15)), dma((3, 15)), dma((3, 3)), dma((3, 3)),
+            dma((4, 15)), dma((4, 15)), dma((4, 3)), dma((4, 3)),
             dma((2, 15)), dma((2, 15)), dma((2, 3)), dma((2, 3)),
         ],
         compiler_params=pltpu.CompilerParams(
@@ -699,6 +702,37 @@
         ),
         name="exchange_all",
     )(idx, meta, g, act, kernel, image, weight)
+
+
+def hand_out_kernel(ig_in, o_in, bb_in, ig_out, o_out, bb_out, ig, o, bb, sem_in, sem_out):
+    pieces = [(o_in.at[k], o.at[k], o_out.at[k]) for k in range(o.shape[0])]
+    pieces += [(ig_in, ig, ig_out), (bb_in, bb, bb_out)]
+    into = [
+        pltpu.make_async_copy(src, held, sem_in.at[k]) for k, (src, held, _) in enumerate(pieces)
+    ]
+    out = [
+        pltpu.make_async_copy(held, dst, sem_out.at[k]) for k, (_, held, dst) in enumerate(pieces)
+    ]
+    for copy in into:
+        copy.start()
+    for first, second in zip(into, out):
+        first.wait()
+        second.start()
+    for copy in out:
+        copy.wait()
+
+
+def hand_out(*arrays):
+    count = arrays[1].shape[0] + 2
+    return pl.pallas_call(
+        hand_out_kernel,
+        out_shape=[jax.ShapeDtypeStruct(a.shape, a.dtype) for a in arrays],
+        in_specs=[HBM] * 3,
+        out_specs=[HBM] * 3,
+        scratch_shapes=[pltpu.VMEM(a.shape, a.dtype) for a in arrays]
+        + [pltpu.SemaphoreType.DMA((count,))] * 2,
+        name="hand_out",
+    )(*arrays)
 
 
 def body(grad_out, bev_act, conv_weight, img_in, backbone_weight, route, offsets, frac_x, frac_y):
@@ -757,9 +791,7 @@
         image,
         backbone_weight,
     )
-    image_grad, conv_sum, backbone_grad = (
-        (part * jnp.asarray(1.0 / UP, BF)) for part in (image_grad, conv_sum, backbone_grad)
-    )
+    image_grad, conv_sum, backbone_grad = hand_out(image_grad, conv_sum, backbone_grad)
     conv_grad = conv_sum.reshape(3, 3, chans, chans).transpose(2, 0, 1, 3)
     return (image_grad[None], conv_grad, backbone_grad)
 

time: 165 us -> 162 us (0.982)
  other arithmetic: 13.1 us -> 4.4 us
  Pallas kernels: 149 us -> 155 us
    mul x2 -> x0, other arithmetic: 6.81 us -> none  [body(): part * jnp.asarray(1.0 / UP, BF)]
    pallas_call x0 -> x1, Pallas kernels: none -> 5.16 us  [hand_out(): pl.pallas_call(hand_out_kernel, out_shape=[jax.ShapeDtypeStruct(a.shape,...]
    broadcast_in_dim x1 -> x0, other arithmetic: 1.88 us -> none  [body(): return (image_grad[None], conv_grad, backbone_grad)]
where the time goes in v6:
time: 162 us
  Pallas kernels  155 us (96%)
  other arithmetic  4.4 us (3%)
    pallas_call x1, Pallas kernels, exchange_all(): pl.pallas_call(functools.partial(exchange_kernel, cell_scale, pixel_scale...  150 us
    pallas_call x1, Pallas kernels, hand_out(): pl.pallas_call(hand_out_kernel, out_shape=[jax.ShapeDtypeStruct(a.shape,...  5.16 us

profile of v6, /device:TPU:1, one launch (start us, length us, event | category | flops | bytes accessed | tf_op | source)
XLA Modules:
  0.0 161.7 jit_solution(11280835670070162637)
XLA Ops:
  0.6 0.7 convert_reduce_fusion.5
  1.4 0.1 stack.27
  1.5 0.7 reduce
  2.2 0.1 squeeze.7
  2.3 0.8 convert_reduce_fusion.1
  3.1 0.1 stack.31
  3.2 0.1 stack.30
  3.3 0.1 stack.29
  3.4 0.1 stack.28
  3.6 0.2 convert_reduce_fusion
  3.8 0.1 select_reduce_fusion
  3.9 0.6 pad_add_fusion.idx_ref
  4.5 0.1 reshape.130
  4.6 0.1 broadcast_in_dim.32
  4.8 0.2 convolution_convert_fusion
  5.0 0.1 copy.18
  5.2 0.1 copy.19
  5.3 0.3 maximum_bitcast_fusion
  5.6 0.1 reshape.126
  5.8 0.1 copy.23
  5.9 0.8 pad_maximum_fusion.m_ref
  6.8 149.6 %exchange_all.1 = (bf16[512,512]{1,0:T(8,128)(2,1)}, bf16[9,2,4,4,16,512]{5,4,3,2,1,0:T(8,128)(2,1)}, bf16[512,512]{1,0:T(8,128)(2,1)}) custom-call(s32[2,128]{1,0:T(2,128)} %pad_add_fusion.idx_ref, bf16[2,8,8,16,128]{4,3,2,1,0:T(8,128)(2,1)} %pad_maximum_fusion.m_ref, bf16[2560,512]{1,0:T(8,128)(2,1)} %bitcast.51, bf16[40,4,16,512]{3,2,1,0:T(8,128)(2,1)} %bitcast.52, ...), custom_call_target="tpu_custom_call" | custom-call | tf_op jit(solution)/shard_map/exchange_all/pallas_call | solution.py:662
  156.3 5.2 %hand_out.1 = (bf16[512,512]{1,0:T(8,128)(2,1)}, bf16[9,2,4,4,16,512]{5,4,3,2,1,0:T(8,128)(2,1)}, bf16[512,512]{1,0:T(8,128)(2,1)}) custom-call(bf16[512,512]{1,0:T(8,128)(2,1)} %get-tuple-element.9.ig_in, bf16[9,2,4,4,16,512]{5,4,3,2,1,0:T(8,128)(2,1)} %get-tuple-element.10.o_in, bf16[512,512]{1,0:T(8,128)(2,1)} %get-tuple-element.11.bb_in), custom_call_target="tpu_custom_call" | custom-call | tf_op jit(solution)/shard_map/hand_out/pallas_call | solution.py:727
  (14 shorter events, 0.2 us)

commit v7 on v6

--- a/solution.py
+++ b/solution.py
@@ -568,8 +568,6 @@
     ]
     for copy in bb_plane:
         copy.start()
-    strips(1)
-    strips(2)
     for copy in bb_plane:
         copy.wait()
     total = w_ref[1, y, rows16(z), :].astype(F32)
@@ -585,6 +583,8 @@
     ]
     for copy in bb_line:
         copy.start()
+    strips(1)
+    strips(2)
 
     def back(c):
         return remote(
@@ -705,8 +705,8 @@
 
 
 def hand_out_kernel(ig_in, o_in, bb_in, ig_out, o_out, bb_out, ig, o, bb, sem_in, sem_out):
-    pieces = [(o_in.at[k], o.at[k], o_out.at[k]) for k in range(o.shape[0])]
-    pieces += [(ig_in, ig, ig_out), (bb_in, bb, bb_out)]
+    pieces = [(ig_in, ig, ig_out), (bb_in, bb, bb_out)]
+    pieces += [(o_in.at[k], o.at[k], o_out.at[k]) for k in range(o.shape[0])]
     into = [
         pltpu.make_async_copy(src, held, sem_in.at[k]) for k, (src, held, _) in enumerate(pieces)
     ]

time: 162 us -> 162 us (level)
  no operation moved by 1% of the time
where the time goes in v7:
time: 162 us
  Pallas kernels  155 us (96%)
  other arithmetic  4.4 us (3%)
    pallas_call x1, Pallas kernels, exchange_all(): pl.pallas_call(functools.partial(exchange_kernel, cell_scale, pixel_scale...  150 us
    pallas_call x1, Pallas kernels, hand_out(): pl.pallas_call(hand_out_kernel, out_shape=[jax.ShapeDtypeStruct(a.shape,...  5.16 us

profile of v7, /device:TPU:1, one launch (start us, length us, event | category | flops | bytes accessed | tf_op | source)
XLA Modules:
  0.0 161.7 jit_solution(7599628455386464343)
XLA Ops:
  0.6 0.7 convert_reduce_fusion.5
  1.4 0.1 stack.27
  1.5 0.7 reduce
  2.2 0.1 squeeze.7
  2.3 0.8 convert_reduce_fusion.1
  3.1 0.1 stack.31
  3.2 0.1 stack.30
  3.3 0.1 stack.29
  3.4 0.1 stack.28
  3.6 0.2 convert_reduce_fusion
  3.8 0.1 select_reduce_fusion
  3.9 0.6 pad_add_fusion.idx_ref
  4.5 0.1 reshape.130
  4.6 0.1 broadcast_in_dim.32
  4.8 0.2 convolution_convert_fusion
  5.0 0.1 copy.18
  5.2 0.1 copy.19
  5.3 0.3 maximum_bitcast_fusion
  5.6 0.1 reshape.126
  5.8 0.1 copy.23
  5.9 0.8 pad_maximum_fusion.m_ref
  6.8 149.6 %exchange_all.1 = (bf16[512,512]{1,0:T(8,128)(2,1)}, bf16[9,2,4,4,16,512]{5,4,3,2,1,0:T(8,128)(2,1)}, bf16[512,512]{1,0:T(8,128)(2,1)}) custom-call(s32[2,128]{1,0:T(2,128)} %pad_add_fusion.idx_ref, bf16[2,8,8,16,128]{4,3,2,1,0:T(8,128)(2,1)} %pad_maximum_fusion.m_ref, bf16[2560,512]{1,0:T(8,128)(2,1)} %bitcast.51, bf16[40,4,16,512]{3,2,1,0:T(8,128)(2,1)} %bitcast.52, ...), custom_call_target="tpu_custom_call" | custom-call | tf_op jit(solution)/shard_map/exchange_all/pallas_call | solution.py:662
  156.3 5.2 %hand_out.1 = (bf16[512,512]{1,0:T(8,128)(2,1)}, bf16[9,2,4,4,16,512]{5,4,3,2,1,0:T(8,128)(2,1)}, bf16[512,512]{1,0:T(8,128)(2,1)}) custom-call(bf16[512,512]{1,0:T(8,128)(2,1)} %get-tuple-element.9.ig_in, bf16[9,2,4,4,16,512]{5,4,3,2,1,0:T(8,128)(2,1)} %get-tuple-element.10.o_in, bf16[512,512]{1,0:T(8,128)(2,1)} %get-tuple-element.11.bb_in), custom_call_target="tpu_custom_call" | custom-call | tf_op jit(solution)/shard_map/hand_out/pallas_call | solution.py:727
  (14 shorter events, 0.2 us)
